TPU v7x, 512 devices: a whole 4x4x16 slice. The times are simulated.
512 devices in a mesh: ia: 16 (over y, z_hi), ja: 32 (over x, z_lo, core).
Axes of the slice: x: 4, y: 4, z: 16 (z_hi: 4, z_lo: 4; z = z_hi * 4 + z_lo), core: 2. Of those that a mesh axis runs over, the one named last changes fastest.
Arguments:
- amplitudes: float32 [16, 32, 512, 512], P('ia', 'ja'), may hold values from -3 to 3
- integrals: bfloat16 [16, 32, 512, 512], P('ia', 'ja'), may hold values from -6 to 6
- pao_fock: float32 [8, 64, 384], replicated, may hold values from -0.3125 to 0.3125
- pao_intersection: float32 [8, 64, 384], replicated, may hold values from -1 to 2
- block_columns: int32 [8, 6], replicated, may hold values from 0 to 7, as said below
- occ_fock: float32 [32, 32], replicated, may hold values from -1 to 0.8, as said below
- pao_energies: float32 [512], replicated, may hold values from 0.3 to 2
- row_links: int32 [16, 32, 4], P('ia', 'ja'), may hold values 0 or 1
- column_links: int32 [16, 32, 2], P('ia', 'ja'), may hold values 0 or 1
Outputs:
- updated: float32 [16, 32, 512, 512], P('ia', 'ja')
Inputs may be any that keep to these rules, and one draw needn't show every extreme that they name: `block_columns`: slot 0 of block row r holds r; the slots of a row hold distinct block columns. `occ_fock`: Symmetric; its diagonal lies between -1 and -0.3.
All inputs are finite; a program needn't handle non-finite values. No bound on the sum of `row_links` or of `column_links` on one device may be relied on, other than what follows from the above.
Results may differ from a plain program's by a relative error of at most 0.0003.
Values sent between devices are 32-bit elements; how exact they have to be, the bound alone decides.
No kernel may reach another device: no remote copies, remote signals or barrier semaphores. Data moves between devices by JAX's collectives and lax.ppermute only.
A program may use at most 64 MiB of HBM per device.

v0:
```python
import jax
import jax.numpy as jnp
import numpy as np
from jax import lax
from jax.sharding import PartitionSpec as P

ITERS = 2
CHUNKS = 2
NX, NY, NHI, NLO = 4, 4, 4, 4
NZ = NHI * NLO
NI = NY * NHI
NJ = NX * NLO * 2

HIGH = lax.Precision.HIGH
AXES = ("ia", "ja")


def chip(i, j):
    return j // (2 * NLO), i // NHI, (i % NHI) * NLO + (j // 2) % NLO, j % 2


def pair(x, y, z, c):
    z = z % NZ
    return y * NHI + z // NLO, (x * NLO + z % NLO) * 2 + c


def moves(target):
    pairs = []
    for i in range(NI):
        for j in range(NJ):
            to = target(i, j)
            if to is not None:
                pairs.append((i * NJ + j, to[0] * NJ + to[1]))
    return pairs


def first_leg(step):
    def target(i, j):
        if not 0 <= i + step < NI:
            return None
        x, _, z, c = chip(i, j)
        return pair(x, (i + step) // NHI, z + step, c)

    return moves(target)


def middle_leg(step):
    def target(i, j):
        x, y, z, c = chip(i, j)
        di, dj = pair(x, y, z + 3 * step, c)
        edge = NLO - 1 if step > 0 else 0
        if not 0 <= di - step < NI and (dj // 2) % NLO != edge:
            return None
        return pair(x, y, z + 2 * step, c)

    return moves(target)


def last_leg(step):
    def target(i, j):
        x, y, z, c = chip(i, j)
        di, dj = pair(x, y, z + step, c)
        near = 0 if step > 0 else NLO - 1
        if not 0 <= di - step < NI and (dj // 2) % NLO == near:
            return None
        return di, dj

    return moves(target)


def across(i, j):
    x, y, z, c = chip(i, j)
    if z % NLO == NLO - 1 and x + 1 < NX:
        return pair(x + 1, y, z, c)
    if z % NLO == 0 and x > 0:
        return pair(x - 1, y, z, c)
    return None


def goal_links(step):
    def target(i, j):
        x, y, z, c = chip(i, j)
        return pair(x, y, z - 3 * step, c)

    return moves(target)


def along_j(offset):
    def target(i, j):
        return (i, j + offset) if 0 <= j + offset < NJ else None

    return moves(target)


FIRST = {s: first_leg(s) for s in (1, -1)}
MIDDLE = {s: middle_leg(s) for s in (1, -1)}
LAST = {s: last_leg(s) for s in (1, -1)}
ACROSS = moves(across)
PARTNER = moves(lambda i, j: (i, j ^ 1))
GOAL = {s: goal_links(s) for s in (1, -1)}


def send(x, pairs):
    return lax.ppermute(x, AXES, pairs)


def mm(a, b):
    return jnp.dot(a, b, precision=HIGH, preferred_element_type=jnp.float32)


def build_dense(blocks, columns):
    block_rows, block_size, block_wide = blocks.shape
    wide = block_rows * block_size
    slot = jnp.arange(block_wide, dtype=jnp.int32)
    place = jnp.repeat(columns, block_size, axis=1) * block_size + (slot % block_size)[None, :]
    spread = (place[:, :, None] == jnp.arange(wide, dtype=jnp.int32)[None, None, :]).astype(jnp.float32)
    dense = jnp.einsum("rxk,rkn->rxn", blocks, spread, precision=HIGH)
    return dense.reshape(wide, wide)


SOURCES = ("own", "far", "back", "ahead", "behind")
ROW, COLUMN = 0, 4
LINKS = (
    ("ahead", COLUMN),
    ("behind", COLUMN + 1),
    ("far", ROW),
    ("far", ROW + 1),
    ("back", ROW + 3),
    ("back", ROW + 2),
    ("far", ROW),
    ("far", ROW + 1),
    ("back", ROW + 3),
    ("back", ROW + 2),
    ("own", ROW + 2),
    ("own", ROW + 1),
    None,
    None,
)


def tables():
    places = np.zeros((NI, NJ, len(LINKS), 3), np.int32)
    for i in range(NI):
        for j in range(NJ):
            x, y, z, c = chip(i, j)
            low = z % NLO
            up = pair(x, y, z + 3, c)[0]
            down = pair(x, y, z - 3, c)[0]
            top, bottom = low == NLO - 1, low == 0
            odd, even = c == 1, c == 0
            places[i, j] = [
                (up, up - 1, up > 0),
                (down, down + 1, down + 1 < NI),
                (j, j + 2, not top),
                (j + 1, j + 2, even and not top),
                (j, j - 2, not bottom),
                (j - 1, j - 2, odd and not bottom),
                (j, j + 2, top),
                (j + 1, j + 2, even and top),
                (j, j - 2, bottom),
                (j - 1, j - 2, odd and bottom),
                (j + 1, j, even),
                (j - 1, j, odd),
                (i, i, True),
                (j, j, True),
            ]
    return places.reshape(NI * NJ, len(LINKS), 3)


TABLE = tables()
CHOICE = np.zeros((len(LINKS), len(SOURCES) * 8), np.float32)
for entry, link in enumerate(LINKS):
    if link is not None:
        CHOICE[entry, SOURCES.index(link[0]) * 8 + link[1]] = 1.0
FREE = np.array([1.0 if link is None else 0.0 for link in LINKS], np.float32)


def coefficients(occ_fock, row_links, column_links):
    links = jnp.concatenate([row_links, column_links, jnp.zeros((2,), jnp.int32)])
    got = {
        "own": links,
        "far": send(links, along_j(-2)),
        "back": send(links, along_j(2)),
        "ahead": send(links, GOAL[1]),
        "behind": send(links, GOAL[-1]),
    }
    flat = jnp.concatenate([got[name] for name in SOURCES]).astype(jnp.float32)
    where = lax.axis_index("ia") * NJ + lax.axis_index("ja")
    place = lax.dynamic_slice_in_dim(jnp.asarray(TABLE), where, 1, axis=0)[0]
    rows, columns, used = place[:, 0], place[:, 1], place[:, 2]
    spots = jnp.arange(NJ, dtype=jnp.int32)
    hot = (rows[:, None, None] == spots[None, :, None]) & (columns[:, None, None] == spots[None, None, :])
    picked = jnp.sum(jnp.where(hot, occ_fock[None], 0.0), axis=(1, 2))
    weights = jnp.sum(jnp.asarray(CHOICE) * flat[None, :], axis=1) + jnp.asarray(FREE)
    return picked * weights * used.astype(jnp.float32)


def after(values, earlier):
    kept = lax.optimization_barrier((*values, earlier))
    return kept[: len(values)]


def sweep_pieces(pieces, picked, low):
    at_top = (low == NLO - 1).astype(jnp.float32)
    at_bottom = (low == 0).astype(jnp.float32)
    mates = [send(p, PARTNER) for p in pieces]
    firsts = [{s: send(p, FIRST[s]) for s in (1, -1)} for p in pieces]
    crossed = []
    out = None
    for p, m in zip(pieces, mates):
        if out is not None:
            (m,) = after((m,), out)
        out = (picked[6] + picked[8]) * p + (picked[7] + picked[9]) * m
        crossed.append(send(out, ACROSS))
    middles = []
    up = None
    for f, x in zip(firsts, crossed):
        if up is not None:
            (x,) = after((x,), up)
        up = picked[0] * f[1] + at_bottom * x
        down = picked[1] * f[-1] + at_top * x
        middles.append({1: send(up, MIDDLE[1]), -1: send(down, MIDDLE[-1])})
    gathered = []
    up = None
    for p, m, mid in zip(pieces, mates, middles):
        if up is not None:
            p, m = after((p, m), up)
        up = mid[1] + picked[2] * p + picked[3] * m
        down = mid[-1] + picked[4] * p + picked[5] * m
        plus = send(up, LAST[1])
        minus = send(down, LAST[-1])
        gathered.append(plus + minus + (picked[10] + picked[11]) * m)
    return gathered


def body(
    amplitudes,
    integrals,
    pao_fock,
    pao_intersection,
    block_columns,
    occ_fock,
    pao_energies,
    row_links,
    column_links,
):
    start = amplitudes[0, 0]
    integral = integrals[0, 0]
    low = (lax.axis_index("ja") // 2) % NLO
    wide = start.shape[0] // CHUNKS
    spans = [slice(k * wide, (k + 1) * wide) for k in range(CHUNKS)]
    pieces = list(lax.optimization_barrier(tuple(start[span] for span in spans)))
    for sweep_number in range(ITERS):
        if sweep_number == 0:
            picked = coefficients(occ_fock, row_links[0, 0], column_links[0, 0])
            diagonal = picked[12] + picked[13]
            fock_dense = build_dense(pao_fock, block_columns)
            intersection_dense = build_dense(pao_intersection, block_columns)
            shifted = fock_dense - diagonal * intersection_dense
            inverse_gap = 1.0 / (pao_energies[:, None] + pao_energies[None, :] - diagonal)
            current = start
        else:
            current = jnp.concatenate(pieces, axis=0)
        gathered = sweep_pieces(pieces, picked, low)
        local = mm(mm(shifted, current), intersection_dense)
        local = local + mm(mm(intersection_dense, current), fock_dense)
        local = local + integral.astype(jnp.float32)
        rights = [mm(coupled, intersection_dense) for coupled in gathered]
        if sweep_number + 1 == ITERS:
            for right, span in zip(rights, spans):
                local = local - mm(intersection_dense[:, span], right)
            return (current - local * inverse_gap)[None, None]
        rest = [local[span] for span in spans]
        for k, right in enumerate(rights):
            rest = [r - mm(intersection_dense[span, spans[k]], right) for r, span in zip(rest, spans)]
        pieces = [p - r * inverse_gap[span] for p, r, span in zip(pieces, rest, spans)]


def solution(mesh):
    placed = (
        P("ia", "ja", None, None),
        P("ia", "ja", None, None),
        P(),
        P(),
        P(),
        P(),
        P(),
        P("ia", "ja", None),
        P("ia", "ja", None),
    )
    return jax.shard_map(
        body, mesh=mesh, in_specs=placed, out_specs=P("ia", "ja", None, None), check_vma=False
    )
```

profile of v0, /device:TPU:20, one launch (start us, length us, event | category | flops | bytes accessed | tf_op | source)
XLA Modules:
  0.0 266.5 jit_solution(9851344307645600658)
XLA Ops:
  0.8 6.6 %collective-permute-start = (s32[8]{0:T(128)S(1)}, s32[8]{0:T(128)S(1)}, u32[]{:S(2)}, u32[]{:S(2)}) collective-permute-start(s32[8]{0:T(128)S(1)} %pad_add_fusion), channel_id=1, source_target_pairs={{2,0},{3,1},{4,2},{5,3},{6,4},{7,5},{8,6},{9,7},{10,8},{11,9},{12,... | collective-permute-start | bytes 104 | tf_op jit(solution)/shard_map/ppermute | solution.py:104
  9.4 9.7 %collective-permute-start.2 = (s32[8]{0:T(128)S(1)}, s32[8]{0:T(128)S(1)}, u32[]{:S(2)}, u32[]{:S(2)}) collective-permute-start(s32[8]{0:T(128)S(1)} %pad_add_fusion), channel_id=1, source_target_pairs={{0,98},{1,99},{2,100},{3,101},{4,102},{5,103},{6,0},{7,1},{8,106},... | collective-permute-start | bytes 104 | tf_op jit(solution)/shard_map/ppermute | solution.py:104
  25.2 3.1 %fusion.1 = f32[8,512,64]{1,2,0:T(8,128)S(1)} fusion(f32[8,64,384]{2,1,0:T(8,128)} %param.14, s32[8,384]{1,0:T(8,128)S(1)} %broadcast_add_fusion), kind=kOutput, calls=%fused_computation.2 | convolution fusion | flops 605552640 | bytes 1847296 | tf_op jit(solution)/shard_map/rxk,rkn->rxn/dot_general | solution.py:117
  28.7 8.6 %collective-permute-start.9 = (f32[256,512]{1,0:T(8,128)S(1)}, f32[256,512]{1,0:T(8,128)}, u32[]{:S(2)}, u32[]{:S(2)}) collective-permute-start(f32[256,512]{1,0:T(8,128)S(1)} %get-tuple-element.15), channel_id=1, source_target_pairs={{32,6},{33,7},{34,32},{35,33},{36,34},{37,35},{38,36},{39,37},{40,... | collective-permute-start | bytes 1572872 | tf_op jit(solution)/shard_map/ppermute | solution.py:104
  41.4 5.8 %collective-permute-start.17 = (f32[256,512]{1,0:T(8,128)S(1)}, f32[256,512]{1,0:T(8,128)}, u32[]{:S(2)}, u32[]{:S(2)}) collective-permute-start(f32[256,512]{1,0:T(8,128)S(1)} %get-tuple-element.19), channel_id=1, source_target_pairs={{32,6},{33,7},{34,32},{35,33},{36,34},{37,35},{38,36},{39,37},{40,... | collective-permute-start | bytes 1572872 | tf_op jit(solution)/shard_map/ppermute | solution.py:104
  53.3 2.5 fusion.17
  67.1 7.6 %collective-permute-done.6 = f32[256,512]{1,0:T(8,128)S(1)} collective-permute-done((f32[256,512]{1,0:T(8,128)S(1)}, f32[256,512]{1,0:T(8,128)S(1)}, u32[]{:S(2)}, u32[]{:S(2)}) %collective-permute-start.6) | collective-permute-done | bytes 524320 | tf_op jit(solution)/shard_map/ppermute | solution.py:104
  74.7 2.6 multiply_add_fusion.16
  79.3 4.8 %collective-permute-start.7 = (f32[256,512]{1,0:T(8,128)S(1)}, f32[256,512]{1,0:T(8,128)S(1)}, u32[]{:S(2)}, u32[]{:S(2)}) collective-permute-start(f32[256,512]{1,0:T(8,128)S(1)} %get-tuple-element.42), channel_id=1, source_target_pairs={{0,4},{1,5},{2,6},{3,7},{4,32},{5,33},{6,34},{7,35},{8,12},{9,13},... | collective-permute-start | bytes 1572872 | tf_op jit(solution)/shard_map/ppermute | solution.py:104
  87.6 3.1 %collective-permute-start.18 = (f32[256,512]{1,0:T(8,128)S(1)}, f32[256,512]{1,0:T(8,128)S(1)}, u32[]{:S(2)}, u32[]{:S(2)}) collective-permute-start(f32[256,512]{1,0:T(8,128)S(1)} %get-tuple-element.39), channel_id=1, source_target_pairs={{0,100},{1,101},{2,102},{3,103},{4,0},{5,1},{6,2},{7,3},{8,108},{9... | collective-permute-start | bytes 1572872 | tf_op jit(solution)/shard_map/ppermute | solution.py:104
  90.8 3.6 %collective-permute-start.15 = (f32[256,512]{1,0:T(8,128)S(1)}, f32[256,512]{1,0:T(8,128)S(1)}, u32[]{:S(2)}, u32[]{:S(2)}) collective-permute-start(f32[256,512]{1,0:T(8,128)S(1)} %get-tuple-element.40), channel_id=1, source_target_pairs={{0,4},{1,5},{2,6},{3,7},{4,32},{5,33},{6,34},{7,35},{8,12},{9,13},... | collective-permute-start | bytes 1572872 | tf_op jit(solution)/shard_map/ppermute | solution.py:104
  94.4 14.2 %collective-permute-done.10 = f32[256,512]{1,0:T(8,128)S(1)} collective-permute-done((f32[256,512]{1,0:T(8,128)S(1)}, f32[256,512]{1,0:T(8,128)S(1)}, u32[]{:S(2)}, u32[]{:S(2)}) %collective-permute-start.10) | collective-permute-done | bytes 524320 | tf_op jit(solution)/shard_map/ppermute | solution.py:104
  108.6 2.8 %multiply_add_fusion.15 = (f32[256,512]{1,0:T(8,128)S(1)}, f32[256,512]{1,0:T(8,128)S(1)}) fusion(f32[256,512]{1,0:T(8,128)S(1)} %collective-permute-done.5, f32[256,512]{1,0:T(8,128)S(1)} %collective-permute-done.10, f32[256,512]{1,0:T(8,128)S(1)} %get-tuple-element.15, f32[]{:T(128)} %bitcast.24, f32[]{:T(128)} %bitcast.23, f32[]{:T(128)} %bitcast.21, ...), kind=kLoop, calls=%fused_computation.68 | loop fusion | flops 1048576 | bytes 3145744 | tf_op jit(solution)/shard_map/add | solution.py:229
  111.3 4.7 %collective-permute-start.8 = (f32[256,512]{1,0:T(8,128)S(1)}, f32[256,512]{1,0:T(8,128)S(1)}, u32[]{:S(2)}, u32[]{:S(2)}) collective-permute-start(f32[256,512]{1,0:T(8,128)S(1)} %get-tuple-element.32), channel_id=1, source_target_pairs={{0,2},{1,3},{2,4},{3,5},{4,6},{5,7},{6,32},{7,33},{8,10},{9,11},{1... | collective-permute-start | bytes 1572872 | tf_op jit(solution)/shard_map/ppermute | solution.py:104
  118.6 7.5 %collective-permute-done.18 = f32[256,512]{1,0:T(8,128)S(1)} collective-permute-done((f32[256,512]{1,0:T(8,128)S(1)}, f32[256,512]{1,0:T(8,128)S(1)}, u32[]{:S(2)}, u32[]{:S(2)}) %collective-permute-start.18) | collective-permute-done | bytes 524320 | tf_op jit(solution)/shard_map/ppermute | solution.py:104
  126.1 4.1 %collective-permute-done.15 = f32[256,512]{1,0:T(8,128)S(1)} collective-permute-done((f32[256,512]{1,0:T(8,128)S(1)}, f32[256,512]{1,0:T(8,128)S(1)}, u32[]{:S(2)}, u32[]{:S(2)}) %collective-permute-start.15) | collective-permute-done | bytes 524320 | tf_op jit(solution)/shard_map/ppermute | solution.py:104
  130.3 3.8 %multiply_add_fusion.10 = (f32[256,512]{1,0:T(8,128)S(1)}, f32[256,512]{1,0:T(8,128)S(1)}) fusion(f32[256,512]{1,0:T(8,128)} %collective-permute-done.13, f32[256,512]{1,0:T(8,128)S(1)} %collective-permute-done.18, f32[256,512]{1,0:T(8,128)S(1)} %get-tuple-element.19, f32[]{:T(128)} %bitcast.24, f32[]{:T(128)} %bitcast.23, f32[]{:T(128)} %bitcast.21, ...), kind=kLoop, calls=%fused_computation.59 | loop fusion | flops 1048576 | bytes 3145744 | tf_op jit(solution)/shard_map/add | solution.py:229
  134.1 4.1 %collective-permute-start.16 = (f32[256,512]{1,0:T(8,128)S(1)}, f32[256,512]{1,0:T(8,128)S(1)}, u32[]{:S(2)}, u32[]{:S(2)}) collective-permute-start(f32[256,512]{1,0:T(8,128)S(1)} %get-tuple-element.30), channel_id=1, source_target_pairs={{0,2},{1,3},{2,4},{3,5},{4,6},{5,7},{6,32},{7,33},{8,10},{9,11},{1... | collective-permute-start | bytes 1572872 | tf_op jit(solution)/shard_map/ppermute | solution.py:104
  138.1 3.0 %collective-permute-start.19 = (f32[256,512]{1,0:T(8,128)S(1)}, f32[256,512]{1,0:T(8,128)S(1)}, u32[]{:S(2)}, u32[]{:S(2)}) collective-permute-start(f32[256,512]{1,0:T(8,128)S(1)} %get-tuple-element.29), channel_id=1, source_target_pairs={{0,102},{1,103},{2,0},{3,1},{4,2},{5,3},{6,4},{7,5},{8,110},{9,111... | collective-permute-start | bytes 1572872 | tf_op jit(solution)/shard_map/ppermute | solution.py:104
  143.7 9.3 %collective-permute-done.16 = f32[256,512]{1,0:T(8,128)S(1)} collective-permute-done((f32[256,512]{1,0:T(8,128)S(1)}, f32[256,512]{1,0:T(8,128)S(1)}, u32[]{:S(2)}, u32[]{:S(2)}) %collective-permute-start.16) | collective-permute-done | bytes 524320 | tf_op jit(solution)/shard_map/ppermute | solution.py:104
  159.1 3.3 %collective-permute-start.20 = (f32[256,512]{1,0:T(8,128)S(1)}, f32[256,512]{1,0:T(8,128)S(1)}, u32[]{:S(2)}, u32[]{:S(2)}) collective-permute-start(f32[256,512]{1,0:T(8,128)S(1)} %fusion.12), channel_id=1, source_target_pairs={{0,2},{1,3},{2,4},{3,5},{4,6},{5,7},{6,32},{7,33},{8,10},{9,11},{1... | collective-permute-start | bytes 1572872 | tf_op jit(solution)/shard_map/ppermute | solution.py:104
  164.7 5.1 %collective-permute-start.33 = (f32[256,512]{1,0:T(8,128)S(1)}, f32[256,512]{1,0:T(8,128)S(1)}, u32[]{:S(2)}, u32[]{:S(2)}) collective-permute-start(f32[256,512]{1,0:T(8,128)S(1)} %fusion.10), channel_id=1, source_target_pairs={{32,6},{33,7},{34,32},{35,33},{36,34},{37,35},{38,36},{39,37},{40,... | collective-permute-start | bytes 1572872 | tf_op jit(solution)/shard_map/ppermute | solution.py:104
  178.4 9.2 %collective-permute-done.22 = f32[256,512]{1,0:T(8,128)S(1)} collective-permute-done((f32[256,512]{1,0:T(8,128)S(1)}, f32[256,512]{1,0:T(8,128)S(1)}, u32[]{:S(2)}, u32[]{:S(2)}) %collective-permute-start.22) | collective-permute-done | bytes 524320 | tf_op jit(solution)/shard_map/ppermute | solution.py:104
  191.0 4.8 %collective-permute-start.23 = (f32[256,512]{1,0:T(8,128)S(1)}, f32[256,512]{1,0:T(8,128)S(1)}, u32[]{:S(2)}, u32[]{:S(2)}) collective-permute-start(f32[256,512]{1,0:T(8,128)S(1)} %get-tuple-element.38), channel_id=1, source_target_pairs={{0,4},{1,5},{2,6},{3,7},{4,32},{5,33},{6,34},{7,35},{8,12},{9,13},... | collective-permute-start | bytes 1572872 | tf_op jit(solution)/shard_map/ppermute | solution.py:104
  201.4 4.7 %collective-permute-start.31 = (f32[256,512]{1,0:T(8,128)S(1)}, f32[256,512]{1,0:T(8,128)S(1)}, u32[]{:S(2)}, u32[]{:S(2)}) collective-permute-start(f32[256,512]{1,0:T(8,128)S(1)} %get-tuple-element.36), channel_id=1, source_target_pairs={{0,4},{1,5},{2,6},{3,7},{4,32},{5,33},{6,34},{7,35},{8,12},{9,13},... | collective-permute-start | bytes 1572872 | tf_op jit(solution)/shard_map/ppermute | solution.py:104
  206.1 7.6 %collective-permute-done.26 = f32[256,512]{1,0:T(8,128)S(1)} collective-permute-done((f32[256,512]{1,0:T(8,128)S(1)}, f32[256,512]{1,0:T(8,128)S(1)}, u32[]{:S(2)}, u32[]{:S(2)}) %collective-permute-start.26) | collective-permute-done | bytes 524320 | tf_op jit(solution)/shard_map/ppermute | solution.py:104
  215.6 2.7 %multiply_add_fusion.5 = (f32[256,512]{1,0:T(8,128)S(1)}, f32[256,512]{1,0:T(8,128)S(1)}) fusion(f32[256,512]{1,0:T(8,128)S(1)} %collective-permute-done.21, f32[256,512]{1,0:T(8,128)S(1)} %collective-permute-done.26, f32[256,512]{1,0:T(8,128)S(1)} %fusion.12, f32[]{:T(128)} %bitcast.24, f32[]{:T(128)} %bitcast.23, f32[]{:T(128)} %bitcast.21, ...), kind=kLoop, calls=%fused_computation.49 | loop fusion | flops 1048576 | bytes 3145744 | tf_op jit(solution)/shard_map/add | solution.py:229
  218.3 19.0 %collective-permute-start.24 = (f32[256,512]{1,0:T(8,128)S(1)}, f32[256,512]{1,0:T(8,128)S(1)}, u32[]{:S(2)}, u32[]{:S(2)}) collective-permute-start(f32[256,512]{1,0:T(8,128)S(1)} %get-tuple-element.28), channel_id=1, source_target_pairs={{0,2},{1,3},{2,4},{3,5},{4,6},{5,7},{6,32},{7,33},{8,10},{9,11},{1... | collective-permute-start | bytes 1572872 | tf_op jit(solution)/shard_map/ppermute | solution.py:104
  241.6 2.7 %multiply_add_fusion = (f32[256,512]{1,0:T(8,128)S(1)}, f32[256,512]{1,0:T(8,128)S(1)}) fusion(f32[256,512]{1,0:T(8,128)S(1)} %collective-permute-done.29, f32[256,512]{1,0:T(8,128)S(1)} %collective-permute-done.34, f32[256,512]{1,0:T(8,128)S(1)} %fusion.10, f32[]{:T(128)} %bitcast.24, f32[]{:T(128)} %bitcast.23, f32[]{:T(128)} %bitcast.21, ...), kind=kLoop, calls=%fused_computation.40 | loop fusion | flops 1048576 | bytes 3145744 | tf_op jit(solution)/shard_map/add | solution.py:229
  244.4 5.0 %collective-permute-start.32 = (f32[256,512]{1,0:T(8,128)S(1)}, f32[256,512]{1,0:T(8,128)S(1)}, u32[]{:S(2)}, u32[]{:S(2)}) collective-permute-start(f32[256,512]{1,0:T(8,128)S(1)} %get-tuple-element.26), channel_id=1, source_target_pairs={{0,2},{1,3},{2,4},{3,5},{4,6},{5,7},{6,32},{7,33},{8,10},{9,11},{1... | collective-permute-start | bytes 1572872 | tf_op jit(solution)/shard_map/ppermute | solution.py:104
  251.4 3.1 %collective-permute-done.24 = f32[256,512]{1,0:T(8,128)S(1)} collective-permute-done((f32[256,512]{1,0:T(8,128)S(1)}, f32[256,512]{1,0:T(8,128)S(1)}, u32[]{:S(2)}, u32[]{:S(2)}) %collective-permute-start.24) | collective-permute-done | bytes 524320 | tf_op jit(solution)/shard_map/ppermute | solution.py:104
  255.8 8.2 %collective-permute-done.32 = f32[256,512]{1,0:T(8,128)S(1)} collective-permute-done((f32[256,512]{1,0:T(8,128)S(1)}, f32[256,512]{1,0:T(8,128)S(1)}, u32[]{:S(2)}, u32[]{:S(2)}) %collective-permute-start.32) | collective-permute-done | bytes 524320 | tf_op jit(solution)/shard_map/ppermute | solution.py:104
  (110 shorter events, 73.5 us)
Async XLA Ops:
  0.8 27.8 %collective-permute-start = (s32[8]{0:T(128)S(1)}, s32[8]{0:T(128)S(1)}, u32[]{:S(2)}, u32[]{:S(2)}) collective-permute-start(s32[8]{0:T(128)S(1)} %pad_add_fusion), channel_id=1, source_target_pairs={{2,0},{3,1},{4,2},{5,3},{6,4},{7,5},{8,6},{9,7},{10,8},{11,9},{12,... | collective-permute-start | bytes 104 | tf_op jit(solution)/shard_map/ppermute | solution.py:104
  7.5 29.8 %collective-permute-start.1 = (s32[8]{0:T(128)S(1)}, s32[8]{0:T(128)S(1)}, u32[]{:S(2)}, u32[]{:S(2)}) collective-permute-start(s32[8]{0:T(128)S(1)} %pad_add_fusion), channel_id=1, source_target_pairs={{0,2},{1,3},{2,4},{3,5},{4,6},{5,7},{6,8},{7,9},{8,10},{9,11},{10,... | collective-permute-start | bytes 104 | tf_op jit(solution)/shard_map/ppermute | solution.py:104
  9.4 29.8 %collective-permute-start.2 = (s32[8]{0:T(128)S(1)}, s32[8]{0:T(128)S(1)}, u32[]{:S(2)}, u32[]{:S(2)}) collective-permute-start(s32[8]{0:T(128)S(1)} %pad_add_fusion), channel_id=1, source_target_pairs={{0,98},{1,99},{2,100},{3,101},{4,102},{5,103},{6,0},{7,1},{8,106},... | collective-permute-start | bytes 104 | tf_op jit(solution)/shard_map/ppermute | solution.py:104
  19.1 22.3 %collective-permute-start.3 = (s32[8]{0:T(128)S(1)}, s32[8]{0:T(128)S(1)}, u32[]{:S(2)}, u32[]{:S(2)}) collective-permute-start(s32[8]{0:T(128)S(1)} %pad_add_fusion), channel_id=1, source_target_pairs={{0,6},{1,7},{2,32},{3,33},{4,34},{5,35},{6,36},{7,37},{8,14},{9,15... | collective-permute-start | bytes 104 | tf_op jit(solution)/shard_map/ppermute | solution.py:104
  22.3 35.6 %collective-permute-start.5 = (f32[256,512]{1,0:T(8,128)S(1)}, f32[256,512]{1,0:T(8,128)S(1)}, u32[]{:S(2)}, u32[]{:S(2)}) collective-permute-start(f32[256,512]{1,0:T(8,128)S(1)} %get-tuple-element.15), channel_id=1, source_target_pairs={{0,1},{1,0},{2,3},{3,2},{4,5},{5,4},{6,7},{7,6},{8,9},{9,8},{10,11... | collective-permute-start | bytes 1572872 | tf_op jit(solution)/shard_map/ppermute | solution.py:104
  28.7 36.0 %collective-permute-start.9 = (f32[256,512]{1,0:T(8,128)S(1)}, f32[256,512]{1,0:T(8,128)}, u32[]{:S(2)}, u32[]{:S(2)}) collective-permute-start(f32[256,512]{1,0:T(8,128)S(1)} %get-tuple-element.15), channel_id=1, source_target_pairs={{32,6},{33,7},{34,32},{35,33},{36,34},{37,35},{38,36},{39,37},{40,... | collective-permute-start | bytes 1572872 | tf_op jit(solution)/shard_map/ppermute | solution.py:104
  37.3 29.8 %collective-permute-start.4 = (f32[256,512]{1,0:T(8,128)S(1)}, f32[256,512]{1,0:T(8,128)}, u32[]{:S(2)}, u32[]{:S(2)}) collective-permute-start(f32[256,512]{1,0:T(8,128)S(1)} %get-tuple-element.15), channel_id=1, source_target_pairs={{0,2},{1,3},{2,4},{3,5},{4,6},{5,7},{6,32},{7,33},{8,10},{9,11},{1... | collective-permute-start | bytes 1572872 | tf_op jit(solution)/shard_map/ppermute | solution.py:104
  39.2 22.3 %collective-permute-start.13 = (f32[256,512]{1,0:T(8,128)S(1)}, f32[256,512]{1,0:T(8,128)}, u32[]{:S(2)}, u32[]{:S(2)}) collective-permute-start(f32[256,512]{1,0:T(8,128)S(1)} %get-tuple-element.19), channel_id=1, source_target_pairs={{0,1},{1,0},{2,3},{3,2},{4,5},{5,4},{6,7},{7,6},{8,9},{9,8},{10,11... | collective-permute-start | bytes 1572872 | tf_op jit(solution)/shard_map/ppermute | solution.py:104
  41.4 43.8 %collective-permute-start.17 = (f32[256,512]{1,0:T(8,128)S(1)}, f32[256,512]{1,0:T(8,128)}, u32[]{:S(2)}, u32[]{:S(2)}) collective-permute-start(f32[256,512]{1,0:T(8,128)S(1)} %get-tuple-element.19), channel_id=1, source_target_pairs={{32,6},{33,7},{34,32},{35,33},{36,34},{37,35},{38,36},{39,37},{40,... | collective-permute-start | bytes 1572872 | tf_op jit(solution)/shard_map/ppermute | solution.py:104
  58.0 16.7 %collective-permute-start.6 = (f32[256,512]{1,0:T(8,128)S(1)}, f32[256,512]{1,0:T(8,128)S(1)}, u32[]{:S(2)}, u32[]{:S(2)}) collective-permute-start(f32[256,512]{1,0:T(8,128)S(1)} %multiply_add_fusion.19), channel_id=1, source_target_pairs={{6,14},{7,15},{8,0},{9,1},{14,22},{15,23},{16,8},{17,9},{22,30},{2... | collective-permute-start | bytes 1572872 | tf_op jit(solution)/shard_map/ppermute | solution.py:104
  61.6 23.7 %collective-permute-start.12 = (f32[256,512]{1,0:T(8,128)S(1)}, f32[256,512]{1,0:T(8,128)S(1)}, u32[]{:S(2)}, u32[]{:S(2)}) collective-permute-start(f32[256,512]{1,0:T(8,128)S(1)} %get-tuple-element.19), channel_id=1, source_target_pairs={{0,2},{1,3},{2,4},{3,5},{4,6},{5,7},{6,32},{7,33},{8,10},{9,11},{1... | collective-permute-start | bytes 1572872 | tf_op jit(solution)/shard_map/ppermute | solution.py:104
  64.6 20.6 %collective-permute-start.14 = (f32[256,512]{1,0:T(8,128)S(1)}, f32[256,512]{1,0:T(8,128)S(1)}, u32[]{:S(2)}, u32[]{:S(2)}) collective-permute-start(f32[256,512]{1,0:T(8,128)S(1)} %multiply_add_fusion.14), channel_id=1, source_target_pairs={{6,14},{7,15},{8,0},{9,1},{14,22},{15,23},{16,8},{17,9},{22,30},{2... | collective-permute-start | bytes 1572872 | tf_op jit(solution)/shard_map/ppermute | solution.py:104
  77.4 31.2 %collective-permute-start.10 = (f32[256,512]{1,0:T(8,128)S(1)}, f32[256,512]{1,0:T(8,128)S(1)}, u32[]{:S(2)}, u32[]{:S(2)}) collective-permute-start(f32[256,512]{1,0:T(8,128)S(1)} %get-tuple-element.41), channel_id=1, source_target_pairs={{0,100},{1,101},{2,102},{3,103},{4,0},{5,1},{6,2},{7,3},{8,108},{9... | collective-permute-start | bytes 1572872 | tf_op jit(solution)/shard_map/ppermute | solution.py:104
  79.3 29.3 %collective-permute-start.7 = (f32[256,512]{1,0:T(8,128)S(1)}, f32[256,512]{1,0:T(8,128)S(1)}, u32[]{:S(2)}, u32[]{:S(2)}) collective-permute-start(f32[256,512]{1,0:T(8,128)S(1)} %get-tuple-element.42), channel_id=1, source_target_pairs={{0,4},{1,5},{2,6},{3,7},{4,32},{5,33},{6,34},{7,35},{8,12},{9,13},... | collective-permute-start | bytes 1572872 | tf_op jit(solution)/shard_map/ppermute | solution.py:104
  87.6 38.5 %collective-permute-start.18 = (f32[256,512]{1,0:T(8,128)S(1)}, f32[256,512]{1,0:T(8,128)S(1)}, u32[]{:S(2)}, u32[]{:S(2)}) collective-permute-start(f32[256,512]{1,0:T(8,128)S(1)} %get-tuple-element.39), channel_id=1, source_target_pairs={{0,100},{1,101},{2,102},{3,103},{4,0},{5,1},{6,2},{7,3},{8,108},{9... | collective-permute-start | bytes 1572872 | tf_op jit(solution)/shard_map/ppermute | solution.py:104
  90.8 39.5 %collective-permute-start.15 = (f32[256,512]{1,0:T(8,128)S(1)}, f32[256,512]{1,0:T(8,128)S(1)}, u32[]{:S(2)}, u32[]{:S(2)}) collective-permute-start(f32[256,512]{1,0:T(8,128)S(1)} %get-tuple-element.40), channel_id=1, source_target_pairs={{0,4},{1,5},{2,6},{3,7},{4,32},{5,33},{6,34},{7,35},{8,12},{9,13},... | collective-permute-start | bytes 1572872 | tf_op jit(solution)/shard_map/ppermute | solution.py:104
  111.3 30.9 %collective-permute-start.8 = (f32[256,512]{1,0:T(8,128)S(1)}, f32[256,512]{1,0:T(8,128)S(1)}, u32[]{:S(2)}, u32[]{:S(2)}) collective-permute-start(f32[256,512]{1,0:T(8,128)S(1)} %get-tuple-element.32), channel_id=1, source_target_pairs={{0,2},{1,3},{2,4},{3,5},{4,6},{5,7},{6,32},{7,33},{8,10},{9,11},{1... | collective-permute-start | bytes 1572872 | tf_op jit(solution)/shard_map/ppermute | solution.py:104
  116.0 26.2 %collective-permute-start.11 = (f32[256,512]{1,0:T(8,128)S(1)}, f32[256,512]{1,0:T(8,128)S(1)}, u32[]{:S(2)}, u32[]{:S(2)}) collective-permute-start(f32[256,512]{1,0:T(8,128)S(1)} %get-tuple-element.31), channel_id=1, source_target_pairs={{0,102},{1,103},{2,0},{3,1},{4,2},{5,3},{6,4},{7,5},{8,110},{9,111... | collective-permute-start | bytes 1572872 | tf_op jit(solution)/shard_map/ppermute | solution.py:104
  134.1 19.0 %collective-permute-start.16 = (f32[256,512]{1,0:T(8,128)S(1)}, f32[256,512]{1,0:T(8,128)S(1)}, u32[]{:S(2)}, u32[]{:S(2)}) collective-permute-start(f32[256,512]{1,0:T(8,128)S(1)} %get-tuple-element.30), channel_id=1, source_target_pairs={{0,2},{1,3},{2,4},{3,5},{4,6},{5,7},{6,32},{7,33},{8,10},{9,11},{1... | collective-permute-start | bytes 1572872 | tf_op jit(solution)/shard_map/ppermute | solution.py:104
  157.2 19.3 %collective-permute-start.25 = (f32[256,512]{1,0:T(8,128)S(1)}, f32[256,512]{1,0:T(8,128)S(1)}, u32[]{:S(2)}, u32[]{:S(2)}) collective-permute-start(f32[256,512]{1,0:T(8,128)S(1)} %fusion.12), channel_id=1, source_target_pairs={{32,6},{33,7},{34,32},{35,33},{36,34},{37,35},{38,36},{39,37},{40,... | collective-permute-start | bytes 1572872 | tf_op jit(solution)/shard_map/ppermute | solution.py:104
  159.1 19.3 %collective-permute-start.20 = (f32[256,512]{1,0:T(8,128)S(1)}, f32[256,512]{1,0:T(8,128)S(1)}, u32[]{:S(2)}, u32[]{:S(2)}) collective-permute-start(f32[256,512]{1,0:T(8,128)S(1)} %fusion.12), channel_id=1, source_target_pairs={{0,2},{1,3},{2,4},{3,5},{4,6},{5,7},{6,32},{7,33},{8,10},{9,11},{1... | collective-permute-start | bytes 1572872 | tf_op jit(solution)/shard_map/ppermute | solution.py:104
  164.7 33.2 %collective-permute-start.33 = (f32[256,512]{1,0:T(8,128)S(1)}, f32[256,512]{1,0:T(8,128)S(1)}, u32[]{:S(2)}, u32[]{:S(2)}) collective-permute-start(f32[256,512]{1,0:T(8,128)S(1)} %fusion.10), channel_id=1, source_target_pairs={{32,6},{33,7},{34,32},{35,33},{36,34},{37,35},{38,36},{39,37},{40,... | collective-permute-start | bytes 1572872 | tf_op jit(solution)/shard_map/ppermute | solution.py:104
  171.0 16.7 %collective-permute-start.22 = (f32[256,512]{1,0:T(8,128)S(1)}, f32[256,512]{1,0:T(8,128)S(1)}, u32[]{:S(2)}, u32[]{:S(2)}) collective-permute-start(f32[256,512]{1,0:T(8,128)S(1)} %multiply_add_fusion.9), channel_id=1, source_target_pairs={{6,14},{7,15},{8,0},{9,1},{14,22},{15,23},{16,8},{17,9},{22,30},{2... | collective-permute-start | bytes 1572872 | tf_op jit(solution)/shard_map/ppermute | solution.py:104
  174.5 23.5 %collective-permute-start.28 = (f32[256,512]{1,0:T(8,128)S(1)}, f32[256,512]{1,0:T(8,128)S(1)}, u32[]{:S(2)}, u32[]{:S(2)}) collective-permute-start(f32[256,512]{1,0:T(8,128)S(1)} %fusion.10), channel_id=1, source_target_pairs={{0,2},{1,3},{2,4},{3,5},{4,6},{5,7},{6,32},{7,33},{8,10},{9,11},{1... | collective-permute-start | bytes 1572872 | tf_op jit(solution)/shard_map/ppermute | solution.py:104
  176.5 21.5 %collective-permute-start.30 = (f32[256,512]{1,0:T(8,128)S(1)}, f32[256,512]{1,0:T(8,128)S(1)}, u32[]{:S(2)}, u32[]{:S(2)}) collective-permute-start(f32[256,512]{1,0:T(8,128)S(1)} %multiply_add_fusion.4), channel_id=1, source_target_pairs={{6,14},{7,15},{8,0},{9,1},{14,22},{15,23},{16,8},{17,9},{22,30},{2... | collective-permute-start | bytes 1572872 | tf_op jit(solution)/shard_map/ppermute | solution.py:104
  189.1 24.7 %collective-permute-start.26 = (f32[256,512]{1,0:T(8,128)S(1)}, f32[256,512]{1,0:T(8,128)S(1)}, u32[]{:S(2)}, u32[]{:S(2)}) collective-permute-start(f32[256,512]{1,0:T(8,128)S(1)} %get-tuple-element.37), channel_id=1, source_target_pairs={{0,100},{1,101},{2,102},{3,103},{4,0},{5,1},{6,2},{7,3},{8,108},{9... | collective-permute-start | bytes 1572872 | tf_op jit(solution)/shard_map/ppermute | solution.py:104
  191.0 24.6 %collective-permute-start.23 = (f32[256,512]{1,0:T(8,128)S(1)}, f32[256,512]{1,0:T(8,128)S(1)}, u32[]{:S(2)}, u32[]{:S(2)}) collective-permute-start(f32[256,512]{1,0:T(8,128)S(1)} %get-tuple-element.38), channel_id=1, source_target_pairs={{0,4},{1,5},{2,6},{3,7},{4,32},{5,33},{6,34},{7,35},{8,12},{9,13},... | collective-permute-start | bytes 1572872 | tf_op jit(solution)/shard_map/ppermute | solution.py:104
  199.4 41.0 %collective-permute-start.34 = (f32[256,512]{1,0:T(8,128)S(1)}, f32[256,512]{1,0:T(8,128)S(1)}, u32[]{:S(2)}, u32[]{:S(2)}) collective-permute-start(f32[256,512]{1,0:T(8,128)S(1)} %get-tuple-element.35), channel_id=1, source_target_pairs={{0,100},{1,101},{2,102},{3,103},{4,0},{5,1},{6,2},{7,3},{8,108},{9... | collective-permute-start | bytes 1572872 | tf_op jit(solution)/shard_map/ppermute | solution.py:104
  201.4 40.2 %collective-permute-start.31 = (f32[256,512]{1,0:T(8,128)S(1)}, f32[256,512]{1,0:T(8,128)S(1)}, u32[]{:S(2)}, u32[]{:S(2)}) collective-permute-start(f32[256,512]{1,0:T(8,128)S(1)} %get-tuple-element.36), channel_id=1, source_target_pairs={{0,4},{1,5},{2,6},{3,7},{4,32},{5,33},{6,34},{7,35},{8,12},{9,13},... | collective-permute-start | bytes 1572872 | tf_op jit(solution)/shard_map/ppermute | solution.py:104
  218.3 36.1 %collective-permute-start.24 = (f32[256,512]{1,0:T(8,128)S(1)}, f32[256,512]{1,0:T(8,128)S(1)}, u32[]{:S(2)}, u32[]{:S(2)}) collective-permute-start(f32[256,512]{1,0:T(8,128)S(1)} %get-tuple-element.28), channel_id=1, source_target_pairs={{0,2},{1,3},{2,4},{3,5},{4,6},{5,7},{6,32},{7,33},{8,10},{9,11},{1... | collective-permute-start | bytes 1572872 | tf_op jit(solution)/shard_map/ppermute | solution.py:104
  237.4 17.1 %collective-permute-start.27 = (f32[256,512]{1,0:T(8,128)S(1)}, f32[256,512]{1,0:T(8,128)S(1)}, u32[]{:S(2)}, u32[]{:S(2)}) collective-permute-start(f32[256,512]{1,0:T(8,128)S(1)} %get-tuple-element.27), channel_id=1, source_target_pairs={{0,102},{1,103},{2,0},{3,1},{4,2},{5,3},{6,4},{7,5},{8,110},{9,111... | collective-permute-start | bytes 1572872 | tf_op jit(solution)/shard_map/ppermute | solution.py:104
  244.4 19.7 %collective-permute-start.32 = (f32[256,512]{1,0:T(8,128)S(1)}, f32[256,512]{1,0:T(8,128)S(1)}, u32[]{:S(2)}, u32[]{:S(2)}) collective-permute-start(f32[256,512]{1,0:T(8,128)S(1)} %get-tuple-element.26), channel_id=1, source_target_pairs={{0,2},{1,3},{2,4},{3,5},{4,6},{5,7},{6,32},{7,33},{8,10},{9,11},{1... | collective-permute-start | bytes 1572872 | tf_op jit(solution)/shard_map/ppermute | solution.py:104
  (14 other events, 247.2 us)
where the time goes:
time: 268 us; the launch traced here: 267 us
  starting transfers between devices  137 us (51%)
  waiting for transfers between devices  76.3 us (28%)
  other arithmetic  22.8 us (9%)
  matrix products  21.7 us (8%)
  between operations  5.92 us (2%)
  local copies, waits for them, and re-layouts  2.97 us (1%)
    ppermute x36, starting transfers between devices, send(): return lax.ppermute(x, AXES, pairs)  137 us
    ppermute x36, waiting for transfers between devices, send(): return lax.ppermute(x, AXES, pairs)  76.3 us
    dot_general x18, matrix products, mm(): return jnp.dot(a, b, precision=HIGH, preferred_element_type=jnp.float32)  16.2 us
    add x4, other arithmetic, sweep_pieces(): down = mid[-1] + picked[4] * p + picked[5] * m  12 us
    add x4, other arithmetic, sweep_pieces(): down = picked[1] * f[-1] + at_top * x  7.79 us
    dot_general x2, matrix products, build_dense(): dense = jnp.einsum('rxk,rkn->rxn', blocks, spread, precision=HIGH)  5.55 us
  transfers between devices with their start and end apart: 36, of which 13 were waited for; matrix products, arithmetic and copies ran while one was open for 16% of the time, Pallas kernels for 0%

commit v1 on v0

--- a/solution.py
+++ b/solution.py
@@ -119,27 +119,14 @@
 
 
 SOURCES = ("own", "far", "back", "ahead", "behind")
-ROW, COLUMN = 0, 4
-LINKS = (
-    ("ahead", COLUMN),
-    ("behind", COLUMN + 1),
-    ("far", ROW),
-    ("far", ROW + 1),
-    ("back", ROW + 3),
-    ("back", ROW + 2),
-    ("far", ROW),
-    ("far", ROW + 1),
-    ("back", ROW + 3),
-    ("back", ROW + 2),
-    ("own", ROW + 2),
-    ("own", ROW + 1),
-    None,
-    None,
-)
+LINK = {name: 8 * n for n, name in enumerate(SOURCES)}
+UNIT = 8 * len(SOURCES)
+AHEAD, BEHIND, UP, UP_MATE, DOWN, DOWN_MATE, OUT, OUT_MATE, MATE, FIRST_DIAGONAL, SECOND_DIAGONAL = range(11)
+COLUMN = 4
 
 
 def tables():
-    places = np.zeros((NI, NJ, len(LINKS), 3), np.int32)
+    places = np.zeros((NI * NJ, 11, 4), np.int32)
     for i in range(NI):
         for j in range(NJ):
             x, y, z, c = chip(i, j)
@@ -148,31 +135,28 @@
             down = pair(x, y, z - 3, c)[0]
             top, bottom = low == NLO - 1, low == 0
             odd, even = c == 1, c == 0
-            places[i, j] = [
-                (up, up - 1, up > 0),
-                (down, down + 1, down + 1 < NI),
-                (j, j + 2, not top),
-                (j + 1, j + 2, even and not top),
-                (j, j - 2, not bottom),
-                (j - 1, j - 2, odd and not bottom),
-                (j, j + 2, top),
-                (j + 1, j + 2, even and top),
-                (j, j - 2, bottom),
-                (j - 1, j - 2, odd and bottom),
-                (j + 1, j, even),
-                (j - 1, j, odd),
-                (i, i, True),
-                (j, j, True),
+            to_next = (j, j + 2, LINK["far"])
+            to_next_mate = (j + 1, j + 2, LINK["far"] + 1)
+            to_last = (j, j - 2, LINK["back"] + 3)
+            to_last_mate = (j - 1, j - 2, LINK["back"] + 2)
+            own_mate = (j + 1, j, LINK["own"] + 2) if even else (j - 1, j, LINK["own"] + 1)
+            places[i * NJ + j] = [
+                (up, up - 1, LINK["ahead"] + COLUMN, up > 0),
+                (down, down + 1, LINK["behind"] + COLUMN + 1, down + 1 < NI),
+                (*to_next, not top),
+                (*to_next_mate, even and not top),
+                (*to_last, not bottom),
+                (*to_last_mate, odd and not bottom),
+                (*(to_next if top else to_last), top or bottom),
+                (*(to_next_mate if top else to_last_mate), (top and even) or (bottom and odd)),
+                (*own_mate, True),
+                (i, i, UNIT, True),
+                (j, j, UNIT, True),
             ]
-    return places.reshape(NI * NJ, len(LINKS), 3)
+    return places
 
 
 TABLE = tables()
-CHOICE = np.zeros((len(LINKS), len(SOURCES) * 8), np.float32)
-for entry, link in enumerate(LINKS):
-    if link is not None:
-        CHOICE[entry, SOURCES.index(link[0]) * 8 + link[1]] = 1.0
-FREE = np.array([1.0 if link is None else 0.0 for link in LINKS], np.float32)
 
 
 def coefficients(occ_fock, row_links, column_links):
@@ -184,20 +168,21 @@
         "ahead": send(links, GOAL[1]),
         "behind": send(links, GOAL[-1]),
     }
-    flat = jnp.concatenate([got[name] for name in SOURCES]).astype(jnp.float32)
     where = lax.axis_index("ia") * NJ + lax.axis_index("ja")
     place = lax.dynamic_slice_in_dim(jnp.asarray(TABLE), where, 1, axis=0)[0]
-    rows, columns, used = place[:, 0], place[:, 1], place[:, 2]
+    rows, columns, link, used = place[:, 0], place[:, 1], place[:, 2], place[:, 3]
     spots = jnp.arange(NJ, dtype=jnp.int32)
     hot = (rows[:, None, None] == spots[None, :, None]) & (columns[:, None, None] == spots[None, None, :])
+    hot = hot & (used[:, None, None] > 0)
     picked = jnp.sum(jnp.where(hot, occ_fock[None], 0.0), axis=(1, 2))
-    weights = jnp.sum(jnp.asarray(CHOICE) * flat[None, :], axis=1) + jnp.asarray(FREE)
-    return picked * weights * used.astype(jnp.float32)
-
-
-def after(values, earlier):
-    kept = lax.optimization_barrier((*values, earlier))
-    return kept[: len(values)]
+    chosen = link[:, None] == jnp.arange(UNIT + 8, dtype=jnp.int32)[None, :]
+    flat = jnp.concatenate([got[name] for name in SOURCES] + [jnp.ones((8,), jnp.int32)])
+    weights = jnp.sum(jnp.where(chosen, flat[None, :], 0), axis=1)
+    return picked * weights.astype(jnp.float32)
+
+
+def after(value, earlier):
+    return lax.optimization_barrier((value, earlier))[0]
 
 
 def sweep_pieces(pieces, picked, low):
@@ -209,27 +194,27 @@
     out = None
     for p, m in zip(pieces, mates):
         if out is not None:
-            (m,) = after((m,), out)
-        out = (picked[6] + picked[8]) * p + (picked[7] + picked[9]) * m
+            p = after(p, out)
+        out = picked[OUT] * p + picked[OUT_MATE] * m
         crossed.append(send(out, ACROSS))
     middles = []
     up = None
     for f, x in zip(firsts, crossed):
         if up is not None:
-            (x,) = after((x,), up)
-        up = picked[0] * f[1] + at_bottom * x
-        down = picked[1] * f[-1] + at_top * x
+            x = after(x, up)
+        up = picked[AHEAD] * f[1] + at_bottom * x
+        down = picked[BEHIND] * f[-1] + at_top * x
         middles.append({1: send(up, MIDDLE[1]), -1: send(down, MIDDLE[-1])})
     gathered = []
     up = None
     for p, m, mid in zip(pieces, mates, middles):
         if up is not None:
-            p, m = after((p, m), up)
-        up = mid[1] + picked[2] * p + picked[3] * m
-        down = mid[-1] + picked[4] * p + picked[5] * m
+            p = after(p, up)
+        up = mid[1] + picked[UP] * p + picked[UP_MATE] * m
+        down = mid[-1] + picked[DOWN] * p + picked[DOWN_MATE] * m
         plus = send(up, LAST[1])
         minus = send(down, LAST[-1])
-        gathered.append(plus + minus + (picked[10] + picked[11]) * m)
+        gathered.append(plus + minus + picked[MATE] * m)
     return gathered
 
 
@@ -253,7 +238,7 @@
     for sweep_number in range(ITERS):
         if sweep_number == 0:
             picked = coefficients(occ_fock, row_links[0, 0], column_links[0, 0])
-            diagonal = picked[12] + picked[13]
+            diagonal = picked[FIRST_DIAGONAL] + picked[SECOND_DIAGONAL]
             fock_dense = build_dense(pao_fock, block_columns)
             intersection_dense = build_dense(pao_intersection, block_columns)
             shifted = fock_dense - diagonal * intersection_dense
@@ -262,9 +247,10 @@
         else:
             current = jnp.concatenate(pieces, axis=0)
         gathered = sweep_pieces(pieces, picked, low)
-        local = mm(mm(shifted, current), intersection_dense)
-        local = local + mm(mm(intersection_dense, current), fock_dense)
-        local = local + integral.astype(jnp.float32)
+        from_fock = mm(shifted, current)
+        from_intersection = mm(intersection_dense, current)
+        local = mm(from_fock, intersection_dense)
+        local = local + mm(from_intersection, fock_dense) + integral.astype(jnp.float32)
         rights = [mm(coupled, intersection_dense) for coupled in gathered]
         if sweep_number + 1 == ITERS:
             for right, span in zip(rights, spans):

time: 268 us -> 266 us (level)
  the two profiles are of different devices: /device:TPU:20 before, /device:TPU:21 now
where the time goes in v1:
time: 266 us; the launch traced here: 265 us
  starting transfers between devices  135 us (51%)
  waiting for transfers between devices  72.7 us (27%)
  other arithmetic  27.5 us (10%)
  matrix products  24 us (9%)
  local copies, waits for them, and re-layouts  2.94 us (1%)
    ppermute x36, starting transfers between devices, send(): return lax.ppermute(x, AXES, pairs)  135 us
    ppermute x36, waiting for transfers between devices, send(): return lax.ppermute(x, AXES, pairs)  72.7 us
    dot_general x18, matrix products, mm(): return jnp.dot(a, b, precision=HIGH, preferred_element_type=jnp.float32)  18.4 us
    add x4, other arithmetic, sweep_pieces(): down = mid[-1] + picked[DOWN] * p + picked[DOWN_MATE] * m  11.7 us
    add x4, other arithmetic, sweep_pieces(): down = picked[BEHIND] * f[-1] + at_top * x  7.77 us
    add x4, other arithmetic, sweep_pieces(): out = picked[OUT] * p + picked[OUT_MATE] * m  6.41 us
    dot_general x2, matrix products, build_dense(): dense = jnp.einsum('rxk,rkn->rxn', blocks, spread, precision=HIGH)  5.54 us
  transfers between devices with their start and end apart: 36, of which 15 were waited for; matrix products, arithmetic and copies ran while one was open for 18% of the time, Pallas kernels for 0%

profile of v1, /device:TPU:21, one launch (start us, length us, event | category | flops | bytes accessed | tf_op | source)
XLA Modules:
  0.0 264.5 jit_solution(17582216789827207200)
XLA Ops:
  0.8 6.4 %collective-permute-start.3 = (s32[8]{0:T(128)S(1)}, s32[8]{0:T(128)S(1)}, u32[]{:S(2)}, u32[]{:S(2)}) collective-permute-start(s32[8]{0:T(128)S(1)} %pad_add_fusion), channel_id=1, source_target_pairs={{0,6},{1,7},{2,32},{3,33},{4,34},{5,35},{6,36},{7,37},{8,14},{9,15... | collective-permute-start | bytes 104 | tf_op jit(solution)/shard_map/ppermute | solution.py:104
  7.2 7.7 %collective-permute-start.2 = (s32[8]{0:T(128)S(1)}, s32[8]{0:T(128)S(1)}, u32[]{:S(2)}, u32[]{:S(2)}) collective-permute-start(s32[8]{0:T(128)S(1)} %pad_add_fusion), channel_id=1, source_target_pairs={{0,98},{1,99},{2,100},{3,101},{4,102},{5,103},{6,0},{7,1},{8,106},... | collective-permute-start | bytes 104 | tf_op jit(solution)/shard_map/ppermute | solution.py:104
  17.6 5.3 %collective-permute-start = (s32[8]{0:T(128)S(1)}, s32[8]{0:T(128)S(1)}, u32[]{:S(2)}, u32[]{:S(2)}) collective-permute-start(s32[8]{0:T(128)S(1)} %pad_add_fusion), channel_id=1, source_target_pairs={{2,0},{3,1},{4,2},{5,3},{6,4},{7,5},{8,6},{9,7},{10,8},{11,9},{12,... | collective-permute-start | bytes 104 | tf_op jit(solution)/shard_map/ppermute | solution.py:104
  24.2 3.5 %collective-permute-start.9 = (f32[256,512]{1,0:T(8,128)S(1)}, f32[256,512]{1,0:T(8,128)}, u32[]{:S(2)}, u32[]{:S(2)}) collective-permute-start(f32[256,512]{1,0:T(8,128)S(1)} %get-tuple-element.13), channel_id=1, source_target_pairs={{32,6},{33,7},{34,32},{35,33},{36,34},{37,35},{38,36},{39,37},{40,... | collective-permute-start | bytes 1572872 | tf_op jit(solution)/shard_map/ppermute | solution.py:104
  28.7 3.1 %fusion.1 = f32[8,512,64]{1,2,0:T(8,128)S(1)} fusion(f32[8,64,384]{2,1,0:T(8,128)} %param.12, s32[8,384]{1,0:T(8,128)S(1)} %broadcast_add_fusion), kind=kOutput, calls=%fused_computation.2 | convolution fusion | flops 605552640 | bytes 1847296 | tf_op jit(solution)/shard_map/rxk,rkn->rxn/dot_general | solution.py:117
  32.0 3.7 %collective-permute-start.5 = (f32[256,512]{1,0:T(8,128)S(1)}, f32[256,512]{1,0:T(8,128)S(1)}, u32[]{:S(2)}, u32[]{:S(2)}) collective-permute-start(f32[256,512]{1,0:T(8,128)S(1)} %get-tuple-element.13), channel_id=1, source_target_pairs={{0,1},{1,0},{2,3},{3,2},{4,5},{5,4},{6,7},{7,6},{8,9},{9,8},{10,11... | collective-permute-start | bytes 1572872 | tf_op jit(solution)/shard_map/ppermute | solution.py:104
  37.7 5.5 %collective-permute-start.17 = (f32[256,512]{1,0:T(8,128)S(1)}, f32[256,512]{1,0:T(8,128)}, u32[]{:S(2)}, u32[]{:S(2)}) collective-permute-start(f32[256,512]{1,0:T(8,128)S(1)} %get-tuple-element.17), channel_id=1, source_target_pairs={{32,6},{33,7},{34,32},{35,33},{36,34},{37,35},{38,36},{39,37},{40,... | collective-permute-start | bytes 1572872 | tf_op jit(solution)/shard_map/ppermute | solution.py:104
  64.0 5.3 %collective-permute-done.6 = f32[256,512]{1,0:T(8,128)S(1)} collective-permute-done((f32[256,512]{1,0:T(8,128)S(1)}, f32[256,512]{1,0:T(8,128)S(1)}, u32[]{:S(2)}, u32[]{:S(2)}) %collective-permute-start.6) | collective-permute-done | bytes 524320 | tf_op jit(solution)/shard_map/ppermute | solution.py:104
  73.9 4.3 %collective-permute-start.7 = (f32[256,512]{1,0:T(8,128)S(1)}, f32[256,512]{1,0:T(8,128)S(1)}, u32[]{:S(2)}, u32[]{:S(2)}) collective-permute-start(f32[256,512]{1,0:T(8,128)S(1)} %get-tuple-element.38), channel_id=1, source_target_pairs={{0,4},{1,5},{2,6},{3,7},{4,32},{5,33},{6,34},{7,35},{8,12},{9,13},... | collective-permute-start | bytes 1572872 | tf_op jit(solution)/shard_map/ppermute | solution.py:104
  84.9 4.3 %collective-permute-start.15 = (f32[256,512]{1,0:T(8,128)S(1)}, f32[256,512]{1,0:T(8,128)S(1)}, u32[]{:S(2)}, u32[]{:S(2)}) collective-permute-start(f32[256,512]{1,0:T(8,128)S(1)} %get-tuple-element.36), channel_id=1, source_target_pairs={{0,4},{1,5},{2,6},{3,7},{4,32},{5,33},{6,34},{7,35},{8,12},{9,13},... | collective-permute-start | bytes 1572872 | tf_op jit(solution)/shard_map/ppermute | solution.py:104
  89.2 16.7 %collective-permute-done.10 = f32[256,512]{1,0:T(8,128)S(1)} collective-permute-done((f32[256,512]{1,0:T(8,128)S(1)}, f32[256,512]{1,0:T(8,128)S(1)}, u32[]{:S(2)}, u32[]{:S(2)}) %collective-permute-start.10) | collective-permute-done | bytes 524320 | tf_op jit(solution)/shard_map/ppermute | solution.py:104
  105.9 7.1 %collective-permute-done.7 = f32[256,512]{1,0:T(8,128)S(1)} collective-permute-done((f32[256,512]{1,0:T(8,128)S(1)}, f32[256,512]{1,0:T(8,128)S(1)}, u32[]{:S(2)}, u32[]{:S(2)}) %collective-permute-start.7) | collective-permute-done | bytes 524320 | tf_op jit(solution)/shard_map/ppermute | solution.py:104
  113.0 2.7 %multiply_add_fusion.15 = (f32[256,512]{1,0:T(8,128)S(1)}, f32[256,512]{1,0:T(8,128)S(1)}) fusion(f32[256,512]{1,0:T(8,128)S(1)} %collective-permute-done.5, f32[256,512]{1,0:T(8,128)S(1)} %collective-permute-done.10, f32[256,512]{1,0:T(8,128)S(1)} %get-tuple-element.13, f32[]{:T(128)} %bitcast.25, f32[]{:T(128)} %bitcast.24, f32[]{:T(128)} %bitcast.22, ...), kind=kLoop, calls=%fused_computation.68 | loop fusion | flops 1048576 | bytes 3145744 | tf_op jit(solution)/shard_map/add | solution.py:214
  117.6 3.4 %collective-permute-start.8 = (f32[256,512]{1,0:T(8,128)S(1)}, f32[256,512]{1,0:T(8,128)S(1)}, u32[]{:S(2)}, u32[]{:S(2)}) collective-permute-start(f32[256,512]{1,0:T(8,128)S(1)} %get-tuple-element.28), channel_id=1, source_target_pairs={{0,2},{1,3},{2,4},{3,5},{4,6},{5,7},{6,32},{7,33},{8,10},{9,11},{1... | collective-permute-start | bytes 1572872 | tf_op jit(solution)/shard_map/ppermute | solution.py:104
  121.2 3.0 %collective-permute-done.15 = f32[256,512]{1,0:T(8,128)S(1)} collective-permute-done((f32[256,512]{1,0:T(8,128)S(1)}, f32[256,512]{1,0:T(8,128)S(1)}, u32[]{:S(2)}, u32[]{:S(2)}) %collective-permute-start.15) | collective-permute-done | bytes 524320 | tf_op jit(solution)/shard_map/ppermute | solution.py:104
  124.2 3.7 %multiply_add_fusion.10 = (f32[256,512]{1,0:T(8,128)S(1)}, f32[256,512]{1,0:T(8,128)S(1)}) fusion(f32[256,512]{1,0:T(8,128)} %collective-permute-done.13, f32[256,512]{1,0:T(8,128)S(1)} %collective-permute-done.18, f32[256,512]{1,0:T(8,128)S(1)} %get-tuple-element.17, f32[]{:T(128)} %bitcast.25, f32[]{:T(128)} %bitcast.24, f32[]{:T(128)} %bitcast.22, ...), kind=kLoop, calls=%fused_computation.59 | loop fusion | flops 1048576 | bytes 3145744 | tf_op jit(solution)/shard_map/add | solution.py:214
  129.9 4.0 %collective-permute-start.16 = (f32[256,512]{1,0:T(8,128)S(1)}, f32[256,512]{1,0:T(8,128)S(1)}, u32[]{:S(2)}, u32[]{:S(2)}) collective-permute-start(f32[256,512]{1,0:T(8,128)S(1)} %get-tuple-element.26), channel_id=1, source_target_pairs={{0,2},{1,3},{2,4},{3,5},{4,6},{5,7},{6,32},{7,33},{8,10},{9,11},{1... | collective-permute-start | bytes 1572872 | tf_op jit(solution)/shard_map/ppermute | solution.py:104
  138.4 3.5 %collective-permute-done.19 = f32[256,512]{1,0:T(8,128)S(1)} collective-permute-done((f32[256,512]{1,0:T(8,128)S(1)}, f32[256,512]{1,0:T(8,128)S(1)}, u32[]{:S(2)}, u32[]{:S(2)}) %collective-permute-start.19) | collective-permute-done | bytes 524320 | tf_op jit(solution)/shard_map/ppermute | solution.py:104
  141.9 5.0 %collective-permute-done.16 = f32[256,512]{1,0:T(8,128)S(1)} collective-permute-done((f32[256,512]{1,0:T(8,128)S(1)}, f32[256,512]{1,0:T(8,128)S(1)}, u32[]{:S(2)}, u32[]{:S(2)}) %collective-permute-start.16) | collective-permute-done | bytes 524320 | tf_op jit(solution)/shard_map/ppermute | solution.py:104
  149.7 4.1 %collective-permute-start.21 = (f32[256,512]{1,0:T(8,128)S(1)}, f32[256,512]{1,0:T(8,128)S(1)}, u32[]{:S(2)}, u32[]{:S(2)}) collective-permute-start(f32[256,512]{1,0:T(8,128)S(1)} %fusion.12), channel_id=1, source_target_pairs={{0,1},{1,0},{2,3},{3,2},{4,5},{5,4},{6,7},{7,6},{8,9},{9,8},{10,11... | collective-permute-start | bytes 1572872 | tf_op jit(solution)/shard_map/ppermute | solution.py:104
  158.1 3.0 %collective-permute-start.25 = (f32[256,512]{1,0:T(8,128)S(1)}, f32[256,512]{1,0:T(8,128)S(1)}, u32[]{:S(2)}, u32[]{:S(2)}) collective-permute-start(f32[256,512]{1,0:T(8,128)S(1)} %fusion.12), channel_id=1, source_target_pairs={{32,6},{33,7},{34,32},{35,33},{36,34},{37,35},{38,36},{39,37},{40,... | collective-permute-start | bytes 1572872 | tf_op jit(solution)/shard_map/ppermute | solution.py:104
  172.0 9.8 %collective-permute-done.25 = f32[256,512]{1,0:T(8,128)S(1)} collective-permute-done((f32[256,512]{1,0:T(8,128)S(1)}, f32[256,512]{1,0:T(8,128)S(1)}, u32[]{:S(2)}, u32[]{:S(2)}) %collective-permute-start.25) | collective-permute-done | bytes 524320 | tf_op jit(solution)/shard_map/ppermute | solution.py:104
  187.5 4.3 %collective-permute-start.23 = (f32[256,512]{1,0:T(8,128)S(1)}, f32[256,512]{1,0:T(8,128)S(1)}, u32[]{:S(2)}, u32[]{:S(2)}) collective-permute-start(f32[256,512]{1,0:T(8,128)S(1)} %get-tuple-element.34), channel_id=1, source_target_pairs={{0,4},{1,5},{2,6},{3,7},{4,32},{5,33},{6,34},{7,35},{8,12},{9,13},... | collective-permute-start | bytes 1572872 | tf_op jit(solution)/shard_map/ppermute | solution.py:104
  192.9 3.4 %collective-permute-done.30 = f32[256,512]{1,0:T(8,128)S(1)} collective-permute-done((f32[256,512]{1,0:T(8,128)S(1)}, f32[256,512]{1,0:T(8,128)S(1)}, u32[]{:S(2)}, u32[]{:S(2)}) %collective-permute-start.30) | collective-permute-done | bytes 524320 | tf_op jit(solution)/shard_map/ppermute | solution.py:104
  199.5 4.3 %collective-permute-start.31 = (f32[256,512]{1,0:T(8,128)S(1)}, f32[256,512]{1,0:T(8,128)S(1)}, u32[]{:S(2)}, u32[]{:S(2)}) collective-permute-start(f32[256,512]{1,0:T(8,128)S(1)} %get-tuple-element.32), channel_id=1, source_target_pairs={{0,4},{1,5},{2,6},{3,7},{4,32},{5,33},{6,34},{7,35},{8,12},{9,13},... | collective-permute-start | bytes 1572872 | tf_op jit(solution)/shard_map/ppermute | solution.py:104
  208.6 22.6 %collective-permute-start.27 = (f32[256,512]{1,0:T(8,128)S(1)}, f32[256,512]{1,0:T(8,128)S(1)}, u32[]{:S(2)}, u32[]{:S(2)}) collective-permute-start(f32[256,512]{1,0:T(8,128)S(1)} %get-tuple-element.23), channel_id=1, source_target_pairs={{0,102},{1,103},{2,0},{3,1},{4,2},{5,3},{6,4},{7,5},{8,110},{9,111... | collective-permute-start | bytes 1572872 | tf_op jit(solution)/shard_map/ppermute | solution.py:104
  231.2 3.8 %collective-permute-start.24 = (f32[256,512]{1,0:T(8,128)S(1)}, f32[256,512]{1,0:T(8,128)S(1)}, u32[]{:S(2)}, u32[]{:S(2)}) collective-permute-start(f32[256,512]{1,0:T(8,128)S(1)} %get-tuple-element.24), channel_id=1, source_target_pairs={{0,2},{1,3},{2,4},{3,5},{4,6},{5,7},{6,32},{7,33},{8,10},{9,11},{1... | collective-permute-start | bytes 1572872 | tf_op jit(solution)/shard_map/ppermute | solution.py:104
  238.8 3.8 %collective-permute-start.35 = (f32[256,512]{1,0:T(8,128)S(1)}, f32[256,512]{1,0:T(8,128)S(1)}, u32[]{:S(2)}, u32[]{:S(2)}) collective-permute-start(f32[256,512]{1,0:T(8,128)S(1)} %get-tuple-element.21), channel_id=1, source_target_pairs={{0,102},{1,103},{2,0},{3,1},{4,2},{5,3},{6,4},{7,5},{8,110},{9,111... | collective-permute-start | bytes 1572872 | tf_op jit(solution)/shard_map/ppermute | solution.py:104
  242.7 4.1 %collective-permute-start.32 = (f32[256,512]{1,0:T(8,128)S(1)}, f32[256,512]{1,0:T(8,128)S(1)}, u32[]{:S(2)}, u32[]{:S(2)}) collective-permute-start(f32[256,512]{1,0:T(8,128)S(1)} %get-tuple-element.22), channel_id=1, source_target_pairs={{0,2},{1,3},{2,4},{3,5},{4,6},{5,7},{6,32},{7,33},{8,10},{9,11},{1... | collective-permute-start | bytes 1572872 | tf_op jit(solution)/shard_map/ppermute | solution.py:104
  246.8 3.5 %collective-permute-done.24 = f32[256,512]{1,0:T(8,128)S(1)} collective-permute-done((f32[256,512]{1,0:T(8,128)S(1)}, f32[256,512]{1,0:T(8,128)S(1)}, u32[]{:S(2)}, u32[]{:S(2)}) %collective-permute-start.24) | collective-permute-done | bytes 524320 | tf_op jit(solution)/shard_map/ppermute | solution.py:104
  252.2 4.8 %collective-permute-done.35 = f32[256,512]{1,0:T(8,128)S(1)} collective-permute-done((f32[256,512]{1,0:T(8,128)S(1)}, f32[256,512]{1,0:T(8,128)S(1)}, u32[]{:S(2)}, u32[]{:S(2)}) %collective-permute-start.35) | collective-permute-done | bytes 524320 | tf_op jit(solution)/shard_map/ppermute | solution.py:104
  257.0 4.5 %collective-permute-done.32 = f32[256,512]{1,0:T(8,128)S(1)} collective-permute-done((f32[256,512]{1,0:T(8,128)S(1)}, f32[256,512]{1,0:T(8,128)S(1)}, u32[]{:S(2)}, u32[]{:S(2)}) %collective-permute-start.32) | collective-permute-done | bytes 524320 | tf_op jit(solution)/shard_map/ppermute | solution.py:104
  (107 shorter events, 88.4 us)
Async XLA Ops:
  0.8 31.2 %collective-permute-start.3 = (s32[8]{0:T(128)S(1)}, s32[8]{0:T(128)S(1)}, u32[]{:S(2)}, u32[]{:S(2)}) collective-permute-start(s32[8]{0:T(128)S(1)} %pad_add_fusion), channel_id=1, source_target_pairs={{0,6},{1,7},{2,32},{3,33},{4,34},{5,35},{6,36},{7,37},{8,14},{9,15... | collective-permute-start | bytes 104 | tf_op jit(solution)/shard_map/ppermute | solution.py:104
  7.2 28.5 %collective-permute-start.2 = (s32[8]{0:T(128)S(1)}, s32[8]{0:T(128)S(1)}, u32[]{:S(2)}, u32[]{:S(2)}) collective-permute-start(s32[8]{0:T(128)S(1)} %pad_add_fusion), channel_id=1, source_target_pairs={{0,98},{1,99},{2,100},{3,101},{4,102},{5,103},{6,0},{7,1},{8,106},... | collective-permute-start | bytes 104 | tf_op jit(solution)/shard_map/ppermute | solution.py:104
  14.9 22.8 %collective-permute-start.1 = (s32[8]{0:T(128)S(1)}, s32[8]{0:T(128)S(1)}, u32[]{:S(2)}, u32[]{:S(2)}) collective-permute-start(s32[8]{0:T(128)S(1)} %pad_add_fusion), channel_id=1, source_target_pairs={{0,2},{1,3},{2,4},{3,5},{4,6},{5,7},{6,8},{7,9},{8,10},{9,11},{10,... | collective-permute-start | bytes 104 | tf_op jit(solution)/shard_map/ppermute | solution.py:104
  17.6 25.6 %collective-permute-start = (s32[8]{0:T(128)S(1)}, s32[8]{0:T(128)S(1)}, u32[]{:S(2)}, u32[]{:S(2)}) collective-permute-start(s32[8]{0:T(128)S(1)} %pad_add_fusion), channel_id=1, source_target_pairs={{2,0},{3,1},{4,2},{5,3},{6,4},{7,5},{8,6},{9,7},{10,8},{11,9},{12,... | collective-permute-start | bytes 104 | tf_op jit(solution)/shard_map/ppermute | solution.py:104
  24.2 37.6 %collective-permute-start.9 = (f32[256,512]{1,0:T(8,128)S(1)}, f32[256,512]{1,0:T(8,128)}, u32[]{:S(2)}, u32[]{:S(2)}) collective-permute-start(f32[256,512]{1,0:T(8,128)S(1)} %get-tuple-element.13), channel_id=1, source_target_pairs={{32,6},{33,7},{34,32},{35,33},{36,34},{37,35},{38,36},{39,37},{40,... | collective-permute-start | bytes 1572872 | tf_op jit(solution)/shard_map/ppermute | solution.py:104
  32.0 20.6 %collective-permute-start.5 = (f32[256,512]{1,0:T(8,128)S(1)}, f32[256,512]{1,0:T(8,128)S(1)}, u32[]{:S(2)}, u32[]{:S(2)}) collective-permute-start(f32[256,512]{1,0:T(8,128)S(1)} %get-tuple-element.13), channel_id=1, source_target_pairs={{0,1},{1,0},{2,3},{3,2},{4,5},{5,4},{6,7},{7,6},{8,9},{9,8},{10,11... | collective-permute-start | bytes 1572872 | tf_op jit(solution)/shard_map/ppermute | solution.py:104
  35.8 28.2 %collective-permute-start.4 = (f32[256,512]{1,0:T(8,128)S(1)}, f32[256,512]{1,0:T(8,128)}, u32[]{:S(2)}, u32[]{:S(2)}) collective-permute-start(f32[256,512]{1,0:T(8,128)S(1)} %get-tuple-element.13), channel_id=1, source_target_pairs={{0,2},{1,3},{2,4},{3,5},{4,6},{5,7},{6,32},{7,33},{8,10},{9,11},{1... | collective-permute-start | bytes 1572872 | tf_op jit(solution)/shard_map/ppermute | solution.py:104
  37.7 42.9 %collective-permute-start.17 = (f32[256,512]{1,0:T(8,128)S(1)}, f32[256,512]{1,0:T(8,128)}, u32[]{:S(2)}, u32[]{:S(2)}) collective-permute-start(f32[256,512]{1,0:T(8,128)S(1)} %get-tuple-element.17), channel_id=1, source_target_pairs={{32,6},{33,7},{34,32},{35,33},{36,34},{37,35},{38,36},{39,37},{40,... | collective-permute-start | bytes 1572872 | tf_op jit(solution)/shard_map/ppermute | solution.py:104
  54.0 15.4 %collective-permute-start.6 = (f32[256,512]{1,0:T(8,128)S(1)}, f32[256,512]{1,0:T(8,128)S(1)}, u32[]{:S(2)}, u32[]{:S(2)}) collective-permute-start(f32[256,512]{1,0:T(8,128)S(1)} %multiply_add_fusion.19), channel_id=1, source_target_pairs={{6,14},{7,15},{8,0},{9,1},{14,22},{15,23},{16,8},{17,9},{22,30},{2... | collective-permute-start | bytes 1572872 | tf_op jit(solution)/shard_map/ppermute | solution.py:104
  57.5 23.1 %collective-permute-start.12 = (f32[256,512]{1,0:T(8,128)S(1)}, f32[256,512]{1,0:T(8,128)S(1)}, u32[]{:S(2)}, u32[]{:S(2)}) collective-permute-start(f32[256,512]{1,0:T(8,128)S(1)} %get-tuple-element.17), channel_id=1, source_target_pairs={{0,2},{1,3},{2,4},{3,5},{4,6},{5,7},{6,32},{7,33},{8,10},{9,11},{1... | collective-permute-start | bytes 1572872 | tf_op jit(solution)/shard_map/ppermute | solution.py:104
  61.8 18.8 %collective-permute-start.14 = (f32[256,512]{1,0:T(8,128)S(1)}, f32[256,512]{1,0:T(8,128)S(1)}, u32[]{:S(2)}, u32[]{:S(2)}) collective-permute-start(f32[256,512]{1,0:T(8,128)S(1)} %multiply_add_fusion.14), channel_id=1, source_target_pairs={{6,14},{7,15},{8,0},{9,1},{14,22},{15,23},{16,8},{17,9},{22,30},{2... | collective-permute-start | bytes 1572872 | tf_op jit(solution)/shard_map/ppermute | solution.py:104
  72.0 33.9 %collective-permute-start.10 = (f32[256,512]{1,0:T(8,128)S(1)}, f32[256,512]{1,0:T(8,128)S(1)}, u32[]{:S(2)}, u32[]{:S(2)}) collective-permute-start(f32[256,512]{1,0:T(8,128)S(1)} %get-tuple-element.37), channel_id=1, source_target_pairs={{0,100},{1,101},{2,102},{3,103},{4,0},{5,1},{6,2},{7,3},{8,108},{9... | collective-permute-start | bytes 1572872 | tf_op jit(solution)/shard_map/ppermute | solution.py:104
  73.9 39.1 %collective-permute-start.7 = (f32[256,512]{1,0:T(8,128)S(1)}, f32[256,512]{1,0:T(8,128)S(1)}, u32[]{:S(2)}, u32[]{:S(2)}) collective-permute-start(f32[256,512]{1,0:T(8,128)S(1)} %get-tuple-element.38), channel_id=1, source_target_pairs={{0,4},{1,5},{2,6},{3,7},{4,32},{5,33},{6,34},{7,35},{8,12},{9,13},... | collective-permute-start | bytes 1572872 | tf_op jit(solution)/shard_map/ppermute | solution.py:104
  83.0 38.2 %collective-permute-start.18 = (f32[256,512]{1,0:T(8,128)S(1)}, f32[256,512]{1,0:T(8,128)S(1)}, u32[]{:S(2)}, u32[]{:S(2)}) collective-permute-start(f32[256,512]{1,0:T(8,128)S(1)} %get-tuple-element.35), channel_id=1, source_target_pairs={{0,100},{1,101},{2,102},{3,103},{4,0},{5,1},{6,2},{7,3},{8,108},{9... | collective-permute-start | bytes 1572872 | tf_op jit(solution)/shard_map/ppermute | solution.py:104
  84.9 39.3 %collective-permute-start.15 = (f32[256,512]{1,0:T(8,128)S(1)}, f32[256,512]{1,0:T(8,128)S(1)}, u32[]{:S(2)}, u32[]{:S(2)}) collective-permute-start(f32[256,512]{1,0:T(8,128)S(1)} %get-tuple-element.36), channel_id=1, source_target_pairs={{0,4},{1,5},{2,6},{3,7},{4,32},{5,33},{6,34},{7,35},{8,12},{9,13},... | collective-permute-start | bytes 1572872 | tf_op jit(solution)/shard_map/ppermute | solution.py:104
  115.7 18.1 %collective-permute-start.11 = (f32[256,512]{1,0:T(8,128)S(1)}, f32[256,512]{1,0:T(8,128)S(1)}, u32[]{:S(2)}, u32[]{:S(2)}) collective-permute-start(f32[256,512]{1,0:T(8,128)S(1)} %get-tuple-element.27), channel_id=1, source_target_pairs={{0,102},{1,103},{2,0},{3,1},{4,2},{5,3},{6,4},{7,5},{8,110},{9,111... | collective-permute-start | bytes 1572872 | tf_op jit(solution)/shard_map/ppermute | solution.py:104
  117.6 18.7 %collective-permute-start.8 = (f32[256,512]{1,0:T(8,128)S(1)}, f32[256,512]{1,0:T(8,128)S(1)}, u32[]{:S(2)}, u32[]{:S(2)}) collective-permute-start(f32[256,512]{1,0:T(8,128)S(1)} %get-tuple-element.28), channel_id=1, source_target_pairs={{0,2},{1,3},{2,4},{3,5},{4,6},{5,7},{6,32},{7,33},{8,10},{9,11},{1... | collective-permute-start | bytes 1572872 | tf_op jit(solution)/shard_map/ppermute | solution.py:104
  129.9 17.1 %collective-permute-start.16 = (f32[256,512]{1,0:T(8,128)S(1)}, f32[256,512]{1,0:T(8,128)S(1)}, u32[]{:S(2)}, u32[]{:S(2)}) collective-permute-start(f32[256,512]{1,0:T(8,128)S(1)} %get-tuple-element.26), channel_id=1, source_target_pairs={{0,2},{1,3},{2,4},{3,5},{4,6},{5,7},{6,32},{7,33},{8,10},{9,11},{1... | collective-permute-start | bytes 1572872 | tf_op jit(solution)/shard_map/ppermute | solution.py:104
  154.2 42.0 %collective-permute-start.33 = (f32[256,512]{1,0:T(8,128)S(1)}, f32[256,512]{1,0:T(8,128)S(1)}, u32[]{:S(2)}, u32[]{:S(2)}) collective-permute-start(f32[256,512]{1,0:T(8,128)S(1)} %fusion.10), channel_id=1, source_target_pairs={{32,6},{33,7},{34,32},{35,33},{36,34},{37,35},{38,36},{39,37},{40,... | collective-permute-start | bytes 1572872 | tf_op jit(solution)/shard_map/ppermute | solution.py:104
  158.1 23.6 %collective-permute-start.25 = (f32[256,512]{1,0:T(8,128)S(1)}, f32[256,512]{1,0:T(8,128)S(1)}, u32[]{:S(2)}, u32[]{:S(2)}) collective-permute-start(f32[256,512]{1,0:T(8,128)S(1)} %fusion.12), channel_id=1, source_target_pairs={{32,6},{33,7},{34,32},{35,33},{36,34},{37,35},{38,36},{39,37},{40,... | collective-permute-start | bytes 1572872 | tf_op jit(solution)/shard_map/ppermute | solution.py:104
  161.1 23.1 %collective-permute-start.20 = (f32[256,512]{1,0:T(8,128)S(1)}, f32[256,512]{1,0:T(8,128)S(1)}, u32[]{:S(2)}, u32[]{:S(2)}) collective-permute-start(f32[256,512]{1,0:T(8,128)S(1)} %fusion.12), channel_id=1, source_target_pairs={{0,2},{1,3},{2,4},{3,5},{4,6},{5,7},{6,32},{7,33},{8,10},{9,11},{1... | collective-permute-start | bytes 1572872 | tf_op jit(solution)/shard_map/ppermute | solution.py:104
  165.5 18.8 %collective-permute-start.22 = (f32[256,512]{1,0:T(8,128)S(1)}, f32[256,512]{1,0:T(8,128)S(1)}, u32[]{:S(2)}, u32[]{:S(2)}) collective-permute-start(f32[256,512]{1,0:T(8,128)S(1)} %multiply_add_fusion.9), channel_id=1, source_target_pairs={{6,14},{7,15},{8,0},{9,1},{14,22},{15,23},{16,8},{17,9},{22,30},{2... | collective-permute-start | bytes 1572872 | tf_op jit(solution)/shard_map/ppermute | solution.py:104
  168.7 27.5 %collective-permute-start.28 = (f32[256,512]{1,0:T(8,128)S(1)}, f32[256,512]{1,0:T(8,128)S(1)}, u32[]{:S(2)}, u32[]{:S(2)}) collective-permute-start(f32[256,512]{1,0:T(8,128)S(1)} %fusion.10), channel_id=1, source_target_pairs={{0,2},{1,3},{2,4},{3,5},{4,6},{5,7},{6,32},{7,33},{8,10},{9,11},{1... | collective-permute-start | bytes 1572872 | tf_op jit(solution)/shard_map/ppermute | solution.py:104
  181.7 14.5 %collective-permute-start.30 = (f32[256,512]{1,0:T(8,128)S(1)}, f32[256,512]{1,0:T(8,128)S(1)}, u32[]{:S(2)}, u32[]{:S(2)}) collective-permute-start(f32[256,512]{1,0:T(8,128)S(1)} %multiply_add_fusion.4), channel_id=1, source_target_pairs={{6,14},{7,15},{8,0},{9,1},{14,22},{15,23},{16,8},{17,9},{22,30},{2... | collective-permute-start | bytes 1572872 | tf_op jit(solution)/shard_map/ppermute | solution.py:104
  185.6 18.6 %collective-permute-start.26 = (f32[256,512]{1,0:T(8,128)S(1)}, f32[256,512]{1,0:T(8,128)S(1)}, u32[]{:S(2)}, u32[]{:S(2)}) collective-permute-start(f32[256,512]{1,0:T(8,128)S(1)} %get-tuple-element.33), channel_id=1, source_target_pairs={{0,100},{1,101},{2,102},{3,103},{4,0},{5,1},{6,2},{7,3},{8,108},{9... | collective-permute-start | bytes 1572872 | tf_op jit(solution)/shard_map/ppermute | solution.py:104
  187.5 18.4 %collective-permute-start.23 = (f32[256,512]{1,0:T(8,128)S(1)}, f32[256,512]{1,0:T(8,128)S(1)}, u32[]{:S(2)}, u32[]{:S(2)}) collective-permute-start(f32[256,512]{1,0:T(8,128)S(1)} %get-tuple-element.34), channel_id=1, source_target_pairs={{0,4},{1,5},{2,6},{3,7},{4,32},{5,33},{6,34},{7,35},{8,12},{9,13},... | collective-permute-start | bytes 1572872 | tf_op jit(solution)/shard_map/ppermute | solution.py:104
  197.6 38.5 %collective-permute-start.34 = (f32[256,512]{1,0:T(8,128)S(1)}, f32[256,512]{1,0:T(8,128)S(1)}, u32[]{:S(2)}, u32[]{:S(2)}) collective-permute-start(f32[256,512]{1,0:T(8,128)S(1)} %get-tuple-element.31), channel_id=1, source_target_pairs={{0,100},{1,101},{2,102},{3,103},{4,0},{5,1},{6,2},{7,3},{8,108},{9... | collective-permute-start | bytes 1572872 | tf_op jit(solution)/shard_map/ppermute | solution.py:104
  199.5 36.6 %collective-permute-start.31 = (f32[256,512]{1,0:T(8,128)S(1)}, f32[256,512]{1,0:T(8,128)S(1)}, u32[]{:S(2)}, u32[]{:S(2)}) collective-permute-start(f32[256,512]{1,0:T(8,128)S(1)} %get-tuple-element.32), channel_id=1, source_target_pairs={{0,4},{1,5},{2,6},{3,7},{4,32},{5,33},{6,34},{7,35},{8,12},{9,13},... | collective-permute-start | bytes 1572872 | tf_op jit(solution)/shard_map/ppermute | solution.py:104
  208.6 38.2 %collective-permute-start.27 = (f32[256,512]{1,0:T(8,128)S(1)}, f32[256,512]{1,0:T(8,128)S(1)}, u32[]{:S(2)}, u32[]{:S(2)}) collective-permute-start(f32[256,512]{1,0:T(8,128)S(1)} %get-tuple-element.23), channel_id=1, source_target_pairs={{0,102},{1,103},{2,0},{3,1},{4,2},{5,3},{6,4},{7,5},{8,110},{9,111... | collective-permute-start | bytes 1572872 | tf_op jit(solution)/shard_map/ppermute | solution.py:104
  231.2 19.0 %collective-permute-start.24 = (f32[256,512]{1,0:T(8,128)S(1)}, f32[256,512]{1,0:T(8,128)S(1)}, u32[]{:S(2)}, u32[]{:S(2)}) collective-permute-start(f32[256,512]{1,0:T(8,128)S(1)} %get-tuple-element.24), channel_id=1, source_target_pairs={{0,2},{1,3},{2,4},{3,5},{4,6},{5,7},{6,32},{7,33},{8,10},{9,11},{1... | collective-permute-start | bytes 1572872 | tf_op jit(solution)/shard_map/ppermute | solution.py:104
  238.8 18.1 %collective-permute-start.35 = (f32[256,512]{1,0:T(8,128)S(1)}, f32[256,512]{1,0:T(8,128)S(1)}, u32[]{:S(2)}, u32[]{:S(2)}) collective-permute-start(f32[256,512]{1,0:T(8,128)S(1)} %get-tuple-element.21), channel_id=1, source_target_pairs={{0,102},{1,103},{2,0},{3,1},{4,2},{5,3},{6,4},{7,5},{8,110},{9,111... | collective-permute-start | bytes 1572872 | tf_op jit(solution)/shard_map/ppermute | solution.py:104
  242.7 18.9 %collective-permute-start.32 = (f32[256,512]{1,0:T(8,128)S(1)}, f32[256,512]{1,0:T(8,128)S(1)}, u32[]{:S(2)}, u32[]{:S(2)}) collective-permute-start(f32[256,512]{1,0:T(8,128)S(1)} %get-tuple-element.22), channel_id=1, source_target_pairs={{0,2},{1,3},{2,4},{3,5},{4,6},{5,7},{6,32},{7,33},{8,10},{9,11},{1... | collective-permute-start | bytes 1572872 | tf_op jit(solution)/shard_map/ppermute | solution.py:104
  (12 other events, 187.3 us)

commit v2 on v1

--- a/solution.py
+++ b/solution.py
@@ -121,12 +121,13 @@
 SOURCES = ("own", "far", "back", "ahead", "behind")
 LINK = {name: 8 * n for n, name in enumerate(SOURCES)}
 UNIT = 8 * len(SOURCES)
-AHEAD, BEHIND, UP, UP_MATE, DOWN, DOWN_MATE, OUT, OUT_MATE, MATE, FIRST_DIAGONAL, SECOND_DIAGONAL = range(11)
+AHEAD, BEHIND, PLUS, PLUS_MATE, MINUS, MINUS_MATE, FIRST_DIAGONAL, SECOND_DIAGONAL = range(8)
+UP, UP_MATE, DOWN, DOWN_MATE, OUT, OUT_MATE, MATE = range(7)
 COLUMN = 4
 
 
 def tables():
-    places = np.zeros((NI * NJ, 11, 4), np.int32)
+    places = np.zeros((NI * NJ, 15, 4), np.int32)
     for i in range(NI):
         for j in range(NJ):
             x, y, z, c = chip(i, j)
@@ -143,6 +144,12 @@
             places[i * NJ + j] = [
                 (up, up - 1, LINK["ahead"] + COLUMN, up > 0),
                 (down, down + 1, LINK["behind"] + COLUMN + 1, down + 1 < NI),
+                (j + 8, j + 6, LINK["ahead"] + 3, bottom),
+                (j + 7, j + 6, LINK["ahead"] + 2, bottom and odd),
+                (j - 8, j - 6, LINK["behind"], top),
+                (j - 7, j - 6, LINK["behind"] + 1, top and even),
+                (i, i, UNIT, True),
+                (j, j, UNIT, True),
                 (*to_next, not top),
                 (*to_next_mate, even and not top),
                 (*to_last, not bottom),
@@ -150,71 +157,81 @@
                 (*(to_next if top else to_last), top or bottom),
                 (*(to_next_mate if top else to_last_mate), (top and even) or (bottom and odd)),
                 (*own_mate, True),
-                (i, i, UNIT, True),
-                (j, j, UNIT, True),
             ]
-    return places
+    places[..., 0] = np.where(places[..., 3] > 0, places[..., 0], -1)
+    return places[..., :3].astype(np.int8)
 
 
 TABLE = tables()
+
+
+def chosen(place, occ_fock, got):
+    rows, columns, link = place[:, 0], place[:, 1], place[:, 2]
+    spots = jnp.arange(NJ, dtype=jnp.int32)
+    hot = (rows[:, None, None] == spots[None, :, None]) & (columns[:, None, None] == spots[None, None, :])
+    picked = jnp.sum(jnp.where(hot, occ_fock[None], 0.0), axis=(1, 2))
+    nothing = jnp.zeros((8,), jnp.int32)
+    flat = jnp.concatenate([got.get(name, nothing) for name in SOURCES] + [jnp.ones((8,), jnp.int32)])
+    taken = link[:, None] == jnp.arange(UNIT + 8, dtype=jnp.int32)[None, :]
+    weights = jnp.sum(jnp.where(taken, flat[None, :], 0), axis=1)
+    return picked * weights.astype(jnp.float32)
 
 
 def coefficients(occ_fock, row_links, column_links):
     links = jnp.concatenate([row_links, column_links, jnp.zeros((2,), jnp.int32)])
-    got = {
-        "own": links,
-        "far": send(links, along_j(-2)),
-        "back": send(links, along_j(2)),
-        "ahead": send(links, GOAL[1]),
-        "behind": send(links, GOAL[-1]),
-    }
     where = lax.axis_index("ia") * NJ + lax.axis_index("ja")
-    place = lax.dynamic_slice_in_dim(jnp.asarray(TABLE), where, 1, axis=0)[0]
-    rows, columns, link, used = place[:, 0], place[:, 1], place[:, 2], place[:, 3]
-    spots = jnp.arange(NJ, dtype=jnp.int32)
-    hot = (rows[:, None, None] == spots[None, :, None]) & (columns[:, None, None] == spots[None, None, :])
-    hot = hot & (used[:, None, None] > 0)
-    picked = jnp.sum(jnp.where(hot, occ_fock[None], 0.0), axis=(1, 2))
-    chosen = link[:, None] == jnp.arange(UNIT + 8, dtype=jnp.int32)[None, :]
-    flat = jnp.concatenate([got[name] for name in SOURCES] + [jnp.ones((8,), jnp.int32)])
-    weights = jnp.sum(jnp.where(chosen, flat[None, :], 0), axis=1)
-    return picked * weights.astype(jnp.float32)
+    place = lax.dynamic_slice_in_dim(jnp.asarray(TABLE), where, 1, axis=0)[0].astype(jnp.int32)
+    first = {"ahead": send(links, GOAL[1]), "behind": send(links, GOAL[-1])}
+    rest = {"own": links, "far": send(links, along_j(-2)), "back": send(links, along_j(2))}
+    return chosen(place[:8], occ_fock, first), chosen(place[8:], occ_fock, rest)
 
 
 def after(value, earlier):
     return lax.optimization_barrier((value, earlier))[0]
 
 
-def sweep_pieces(pieces, picked, low):
+def sweep_pieces(pieces, first, rest, low, raw):
     at_top = (low == NLO - 1).astype(jnp.float32)
     at_bottom = (low == 0).astype(jnp.float32)
     mates = [send(p, PARTNER) for p in pieces]
     firsts = [{s: send(p, FIRST[s]) for s in (1, -1)} for p in pieces]
-    crossed = []
-    out = None
-    for p, m in zip(pieces, mates):
-        if out is not None:
-            p = after(p, out)
-        out = picked[OUT] * p + picked[OUT_MATE] * m
-        crossed.append(send(out, ACROSS))
+    if raw:
+        crossed = [send(p, ACROSS) for p in pieces]
+        others = [send(x, PARTNER) for x in crossed]
+    else:
+        crossed = []
+        out = None
+        for p, m in zip(pieces, mates):
+            if out is not None:
+                p = after(p, out)
+            out = rest[OUT] * p + rest[OUT_MATE] * m
+            crossed.append(send(out, ACROSS))
     middles = []
-    up = None
-    for f, x in zip(firsts, crossed):
-        if up is not None:
-            x = after(x, up)
-        up = picked[AHEAD] * f[1] + at_bottom * x
-        down = picked[BEHIND] * f[-1] + at_top * x
+    done = None
+    for k, (f, x) in enumerate(zip(firsts, crossed)):
+        up, down = f[1], f[-1]
+        if done is not None:
+            up = after(up, done)
+        if raw:
+            up = first[AHEAD] * up + first[PLUS] * x + first[PLUS_MATE] * others[k]
+            down = first[BEHIND] * after(down, up) + first[MINUS] * x + first[MINUS_MATE] * others[k]
+        else:
+            up = first[AHEAD] * up + at_bottom * x
+            down = first[BEHIND] * after(down, up) + at_top * x
         middles.append({1: send(up, MIDDLE[1]), -1: send(down, MIDDLE[-1])})
+        done = down
     gathered = []
-    up = None
+    done = None
     for p, m, mid in zip(pieces, mates, middles):
-        if up is not None:
-            p = after(p, up)
-        up = mid[1] + picked[UP] * p + picked[UP_MATE] * m
-        down = mid[-1] + picked[DOWN] * p + picked[DOWN_MATE] * m
+        up, down = mid[1], mid[-1]
+        if done is not None:
+            up = after(up, done)
+        up = up + rest[UP] * p + rest[UP_MATE] * m
+        down = after(down, up) + rest[DOWN] * p + rest[DOWN_MATE] * m
         plus = send(up, LAST[1])
         minus = send(down, LAST[-1])
-        gathered.append(plus + minus + picked[MATE] * m)
+        gathered.append(plus + minus + rest[MATE] * m)
+        done = down
     return gathered
 
 
@@ -237,8 +254,8 @@
     pieces = list(lax.optimization_barrier(tuple(start[span] for span in spans)))
     for sweep_number in range(ITERS):
         if sweep_number == 0:
-            picked = coefficients(occ_fock, row_links[0, 0], column_links[0, 0])
-            diagonal = picked[FIRST_DIAGONAL] + picked[SECOND_DIAGONAL]
+            first, rest = coefficients(occ_fock, row_links[0, 0], column_links[0, 0])
+            diagonal = first[FIRST_DIAGONAL] + first[SECOND_DIAGONAL]
             fock_dense = build_dense(pao_fock, block_columns)
             intersection_dense = build_dense(pao_intersection, block_columns)
             shifted = fock_dense - diagonal * intersection_dense
@@ -246,7 +263,7 @@
             current = start
         else:
             current = jnp.concatenate(pieces, axis=0)
-        gathered = sweep_pieces(pieces, picked, low)
+        gathered = sweep_pieces(pieces, first, rest, low, sweep_number == 0)
         from_fock = mm(shifted, current)
         from_intersection = mm(intersection_dense, current)
         local = mm(from_fock, intersection_dense)
@@ -256,10 +273,10 @@
             for right, span in zip(rights, spans):
                 local = local - mm(intersection_dense[:, span], right)
             return (current - local * inverse_gap)[None, None]
-        rest = [local[span] for span in spans]
+        parts = [local[span] for span in spans]
         for k, right in enumerate(rights):
-            rest = [r - mm(intersection_dense[span, spans[k]], right) for r, span in zip(rest, spans)]
-        pieces = [p - r * inverse_gap[span] for p, r, span in zip(pieces, rest, spans)]
+            parts = [r - mm(intersection_dense[span, spans[k]], right) for r, span in zip(parts, spans)]
+        pieces = [p - r * inverse_gap[span] for p, r, span in zip(pieces, parts, spans)]
 
 
 def solution(mesh):

time: 266 us -> 275 us (1.034)
  the two profiles are of different devices: /device:TPU:21 before, /device:TPU:18 now
where the time goes in v2:
time: 275 us; the launch traced here: 274 us
  starting transfers between devices  131 us (48%)
  waiting for transfers between devices  84.4 us (31%)
  other arithmetic  30.2 us (11%)
  matrix products  22.8 us (8%)
  local copies, waits for them, and re-layouts  2.99 us (1%)
    ppermute x38, starting transfers between devices, send(): return lax.ppermute(x, AXES, pairs)  131 us
    ppermute x38, waiting for transfers between devices, send(): return lax.ppermute(x, AXES, pairs)  84.4 us
    dot_general x18, matrix products, mm(): return jnp.dot(a, b, precision=HIGH, preferred_element_type=jnp.float32)  17.3 us
    add x4, other arithmetic, sweep_pieces(): up = up + rest[UP] * p + rest[UP_MATE] * m  5.72 us
    add x4, other arithmetic, sweep_pieces(): down = after(down, up) + rest[DOWN] * p + rest[DOWN_MATE] * m  5.66 us
    dot_general x2, matrix products, build_dense(): dense = jnp.einsum('rxk,rkn->rxn', blocks, spread, precision=HIGH)  5.52 us
  transfers between devices with their start and end apart: 38, of which 15 were waited for; matrix products, arithmetic and copies ran while one was open for 18% of the time, Pallas kernels for 0%

profile of v2, /device:TPU:18, one launch (start us, length us, event | category | flops | bytes accessed | tf_op | source)
XLA Modules:
  0.0 273.7 jit_solution(14417607185014083054)
XLA Ops:
  0.8 3.9 %collective-permute-start.7 = (s32[8]{0:T(128)S(1)}, s32[8]{0:T(128)S(1)}, u32[]{:S(2)}, u32[]{:S(2)}) collective-permute-start(s32[8]{0:T(128)S(1)} %pad_add_fusion), channel_id=1, source_target_pairs={{0,2},{1,3},{2,4},{3,5},{4,6},{5,7},{6,8},{7,9},{8,10},{9,11},{10,... | collective-permute-start | bytes 104 | tf_op jit(solution)/shard_map/ppermute | solution.py:104
  4.8 4.7 %collective-permute-start.6 = (s32[8]{0:T(128)S(1)}, s32[8]{0:T(128)S(1)}, u32[]{:S(2)}, u32[]{:S(2)}) collective-permute-start(s32[8]{0:T(128)S(1)} %pad_add_fusion), channel_id=1, source_target_pairs={{2,0},{3,1},{4,2},{5,3},{6,4},{7,5},{8,6},{9,7},{10,8},{11,9},{12,... | collective-permute-start | bytes 104 | tf_op jit(solution)/shard_map/ppermute | solution.py:104
  9.5 3.8 %collective-permute-start.1 = (s32[8]{0:T(128)S(1)}, s32[8]{0:T(128)S(1)}, u32[]{:S(2)}, u32[]{:S(2)}) collective-permute-start(s32[8]{0:T(128)S(1)} %pad_add_fusion), channel_id=1, source_target_pairs={{0,6},{1,7},{2,32},{3,33},{4,34},{5,35},{6,36},{7,37},{8,14},{9,15... | collective-permute-start | bytes 104 | tf_op jit(solution)/shard_map/ppermute | solution.py:104
  13.3 7.7 %collective-permute-start = (s32[8]{0:T(128)S(1)}, s32[8]{0:T(128)S(1)}, u32[]{:S(2)}, u32[]{:S(2)}) collective-permute-start(s32[8]{0:T(128)S(1)} %pad_add_fusion), channel_id=1, source_target_pairs={{0,98},{1,99},{2,100},{3,101},{4,102},{5,103},{6,0},{7,1},{8,106},... | collective-permute-start | bytes 104 | tf_op jit(solution)/shard_map/ppermute | solution.py:104
  22.3 5.5 %collective-permute-start.10 = (f32[256,512]{1,0:T(8,128)S(1)}, f32[256,512]{1,0:T(8,128)}, u32[]{:S(2)}, u32[]{:S(2)}) collective-permute-start(f32[256,512]{1,0:T(8,128)S(1)} %get-tuple-element.20), channel_id=1, source_target_pairs={{32,6},{33,7},{34,32},{35,33},{36,34},{37,35},{38,36},{39,37},{40,... | collective-permute-start | bytes 1572872 | tf_op jit(solution)/shard_map/ppermute | solution.py:104
  29.4 3.1 %fusion.1 = f32[8,512,64]{1,2,0:T(8,128)S(1)} fusion(f32[8,64,384]{2,1,0:T(8,128)} %param.12, s32[8,384]{1,0:T(8,128)S(1)} %broadcast_add_fusion), kind=kOutput, calls=%fused_computation.2 | convolution fusion | flops 605552640 | bytes 1847296 | tf_op jit(solution)/shard_map/rxk,rkn->rxn/dot_general | solution.py:117
  34.4 2.5 collective-permute-start.3
  44.0 2.5 fusion.17
  55.9 4.4 %collective-permute-start.19 = (f32[256,512]{1,0:T(8,128)S(1)}, f32[256,512]{1,0:T(8,128)S(1)}, u32[]{:S(2)}, u32[]{:S(2)}) collective-permute-start(f32[256,512]{1,0:T(8,128)S(1)} %get-tuple-element.23), channel_id=1, source_target_pairs={{32,6},{33,7},{34,32},{35,33},{36,34},{37,35},{38,36},{39,37},{40,... | collective-permute-start | bytes 1572872 | tf_op jit(solution)/shard_map/ppermute | solution.py:104
  65.7 3.2 %multiply_add_fusion.17 = f32[256,512]{1,0:T(8,128)S(1)} fusion(f32[256,512]{1,0:T(8,128)S(1)} %collective-permute-done.4, f32[256,512]{1,0:T(8,128)} %collective-permute-done.3, f32[256,512]{1,0:T(8,128)S(1)} %collective-permute-done.2, f32[]{:T(128)} %bitcast.20, f32[]{:T(128)} %bitcast.19, f32[]{:T(128)} %bitcast.18), kind=kLoop, calls=%fused_computation.70 | loop fusion | flops 655360 | bytes 2097164 | tf_op jit(solution)/shard_map/add | solution.py:216
  71.3 3.2 %multiply_add_fusion.15 = f32[256,512]{1,0:T(8,128)S(1)} fusion(f32[256,512]{1,0:T(8,128)S(1)} %collective-permute-done.4, f32[256,512]{1,0:T(8,128)} %collective-permute-done.3, f32[256,512]{1,0:T(8,128)} %collective-permute-done.10, f32[]{:T(128)} %bitcast.28, f32[]{:T(128)} %bitcast.27, f32[]{:T(128)} %bitcast.26), kind=kLoop, calls=%fused_computation.68 | loop fusion | flops 655360 | bytes 2097164 | tf_op jit(solution)/shard_map/add | solution.py:217
  74.5 4.9 %collective-permute-done.13 = f32[256,512]{1,0:T(8,128)S(1)} collective-permute-done((f32[256,512]{1,0:T(8,128)S(1)}, f32[256,512]{1,0:T(8,128)S(1)}, u32[]{:S(2)}, u32[]{:S(2)}) %collective-permute-start.13) | collective-permute-done | bytes 524320 | tf_op jit(solution)/shard_map/ppermute | solution.py:104
  81.3 4.8 %collective-permute-start.5 = (f32[256,512]{1,0:T(8,128)S(1)}, f32[256,512]{1,0:T(8,128)S(1)}, u32[]{:S(2)}, u32[]{:S(2)}) collective-permute-start(f32[256,512]{1,0:T(8,128)S(1)} %multiply_add_fusion.17), channel_id=1, source_target_pairs={{0,4},{1,5},{2,6},{3,7},{4,32},{5,33},{6,34},{7,35},{8,12},{9,13},... | collective-permute-start | bytes 1572872 | tf_op jit(solution)/shard_map/ppermute | solution.py:104
  92.1 6.0 %collective-permute-start.20 = (f32[256,512]{1,0:T(8,128)S(1)}, f32[256,512]{1,0:T(8,128)S(1)}, u32[]{:S(2)}, u32[]{:S(2)}) collective-permute-start(f32[256,512]{1,0:T(8,128)S(1)} %multiply_add_fusion.11), channel_id=1, source_target_pairs={{0,100},{1,101},{2,102},{3,103},{4,0},{5,1},{6,2},{7,3},{8,108},{9... | collective-permute-start | bytes 1572872 | tf_op jit(solution)/shard_map/ppermute | solution.py:104
  98.2 13.4 %collective-permute-done.5 = f32[256,512]{1,0:T(8,128)S(1)} collective-permute-done((f32[256,512]{1,0:T(8,128)S(1)}, f32[256,512]{1,0:T(8,128)S(1)}, u32[]{:S(2)}, u32[]{:S(2)}) %collective-permute-start.5) | collective-permute-done | bytes 524320 | tf_op jit(solution)/shard_map/ppermute | solution.py:104
  113.0 3.7 %collective-permute-start.9 = (f32[256,512]{1,0:T(8,128)S(1)}, f32[256,512]{1,0:T(8,128)S(1)}, u32[]{:S(2)}, u32[]{:S(2)}) collective-permute-start(f32[256,512]{1,0:T(8,128)S(1)} %multiply_add_fusion.16), channel_id=1, source_target_pairs={{0,2},{1,3},{2,4},{3,5},{4,6},{5,7},{6,32},{7,33},{8,10},{9,11},{1... | collective-permute-start | bytes 1572872 | tf_op jit(solution)/shard_map/ppermute | solution.py:104
  118.2 3.3 %collective-permute-start.12 = (f32[256,512]{1,0:T(8,128)S(1)}, f32[256,512]{1,0:T(8,128)S(1)}, u32[]{:S(2)}, u32[]{:S(2)}) collective-permute-start(f32[256,512]{1,0:T(8,128)S(1)} %multiply_add_fusion.14), channel_id=1, source_target_pairs={{0,102},{1,103},{2,0},{3,1},{4,2},{5,3},{6,4},{7,5},{8,110},{9,111... | collective-permute-start | bytes 1572872 | tf_op jit(solution)/shard_map/ppermute | solution.py:104
  121.5 9.9 %collective-permute-done.16 = f32[256,512]{1,0:T(8,128)S(1)} collective-permute-done((f32[256,512]{1,0:T(8,128)S(1)}, f32[256,512]{1,0:T(8,128)S(1)}, u32[]{:S(2)}, u32[]{:S(2)}) %collective-permute-start.16) | collective-permute-done | bytes 524320 | tf_op jit(solution)/shard_map/ppermute | solution.py:104
  132.9 5.9 %collective-permute-start.18 = (f32[256,512]{1,0:T(8,128)S(1)}, f32[256,512]{1,0:T(8,128)S(1)}, u32[]{:S(2)}, u32[]{:S(2)}) collective-permute-start(f32[256,512]{1,0:T(8,128)S(1)} %multiply_add_fusion.12), channel_id=1, source_target_pairs={{0,2},{1,3},{2,4},{3,5},{4,6},{5,7},{6,32},{7,33},{8,10},{9,11},{1... | collective-permute-start | bytes 1572872 | tf_op jit(solution)/shard_map/ppermute | solution.py:104
  142.3 2.9 %collective-permute-done.9 = f32[256,512]{1,0:T(8,128)S(1)} collective-permute-done((f32[256,512]{1,0:T(8,128)S(1)}, f32[256,512]{1,0:T(8,128)S(1)}, u32[]{:S(2)}, u32[]{:S(2)}) %collective-permute-start.9) | collective-permute-done | bytes 524320 | tf_op jit(solution)/shard_map/ppermute | solution.py:104
  147.2 5.9 %collective-permute-done.21 = f32[256,512]{1,0:T(8,128)S(1)} collective-permute-done((f32[256,512]{1,0:T(8,128)S(1)}, f32[256,512]{1,0:T(8,128)S(1)}, u32[]{:S(2)}, u32[]{:S(2)}) %collective-permute-start.21) | collective-permute-done | bytes 524320 | tf_op jit(solution)/shard_map/ppermute | solution.py:104
  156.8 3.4 %collective-permute-start.35 = (f32[256,512]{1,0:T(8,128)S(1)}, f32[256,512]{1,0:T(8,128)S(1)}, u32[]{:S(2)}, u32[]{:S(2)}) collective-permute-start(f32[256,512]{1,0:T(8,128)S(1)} %fusion.10), channel_id=1, source_target_pairs={{32,6},{33,7},{34,32},{35,33},{36,34},{37,35},{38,36},{39,37},{40,... | collective-permute-start | bytes 1572872 | tf_op jit(solution)/shard_map/ppermute | solution.py:104
  176.8 7.1 %collective-permute-start.27 = (f32[256,512]{1,0:T(8,128)S(1)}, f32[256,512]{1,0:T(8,128)S(1)}, u32[]{:S(2)}, u32[]{:S(2)}) collective-permute-start(f32[256,512]{1,0:T(8,128)S(1)} %fusion.12), channel_id=1, source_target_pairs={{32,6},{33,7},{34,32},{35,33},{36,34},{37,35},{38,36},{39,37},{40,... | collective-permute-start | bytes 1572872 | tf_op jit(solution)/shard_map/ppermute | solution.py:104
  185.3 6.4 %collective-permute-done.22 = f32[256,512]{1,0:T(8,128)S(1)} collective-permute-done((f32[256,512]{1,0:T(8,128)S(1)}, f32[256,512]{1,0:T(8,128)S(1)}, u32[]{:S(2)}, u32[]{:S(2)}) %collective-permute-start.22) | collective-permute-done | bytes 524320 | tf_op jit(solution)/shard_map/ppermute | solution.py:104
  197.5 6.0 %collective-permute-start.28 = (f32[256,512]{1,0:T(8,128)S(1)}, f32[256,512]{1,0:T(8,128)S(1)}, u32[]{:S(2)}, u32[]{:S(2)}) collective-permute-start(f32[256,512]{1,0:T(8,128)S(1)} %multiply_add_fusion.6), channel_id=1, source_target_pairs={{0,100},{1,101},{2,102},{3,103},{4,0},{5,1},{6,2},{7,3},{8,108},{9... | collective-permute-start | bytes 1572872 | tf_op jit(solution)/shard_map/ppermute | solution.py:104
  203.5 3.5 %collective-permute-done.32 = f32[256,512]{1,0:T(8,128)S(1)} collective-permute-done((f32[256,512]{1,0:T(8,128)S(1)}, f32[256,512]{1,0:T(8,128)S(1)}, u32[]{:S(2)}, u32[]{:S(2)}) %collective-permute-start.32) | collective-permute-done | bytes 524320 | tf_op jit(solution)/shard_map/ppermute | solution.py:104
  210.5 6.0 %collective-permute-start.36 = (f32[256,512]{1,0:T(8,128)S(1)}, f32[256,512]{1,0:T(8,128)S(1)}, u32[]{:S(2)}, u32[]{:S(2)}) collective-permute-start(f32[256,512]{1,0:T(8,128)S(1)} %multiply_add_fusion.1), channel_id=1, source_target_pairs={{0,100},{1,101},{2,102},{3,103},{4,0},{5,1},{6,2},{7,3},{8,108},{9... | collective-permute-start | bytes 1572872 | tf_op jit(solution)/shard_map/ppermute | solution.py:104
  216.6 16.9 %collective-permute-done.25 = f32[256,512]{1,0:T(8,128)S(1)} collective-permute-done((f32[256,512]{1,0:T(8,128)S(1)}, f32[256,512]{1,0:T(8,128)S(1)}, u32[]{:S(2)}, u32[]{:S(2)}) %collective-permute-start.25) | collective-permute-done | bytes 524320 | tf_op jit(solution)/shard_map/ppermute | solution.py:104
  238.3 5.1 %collective-permute-start.29 = (f32[256,512]{1,0:T(8,128)S(1)}, f32[256,512]{1,0:T(8,128)S(1)}, u32[]{:S(2)}, u32[]{:S(2)}) collective-permute-start(f32[256,512]{1,0:T(8,128)S(1)} %multiply_add_fusion.5), channel_id=1, source_target_pairs={{0,102},{1,103},{2,0},{3,1},{4,2},{5,3},{6,4},{7,5},{8,110},{9,111... | collective-permute-start | bytes 1572872 | tf_op jit(solution)/shard_map/ppermute | solution.py:104
  249.5 6.7 %collective-permute-start.37 = (f32[256,512]{1,0:T(8,128)S(1)}, f32[256,512]{1,0:T(8,128)S(1)}, u32[]{:S(2)}, u32[]{:S(2)}) collective-permute-start(f32[256,512]{1,0:T(8,128)S(1)} %multiply_add_fusion), channel_id=1, source_target_pairs={{0,102},{1,103},{2,0},{3,1},{4,2},{5,3},{6,4},{7,5},{8,110},{9,111... | collective-permute-start | bytes 1572872 | tf_op jit(solution)/shard_map/ppermute | solution.py:104
  256.2 5.0 %collective-permute-done.29 = f32[256,512]{1,0:T(8,128)S(1)} collective-permute-done((f32[256,512]{1,0:T(8,128)S(1)}, f32[256,512]{1,0:T(8,128)S(1)}, u32[]{:S(2)}, u32[]{:S(2)}) %collective-permute-start.29) | collective-permute-done | bytes 524320 | tf_op jit(solution)/shard_map/ppermute | solution.py:104
  263.1 7.6 %collective-permute-done.37 = f32[256,512]{1,0:T(8,128)S(1)} collective-permute-done((f32[256,512]{1,0:T(8,128)S(1)}, f32[256,512]{1,0:T(8,128)S(1)}, u32[]{:S(2)}, u32[]{:S(2)}) %collective-permute-start.37) | collective-permute-done | bytes 524320 | tf_op jit(solution)/shard_map/ppermute | solution.py:104
  (125 shorter events, 92.6 us)
Async XLA Ops:
  0.8 31.6 %collective-permute-start.7 = (s32[8]{0:T(128)S(1)}, s32[8]{0:T(128)S(1)}, u32[]{:S(2)}, u32[]{:S(2)}) collective-permute-start(s32[8]{0:T(128)S(1)} %pad_add_fusion), channel_id=1, source_target_pairs={{0,2},{1,3},{2,4},{3,5},{4,6},{5,7},{6,8},{7,9},{8,10},{9,11},{10,... | collective-permute-start | bytes 104 | tf_op jit(solution)/shard_map/ppermute | solution.py:104
  4.8 29.6 %collective-permute-start.6 = (s32[8]{0:T(128)S(1)}, s32[8]{0:T(128)S(1)}, u32[]{:S(2)}, u32[]{:S(2)}) collective-permute-start(s32[8]{0:T(128)S(1)} %pad_add_fusion), channel_id=1, source_target_pairs={{2,0},{3,1},{4,2},{5,3},{6,4},{7,5},{8,6},{9,7},{10,8},{11,9},{12,... | collective-permute-start | bytes 104 | tf_op jit(solution)/shard_map/ppermute | solution.py:104
  9.5 28.4 %collective-permute-start.1 = (s32[8]{0:T(128)S(1)}, s32[8]{0:T(128)S(1)}, u32[]{:S(2)}, u32[]{:S(2)}) collective-permute-start(s32[8]{0:T(128)S(1)} %pad_add_fusion), channel_id=1, source_target_pairs={{0,6},{1,7},{2,32},{3,33},{4,34},{5,35},{6,36},{7,37},{8,14},{9,15... | collective-permute-start | bytes 104 | tf_op jit(solution)/shard_map/ppermute | solution.py:104
  13.3 26.5 %collective-permute-start = (s32[8]{0:T(128)S(1)}, s32[8]{0:T(128)S(1)}, u32[]{:S(2)}, u32[]{:S(2)}) collective-permute-start(s32[8]{0:T(128)S(1)} %pad_add_fusion), channel_id=1, source_target_pairs={{0,98},{1,99},{2,100},{3,101},{4,102},{5,103},{6,0},{7,1},{8,106},... | collective-permute-start | bytes 104 | tf_op jit(solution)/shard_map/ppermute | solution.py:104
  22.3 46.6 %collective-permute-start.10 = (f32[256,512]{1,0:T(8,128)S(1)}, f32[256,512]{1,0:T(8,128)}, u32[]{:S(2)}, u32[]{:S(2)}) collective-permute-start(f32[256,512]{1,0:T(8,128)S(1)} %get-tuple-element.20), channel_id=1, source_target_pairs={{32,6},{33,7},{34,32},{35,33},{36,34},{37,35},{38,36},{39,37},{40,... | collective-permute-start | bytes 1572872 | tf_op jit(solution)/shard_map/ppermute | solution.py:104
  32.5 59.6 %collective-permute-start.8 = (f32[256,512]{1,0:T(8,128)S(1)}, f32[256,512]{1,0:T(8,128)S(1)}, u32[]{:S(2)}, u32[]{:S(2)}) collective-permute-start(f32[256,512]{1,0:T(8,128)S(1)} %get-tuple-element.20), channel_id=1, source_target_pairs={{0,1},{1,0},{2,3},{3,2},{4,5},{5,4},{6,7},{7,6},{8,9},{9,8},{10,11... | collective-permute-start | bytes 1572872 | tf_op jit(solution)/shard_map/ppermute | solution.py:104
  37.9 18.0 %collective-permute-start.2 = (f32[256,512]{1,0:T(8,128)S(1)}, f32[256,512]{1,0:T(8,128)S(1)}, u32[]{:S(2)}, u32[]{:S(2)}) collective-permute-start(f32[256,512]{1,0:T(8,128)S(1)} %get-tuple-element.20), channel_id=1, source_target_pairs={{0,2},{1,3},{2,4},{3,5},{4,6},{5,7},{6,32},{7,33},{8,10},{9,11},{1... | collective-permute-start | bytes 1572872 | tf_op jit(solution)/shard_map/ppermute | solution.py:104
  39.8 22.1 %collective-permute-start.14 = (f32[256,512]{1,0:T(8,128)S(1)}, f32[256,512]{1,0:T(8,128)S(1)}, u32[]{:S(2)}, u32[]{:S(2)}) collective-permute-start(f32[256,512]{1,0:T(8,128)S(1)} %get-tuple-element.23), channel_id=1, source_target_pairs={{6,14},{7,15},{8,0},{9,1},{14,22},{15,23},{16,8},{17,9},{22,30},{2... | collective-permute-start | bytes 1572872 | tf_op jit(solution)/shard_map/ppermute | solution.py:104
  55.9 32.3 %collective-permute-start.19 = (f32[256,512]{1,0:T(8,128)S(1)}, f32[256,512]{1,0:T(8,128)S(1)}, u32[]{:S(2)}, u32[]{:S(2)}) collective-permute-start(f32[256,512]{1,0:T(8,128)S(1)} %get-tuple-element.23), channel_id=1, source_target_pairs={{32,6},{33,7},{34,32},{35,33},{36,34},{37,35},{38,36},{39,37},{40,... | collective-permute-start | bytes 1572872 | tf_op jit(solution)/shard_map/ppermute | solution.py:104
  61.9 17.5 %collective-permute-start.13 = (f32[256,512]{1,0:T(8,128)S(1)}, f32[256,512]{1,0:T(8,128)S(1)}, u32[]{:S(2)}, u32[]{:S(2)}) collective-permute-start(f32[256,512]{1,0:T(8,128)S(1)} %get-tuple-element.23), channel_id=1, source_target_pairs={{0,2},{1,3},{2,4},{3,5},{4,6},{5,7},{6,32},{7,33},{8,10},{9,11},{1... | collective-permute-start | bytes 1572872 | tf_op jit(solution)/shard_map/ppermute | solution.py:104
  63.8 17.5 %collective-permute-start.15 = (f32[256,512]{1,0:T(8,128)S(1)}, f32[256,512]{1,0:T(8,128)S(1)}, u32[]{:S(2)}, u32[]{:S(2)}) collective-permute-start(f32[256,512]{1,0:T(8,128)S(1)} %collective-permute-done.14), channel_id=1, source_target_pairs={{0,1},{1,0},{2,3},{3,2},{4,5},{5,4},{6,7},{7,6},{8,9},{9,8},{10,11... | collective-permute-start | bytes 1572872 | tf_op jit(solution)/shard_map/ppermute | solution.py:104
  68.9 62.5 %collective-permute-start.17 = (f32[256,512]{1,0:T(8,128)S(1)}, f32[256,512]{1,0:T(8,128)S(1)}, u32[]{:S(2)}, u32[]{:S(2)}) collective-permute-start(f32[256,512]{1,0:T(8,128)S(1)} %get-tuple-element.23), channel_id=1, source_target_pairs={{0,1},{1,0},{2,3},{3,2},{4,5},{5,4},{6,7},{7,6},{8,9},{9,8},{10,11... | collective-permute-start | bytes 1572872 | tf_op jit(solution)/shard_map/ppermute | solution.py:104
  79.3 37.4 %collective-permute-start.11 = (f32[256,512]{1,0:T(8,128)S(1)}, f32[256,512]{1,0:T(8,128)S(1)}, u32[]{:S(2)}, u32[]{:S(2)}) collective-permute-start(f32[256,512]{1,0:T(8,128)S(1)} %multiply_add_fusion.15), channel_id=1, source_target_pairs={{0,100},{1,101},{2,102},{3,103},{4,0},{5,1},{6,2},{7,3},{8,108},{9... | collective-permute-start | bytes 1572872 | tf_op jit(solution)/shard_map/ppermute | solution.py:104
  81.3 30.3 %collective-permute-start.5 = (f32[256,512]{1,0:T(8,128)S(1)}, f32[256,512]{1,0:T(8,128)S(1)}, u32[]{:S(2)}, u32[]{:S(2)}) collective-permute-start(f32[256,512]{1,0:T(8,128)S(1)} %multiply_add_fusion.17), channel_id=1, source_target_pairs={{0,4},{1,5},{2,6},{3,7},{4,32},{5,33},{6,34},{7,35},{8,12},{9,13},... | collective-permute-start | bytes 1572872 | tf_op jit(solution)/shard_map/ppermute | solution.py:104
  88.2 43.2 %collective-permute-start.16 = (f32[256,512]{1,0:T(8,128)S(1)}, f32[256,512]{1,0:T(8,128)S(1)}, u32[]{:S(2)}, u32[]{:S(2)}) collective-permute-start(f32[256,512]{1,0:T(8,128)S(1)} %multiply_add_fusion.13), channel_id=1, source_target_pairs={{0,4},{1,5},{2,6},{3,7},{4,32},{5,33},{6,34},{7,35},{8,12},{9,13},... | collective-permute-start | bytes 1572872 | tf_op jit(solution)/shard_map/ppermute | solution.py:104
  92.1 46.7 %collective-permute-start.20 = (f32[256,512]{1,0:T(8,128)S(1)}, f32[256,512]{1,0:T(8,128)S(1)}, u32[]{:S(2)}, u32[]{:S(2)}) collective-permute-start(f32[256,512]{1,0:T(8,128)S(1)} %multiply_add_fusion.11), channel_id=1, source_target_pairs={{0,100},{1,101},{2,102},{3,103},{4,0},{5,1},{6,2},{7,3},{8,108},{9... | collective-permute-start | bytes 1572872 | tf_op jit(solution)/shard_map/ppermute | solution.py:104
  113.0 32.2 %collective-permute-start.9 = (f32[256,512]{1,0:T(8,128)S(1)}, f32[256,512]{1,0:T(8,128)S(1)}, u32[]{:S(2)}, u32[]{:S(2)}) collective-permute-start(f32[256,512]{1,0:T(8,128)S(1)} %multiply_add_fusion.16), channel_id=1, source_target_pairs={{0,2},{1,3},{2,4},{3,5},{4,6},{5,7},{6,32},{7,33},{8,10},{9,11},{1... | collective-permute-start | bytes 1572872 | tf_op jit(solution)/shard_map/ppermute | solution.py:104
  118.2 24.2 %collective-permute-start.12 = (f32[256,512]{1,0:T(8,128)S(1)}, f32[256,512]{1,0:T(8,128)S(1)}, u32[]{:S(2)}, u32[]{:S(2)}) collective-permute-start(f32[256,512]{1,0:T(8,128)S(1)} %multiply_add_fusion.14), channel_id=1, source_target_pairs={{0,102},{1,103},{2,0},{3,1},{4,2},{5,3},{6,4},{7,5},{8,110},{9,111... | collective-permute-start | bytes 1572872 | tf_op jit(solution)/shard_map/ppermute | solution.py:104
  132.9 22.3 %collective-permute-start.18 = (f32[256,512]{1,0:T(8,128)S(1)}, f32[256,512]{1,0:T(8,128)S(1)}, u32[]{:S(2)}, u32[]{:S(2)}) collective-permute-start(f32[256,512]{1,0:T(8,128)S(1)} %multiply_add_fusion.12), channel_id=1, source_target_pairs={{0,2},{1,3},{2,4},{3,5},{4,6},{5,7},{6,32},{7,33},{8,10},{9,11},{1... | collective-permute-start | bytes 1572872 | tf_op jit(solution)/shard_map/ppermute | solution.py:104
  156.8 52.9 %collective-permute-start.35 = (f32[256,512]{1,0:T(8,128)S(1)}, f32[256,512]{1,0:T(8,128)S(1)}, u32[]{:S(2)}, u32[]{:S(2)}) collective-permute-start(f32[256,512]{1,0:T(8,128)S(1)} %fusion.10), channel_id=1, source_target_pairs={{32,6},{33,7},{34,32},{35,33},{36,34},{37,35},{38,36},{39,37},{40,... | collective-permute-start | bytes 1572872 | tf_op jit(solution)/shard_map/ppermute | solution.py:104
  162.1 41.4 %collective-permute-start.30 = (f32[256,512]{1,0:T(8,128)S(1)}, f32[256,512]{1,0:T(8,128)S(1)}, u32[]{:S(2)}, u32[]{:S(2)}) collective-permute-start(f32[256,512]{1,0:T(8,128)S(1)} %fusion.10), channel_id=1, source_target_pairs={{0,2},{1,3},{2,4},{3,5},{4,6},{5,7},{6,32},{7,33},{8,10},{9,11},{1... | collective-permute-start | bytes 1572872 | tf_op jit(solution)/shard_map/ppermute | solution.py:104
  166.9 24.8 %collective-permute-start.22 = (f32[256,512]{1,0:T(8,128)S(1)}, f32[256,512]{1,0:T(8,128)S(1)}, u32[]{:S(2)}, u32[]{:S(2)}) collective-permute-start(f32[256,512]{1,0:T(8,128)S(1)} %fusion.12), channel_id=1, source_target_pairs={{0,2},{1,3},{2,4},{3,5},{4,6},{5,7},{6,32},{7,33},{8,10},{9,11},{1... | collective-permute-start | bytes 1572872 | tf_op jit(solution)/shard_map/ppermute | solution.py:104
  173.4 20.7 %collective-permute-start.24 = (f32[256,512]{1,0:T(8,128)S(1)}, f32[256,512]{1,0:T(8,128)S(1)}, u32[]{:S(2)}, u32[]{:S(2)}) collective-permute-start(f32[256,512]{1,0:T(8,128)S(1)} %multiply_add_fusion.9), channel_id=1, source_target_pairs={{6,14},{7,15},{8,0},{9,1},{14,22},{15,23},{16,8},{17,9},{22,30},{2... | collective-permute-start | bytes 1572872 | tf_op jit(solution)/shard_map/ppermute | solution.py:104
  176.8 20.0 %collective-permute-start.27 = (f32[256,512]{1,0:T(8,128)S(1)}, f32[256,512]{1,0:T(8,128)S(1)}, u32[]{:S(2)}, u32[]{:S(2)}) collective-permute-start(f32[256,512]{1,0:T(8,128)S(1)} %fusion.12), channel_id=1, source_target_pairs={{32,6},{33,7},{34,32},{35,33},{36,34},{37,35},{38,36},{39,37},{40,... | collective-permute-start | bytes 1572872 | tf_op jit(solution)/shard_map/ppermute | solution.py:104
  194.8 38.6 %collective-permute-start.25 = (f32[256,512]{1,0:T(8,128)S(1)}, f32[256,512]{1,0:T(8,128)S(1)}, u32[]{:S(2)}, u32[]{:S(2)}) collective-permute-start(f32[256,512]{1,0:T(8,128)S(1)} %multiply_add_fusion.8), channel_id=1, source_target_pairs={{0,4},{1,5},{2,6},{3,7},{4,32},{5,33},{6,34},{7,35},{8,12},{9,13},... | collective-permute-start | bytes 1572872 | tf_op jit(solution)/shard_map/ppermute | solution.py:104
  197.5 39.3 %collective-permute-start.28 = (f32[256,512]{1,0:T(8,128)S(1)}, f32[256,512]{1,0:T(8,128)S(1)}, u32[]{:S(2)}, u32[]{:S(2)}) collective-permute-start(f32[256,512]{1,0:T(8,128)S(1)} %multiply_add_fusion.6), channel_id=1, source_target_pairs={{0,100},{1,101},{2,102},{3,103},{4,0},{5,1},{6,2},{7,3},{8,108},{9... | collective-permute-start | bytes 1572872 | tf_op jit(solution)/shard_map/ppermute | solution.py:104
  207.8 36.9 %collective-permute-start.33 = (f32[256,512]{1,0:T(8,128)S(1)}, f32[256,512]{1,0:T(8,128)S(1)}, u32[]{:S(2)}, u32[]{:S(2)}) collective-permute-start(f32[256,512]{1,0:T(8,128)S(1)} %multiply_add_fusion.3), channel_id=1, source_target_pairs={{0,4},{1,5},{2,6},{3,7},{4,32},{5,33},{6,34},{7,35},{8,12},{9,13},... | collective-permute-start | bytes 1572872 | tf_op jit(solution)/shard_map/ppermute | solution.py:104
  210.5 37.6 %collective-permute-start.36 = (f32[256,512]{1,0:T(8,128)S(1)}, f32[256,512]{1,0:T(8,128)S(1)}, u32[]{:S(2)}, u32[]{:S(2)}) collective-permute-start(f32[256,512]{1,0:T(8,128)S(1)} %multiply_add_fusion.1), channel_id=1, source_target_pairs={{0,100},{1,101},{2,102},{3,103},{4,0},{5,1},{6,2},{7,3},{8,108},{9... | collective-permute-start | bytes 1572872 | tf_op jit(solution)/shard_map/ppermute | solution.py:104
  234.9 26.3 %collective-permute-start.26 = (f32[256,512]{1,0:T(8,128)S(1)}, f32[256,512]{1,0:T(8,128)S(1)}, u32[]{:S(2)}, u32[]{:S(2)}) collective-permute-start(f32[256,512]{1,0:T(8,128)S(1)} %multiply_add_fusion.7), channel_id=1, source_target_pairs={{0,2},{1,3},{2,4},{3,5},{4,6},{5,7},{6,32},{7,33},{8,10},{9,11},{1... | collective-permute-start | bytes 1572872 | tf_op jit(solution)/shard_map/ppermute | solution.py:104
  238.3 23.0 %collective-permute-start.29 = (f32[256,512]{1,0:T(8,128)S(1)}, f32[256,512]{1,0:T(8,128)S(1)}, u32[]{:S(2)}, u32[]{:S(2)}) collective-permute-start(f32[256,512]{1,0:T(8,128)S(1)} %multiply_add_fusion.5), channel_id=1, source_target_pairs={{0,102},{1,103},{2,0},{3,1},{4,2},{5,3},{6,4},{7,5},{8,110},{9,111... | collective-permute-start | bytes 1572872 | tf_op jit(solution)/shard_map/ppermute | solution.py:104
  246.2 24.5 %collective-permute-start.34 = (f32[256,512]{1,0:T(8,128)S(1)}, f32[256,512]{1,0:T(8,128)S(1)}, u32[]{:S(2)}, u32[]{:S(2)}) collective-permute-start(f32[256,512]{1,0:T(8,128)S(1)} %multiply_add_fusion.2), channel_id=1, source_target_pairs={{0,2},{1,3},{2,4},{3,5},{4,6},{5,7},{6,32},{7,33},{8,10},{9,11},{1... | collective-permute-start | bytes 1572872 | tf_op jit(solution)/shard_map/ppermute | solution.py:104
  249.5 21.1 %collective-permute-start.37 = (f32[256,512]{1,0:T(8,128)S(1)}, f32[256,512]{1,0:T(8,128)S(1)}, u32[]{:S(2)}, u32[]{:S(2)}) collective-permute-start(f32[256,512]{1,0:T(8,128)S(1)} %multiply_add_fusion), channel_id=1, source_target_pairs={{0,102},{1,103},{2,0},{3,1},{4,2},{5,3},{6,4},{7,5},{8,110},{9,111... | collective-permute-start | bytes 1572872 | tf_op jit(solution)/shard_map/ppermute | solution.py:104
  (14 other events, 204.9 us)

commit v3 on v2

--- a/solution.py
+++ b/solution.py
@@ -209,29 +209,26 @@
     middles = []
     done = None
     for k, (f, x) in enumerate(zip(firsts, crossed)):
-        up, down = f[1], f[-1]
         if done is not None:
-            up = after(up, done)
+            x = after(x, done)
         if raw:
-            up = first[AHEAD] * up + first[PLUS] * x + first[PLUS_MATE] * others[k]
-            down = first[BEHIND] * after(down, up) + first[MINUS] * x + first[MINUS_MATE] * others[k]
+            up = first[AHEAD] * f[1] + first[PLUS] * x + first[PLUS_MATE] * others[k]
+            down = first[BEHIND] * f[-1] + first[MINUS] * x + first[MINUS_MATE] * others[k]
         else:
-            up = first[AHEAD] * up + at_bottom * x
-            down = first[BEHIND] * after(down, up) + at_top * x
+            up = first[AHEAD] * f[1] + at_bottom * x
+            down = first[BEHIND] * f[-1] + at_top * x
         middles.append({1: send(up, MIDDLE[1]), -1: send(down, MIDDLE[-1])})
-        done = down
+        done = up
+    near = [
+        {1: rest[UP] * p + rest[UP_MATE] * m, -1: rest[DOWN] * p + rest[DOWN_MATE] * m}
+        for p, m in zip([after(p, done) for p in pieces], mates)
+    ]
+    near = lax.optimization_barrier(near)
     gathered = []
-    done = None
-    for p, m, mid in zip(pieces, mates, middles):
-        up, down = mid[1], mid[-1]
-        if done is not None:
-            up = after(up, done)
-        up = up + rest[UP] * p + rest[UP_MATE] * m
-        down = after(down, up) + rest[DOWN] * p + rest[DOWN_MATE] * m
-        plus = send(up, LAST[1])
-        minus = send(down, LAST[-1])
+    for m, mid, add in zip(mates, middles, near):
+        plus = send(mid[1] + add[1], LAST[1])
+        minus = send(mid[-1] + add[-1], LAST[-1])
         gathered.append(plus + minus + rest[MATE] * m)
-        done = down
     return gathered
 
 

time: 275 us -> 296 us (1.076)
  the two profiles are of different devices: /device:TPU:18 before, /device:TPU:10 now
where the time goes in v3:
time: 296 us; the launch traced here: 294 us
  starting transfers between devices  132 us (45%)
  waiting for transfers between devices  105 us (35%)
  other arithmetic  29.9 us (10%)
  matrix products  22.9 us (8%)
  local copies, waits for them, and re-layouts  3.01 us (1%)
    ppermute x38, starting transfers between devices, send(): return lax.ppermute(x, AXES, pairs)  132 us
    ppermute x38, waiting for transfers between devices, send(): return lax.ppermute(x, AXES, pairs)  105 us
    dot_general x18, matrix products, mm(): return jnp.dot(a, b, precision=HIGH, preferred_element_type=jnp.float32)  17.3 us
    add x4, other arithmetic, sweep_pieces(): rest[UP] * p + rest[UP_MATE] * m  11.1 us
    add x2, other arithmetic, sweep_pieces(): first[BEHIND] * f[-1] + first[MINUS] * x + first[MINUS_MATE] * others[k]  10.1 us
  transfers between devices with their start and end apart: 38, of which 15 were waited for; matrix products, arithmetic and copies ran while one was open for 17% of the time, Pallas kernels for 0%

profile of v3, /device:TPU:10, one launch (start us, length us, event | category | flops | bytes accessed | tf_op | source)
XLA Modules:
  0.0 294.2 jit_solution(5826731323241195910)
XLA Ops:
  0.8 12.4 %collective-permute-start = (s32[8]{0:T(128)S(1)}, s32[8]{0:T(128)S(1)}, u32[]{:S(2)}, u32[]{:S(2)}) collective-permute-start(s32[8]{0:T(128)S(1)} %pad_add_fusion), channel_id=1, source_target_pairs={{0,98},{1,99},{2,100},{3,101},{4,102},{5,103},{6,0},{7,1},{8,106},... | collective-permute-start | bytes 104 | tf_op jit(solution)/shard_map/ppermute | solution.py:104
  18.9 6.9 %collective-permute-start.14 = (f32[256,512]{1,0:T(8,128)S(1)}, f32[256,512]{1,0:T(8,128)}, u32[]{:S(2)}, u32[]{:S(2)}) collective-permute-start(f32[256,512]{1,0:T(8,128)S(1)} %get-tuple-element.25), channel_id=1, source_target_pairs={{32,6},{33,7},{34,32},{35,33},{36,34},{37,35},{38,36},{39,37},{40,... | collective-permute-start | bytes 1572872 | tf_op jit(solution)/shard_map/ppermute | solution.py:104
  29.3 3.1 %fusion.1 = f32[8,512,64]{1,2,0:T(8,128)S(1)} fusion(f32[8,64,384]{2,1,0:T(8,128)} %param.12, s32[8,384]{1,0:T(8,128)S(1)} %broadcast_add_fusion), kind=kOutput, calls=%fused_computation.2 | convolution fusion | flops 605552640 | bytes 1847296 | tf_op jit(solution)/shard_map/rxk,rkn->rxn/dot_general | solution.py:117
  34.3 3.9 %collective-permute-start.7 = (s32[8]{0:T(128)S(1)}, s32[8]{0:T(128)S(1)}, u32[]{:S(2)}, u32[]{:S(2)}) collective-permute-start(s32[8]{0:T(128)S(1)} %pad_add_fusion), channel_id=1, source_target_pairs={{0,2},{1,3},{2,4},{3,5},{4,6},{5,7},{6,8},{7,9},{8,10},{9,11},{10,... | collective-permute-start | bytes 104 | tf_op jit(solution)/shard_map/ppermute | solution.py:104
  42.4 9.4 %collective-permute-start.19 = (f32[256,512]{1,0:T(8,128)S(1)}, f32[256,512]{1,0:T(8,128)}, u32[]{:S(2)}, u32[]{:S(2)}) collective-permute-start(f32[256,512]{1,0:T(8,128)S(1)} %get-tuple-element.26), channel_id=1, source_target_pairs={{32,6},{33,7},{34,32},{35,33},{36,34},{37,35},{38,36},{39,37},{40,... | collective-permute-start | bytes 1572872 | tf_op jit(solution)/shard_map/ppermute | solution.py:104
  70.5 5.1 %multiply_add_fusion.11 = (f32[256,512]{1,0:T(8,128)S(1)}, f32[256,512]{1,0:T(8,128)S(1)}) fusion(f32[256,512]{1,0:T(8,128)S(1)} %collective-permute-done.4, f32[256,512]{1,0:T(8,128)S(1)} %collective-permute-done.3, f32[256,512]{1,0:T(8,128)} %collective-permute-done.14, f32[]{:T(128)} %bitcast.30, f32[]{:T(128)} %bitcast.29, f32[]{:T(128)} %bitcast.28, ...), kind=kLoop, calls=%fused_computation.64 | loop fusion | flops 1310720 | bytes 3145752 | tf_op jit(solution)/shard_map/add | solution.py:216
  75.6 3.5 %collective-permute-done.8 = f32[256,512]{1,0:T(8,128)S(1)} collective-permute-done((f32[256,512]{1,0:T(8,128)S(1)}, f32[256,512]{1,0:T(8,128)S(1)}, u32[]{:S(2)}, u32[]{:S(2)}) %collective-permute-start.8) | collective-permute-done | bytes 524320 | tf_op jit(solution)/shard_map/ppermute | solution.py:104
  79.1 5.1 %multiply_add_fusion.10 = (f32[256,512]{1,0:T(8,128)S(1)}, f32[256,512]{1,0:T(8,128)S(1)}) fusion(f32[256,512]{1,0:T(8,128)S(1)} %collective-permute-done.10, f32[256,512]{1,0:T(8,128)} %collective-permute-done.9, f32[256,512]{1,0:T(8,128)} %collective-permute-done.19, f32[]{:T(128)} %bitcast.30, f32[]{:T(128)} %bitcast.29, f32[]{:T(128)} %bitcast.28, ...), kind=kLoop, calls=%fused_computation.59 | loop fusion | flops 1310720 | bytes 3145752 | tf_op jit(solution)/shard_map/add | solution.py:216
  88.0 6.0 %collective-permute-start.15 = (f32[256,512]{1,0:T(8,128)S(1)}, f32[256,512]{1,0:T(8,128)S(1)}, u32[]{:S(2)}, u32[]{:S(2)}) collective-permute-start(f32[256,512]{1,0:T(8,128)S(1)} %get-tuple-element.45), channel_id=1, source_target_pairs={{0,100},{1,101},{2,102},{3,103},{4,0},{5,1},{6,2},{7,3},{8,108},{9... | collective-permute-start | bytes 1572872 | tf_op jit(solution)/shard_map/ppermute | solution.py:104
  94.0 2.8 multiply_add_fusion.12
  96.8 2.8 multiply_add_fusion.14
  99.6 4.8 %collective-permute-start.20 = (f32[256,512]{1,0:T(8,128)S(1)}, f32[256,512]{1,0:T(8,128)S(1)}, u32[]{:S(2)}, u32[]{:S(2)}) collective-permute-start(f32[256,512]{1,0:T(8,128)S(1)} %get-tuple-element.43), channel_id=1, source_target_pairs={{0,100},{1,101},{2,102},{3,103},{4,0},{5,1},{6,2},{7,3},{8,108},{9... | collective-permute-start | bytes 1572872 | tf_op jit(solution)/shard_map/ppermute | solution.py:104
  104.4 21.7 %collective-permute-done.15 = f32[256,512]{1,0:T(8,128)S(1)} collective-permute-done((f32[256,512]{1,0:T(8,128)S(1)}, f32[256,512]{1,0:T(8,128)S(1)}, u32[]{:S(2)}, u32[]{:S(2)}) %collective-permute-start.15) | collective-permute-done | bytes 524320 | tf_op jit(solution)/shard_map/ppermute | solution.py:104
  128.4 3.9 %collective-permute-start.13 = (f32[256,512]{1,0:T(8,128)S(1)}, f32[256,512]{1,0:T(8,128)S(1)}, u32[]{:S(2)}, u32[]{:S(2)}) collective-permute-start(f32[256,512]{1,0:T(8,128)S(1)} %add.201), channel_id=1, source_target_pairs={{0,2},{1,3},{2,4},{3,5},{4,6},{5,7},{6,32},{7,33},{8,10},{9,11},{1... | collective-permute-start | bytes 1572872 | tf_op jit(solution)/shard_map/ppermute | solution.py:104
  133.6 4.4 %collective-permute-done.20 = f32[256,512]{1,0:T(8,128)S(1)} collective-permute-done((f32[256,512]{1,0:T(8,128)S(1)}, f32[256,512]{1,0:T(8,128)S(1)}, u32[]{:S(2)}, u32[]{:S(2)}) %collective-permute-start.20) | collective-permute-done | bytes 524320 | tf_op jit(solution)/shard_map/ppermute | solution.py:104
  138.1 4.6 %collective-permute-start.21 = (f32[256,512]{1,0:T(8,128)S(1)}, f32[256,512]{1,0:T(8,128)S(1)}, u32[]{:S(2)}, u32[]{:S(2)}) collective-permute-start(f32[256,512]{1,0:T(8,128)S(1)} %add.210), channel_id=1, source_target_pairs={{0,102},{1,103},{2,0},{3,1},{4,2},{5,3},{6,4},{7,5},{8,110},{9,111... | collective-permute-start | bytes 1572872 | tf_op jit(solution)/shard_map/ppermute | solution.py:104
  144.8 4.7 %collective-permute-done.16 = f32[256,512]{1,0:T(8,128)S(1)} collective-permute-done((f32[256,512]{1,0:T(8,128)S(1)}, f32[256,512]{1,0:T(8,128)S(1)}, u32[]{:S(2)}, u32[]{:S(2)}) %collective-permute-start.16) | collective-permute-done | bytes 524320 | tf_op jit(solution)/shard_map/ppermute | solution.py:104
  151.5 8.8 %collective-permute-done.21 = f32[256,512]{1,0:T(8,128)S(1)} collective-permute-done((f32[256,512]{1,0:T(8,128)S(1)}, f32[256,512]{1,0:T(8,128)S(1)}, u32[]{:S(2)}, u32[]{:S(2)}) %collective-permute-start.21) | collective-permute-done | bytes 524320 | tf_op jit(solution)/shard_map/ppermute | solution.py:104
  166.0 6.1 %collective-permute-start.30 = (f32[256,512]{1,0:T(8,128)S(1)}, f32[256,512]{1,0:T(8,128)S(1)}, u32[]{:S(2)}, u32[]{:S(2)}) collective-permute-start(f32[256,512]{1,0:T(8,128)S(1)} %fusion.12), channel_id=1, source_target_pairs={{32,6},{33,7},{34,32},{35,33},{36,34},{37,35},{38,36},{39,37},{40,... | collective-permute-start | bytes 1572872 | tf_op jit(solution)/shard_map/ppermute | solution.py:104
  177.4 6.1 %collective-permute-start.35 = (f32[256,512]{1,0:T(8,128)S(1)}, f32[256,512]{1,0:T(8,128)S(1)}, u32[]{:S(2)}, u32[]{:S(2)}) collective-permute-start(f32[256,512]{1,0:T(8,128)S(1)} %fusion.10), channel_id=1, source_target_pairs={{32,6},{33,7},{34,32},{35,33},{36,34},{37,35},{38,36},{39,37},{40,... | collective-permute-start | bytes 1572872 | tf_op jit(solution)/shard_map/ppermute | solution.py:104
  184.8 3.5 %collective-permute-start.24 = (f32[256,512]{1,0:T(8,128)S(1)}, f32[256,512]{1,0:T(8,128)S(1)}, u32[]{:S(2)}, u32[]{:S(2)}) collective-permute-start(f32[256,512]{1,0:T(8,128)S(1)} %multiply_add_fusion.9), channel_id=1, source_target_pairs={{6,14},{7,15},{8,0},{9,1},{14,22},{15,23},{16,8},{17,9},{22,30},{2... | collective-permute-start | bytes 1572872 | tf_op jit(solution)/shard_map/ppermute | solution.py:104
  192.6 8.9 %collective-permute-done.24 = f32[256,512]{1,0:T(8,128)S(1)} collective-permute-done((f32[256,512]{1,0:T(8,128)S(1)}, f32[256,512]{1,0:T(8,128)S(1)}, u32[]{:S(2)}, u32[]{:S(2)}) %collective-permute-start.24) | collective-permute-done | bytes 524320 | tf_op jit(solution)/shard_map/ppermute | solution.py:104
  202.8 8.8 %collective-permute-done.28 = f32[256,512]{1,0:T(8,128)S(1)} collective-permute-done((f32[256,512]{1,0:T(8,128)S(1)}, f32[256,512]{1,0:T(8,128)S(1)}, u32[]{:S(2)}, u32[]{:S(2)}) %collective-permute-start.28) | collective-permute-done | bytes 524320 | tf_op jit(solution)/shard_map/ppermute | solution.py:104
  215.0 3.4 %collective-permute-start.25 = (f32[256,512]{1,0:T(8,128)S(1)}, f32[256,512]{1,0:T(8,128)S(1)}, u32[]{:S(2)}, u32[]{:S(2)}) collective-permute-start(f32[256,512]{1,0:T(8,128)S(1)} %get-tuple-element.56), channel_id=1, source_target_pairs={{0,4},{1,5},{2,6},{3,7},{4,32},{5,33},{6,34},{7,35},{8,12},{9,13},... | collective-permute-start | bytes 1572872 | tf_op jit(solution)/shard_map/ppermute | solution.py:104
  218.4 4.5 %collective-permute-start.31 = (f32[256,512]{1,0:T(8,128)S(1)}, f32[256,512]{1,0:T(8,128)S(1)}, u32[]{:S(2)}, u32[]{:S(2)}) collective-permute-start(f32[256,512]{1,0:T(8,128)S(1)} %get-tuple-element.55), channel_id=1, source_target_pairs={{0,100},{1,101},{2,102},{3,103},{4,0},{5,1},{6,2},{7,3},{8,108},{9... | collective-permute-start | bytes 1572872 | tf_op jit(solution)/shard_map/ppermute | solution.py:104
  225.7 2.8 multiply_add_fusion.4
  228.5 4.8 %collective-permute-start.36 = (f32[256,512]{1,0:T(8,128)S(1)}, f32[256,512]{1,0:T(8,128)S(1)}, u32[]{:S(2)}, u32[]{:S(2)}) collective-permute-start(f32[256,512]{1,0:T(8,128)S(1)} %get-tuple-element.53), channel_id=1, source_target_pairs={{0,100},{1,101},{2,102},{3,103},{4,0},{5,1},{6,2},{7,3},{8,108},{9... | collective-permute-start | bytes 1572872 | tf_op jit(solution)/shard_map/ppermute | solution.py:104
  233.3 21.6 %collective-permute-done.31 = f32[256,512]{1,0:T(8,128)S(1)} collective-permute-done((f32[256,512]{1,0:T(8,128)S(1)}, f32[256,512]{1,0:T(8,128)S(1)}, u32[]{:S(2)}, u32[]{:S(2)}) %collective-permute-start.31) | collective-permute-done | bytes 524320 | tf_op jit(solution)/shard_map/ppermute | solution.py:104
  257.0 5.9 %collective-permute-done.25 = f32[256,512]{1,0:T(8,128)S(1)} collective-permute-done((f32[256,512]{1,0:T(8,128)S(1)}, f32[256,512]{1,0:T(8,128)S(1)}, u32[]{:S(2)}, u32[]{:S(2)}) %collective-permute-start.25) | collective-permute-done | bytes 524320 | tf_op jit(solution)/shard_map/ppermute | solution.py:104
  267.4 4.8 %collective-permute-start.37 = (f32[256,512]{1,0:T(8,128)S(1)}, f32[256,512]{1,0:T(8,128)S(1)}, u32[]{:S(2)}, u32[]{:S(2)}) collective-permute-start(f32[256,512]{1,0:T(8,128)S(1)} %add.234), channel_id=1, source_target_pairs={{0,102},{1,103},{2,0},{3,1},{4,2},{5,3},{6,4},{7,5},{8,110},{9,111... | collective-permute-start | bytes 1572872 | tf_op jit(solution)/shard_map/ppermute | solution.py:104
  274.3 4.5 %collective-permute-done.32 = f32[256,512]{1,0:T(8,128)S(1)} collective-permute-done((f32[256,512]{1,0:T(8,128)S(1)}, f32[256,512]{1,0:T(8,128)S(1)}, u32[]{:S(2)}, u32[]{:S(2)}) %collective-permute-start.32) | collective-permute-done | bytes 524320 | tf_op jit(solution)/shard_map/ppermute | solution.py:104
  282.7 6.3 %collective-permute-done.37 = f32[256,512]{1,0:T(8,128)S(1)} collective-permute-done((f32[256,512]{1,0:T(8,128)S(1)}, f32[256,512]{1,0:T(8,128)S(1)}, u32[]{:S(2)}, u32[]{:S(2)}) %collective-permute-start.37) | collective-permute-done | bytes 524320 | tf_op jit(solution)/shard_map/ppermute | solution.py:104
  (125 shorter events, 86.2 us)
Async XLA Ops:
  0.8 31.5 %collective-permute-start = (s32[8]{0:T(128)S(1)}, s32[8]{0:T(128)S(1)}, u32[]{:S(2)}, u32[]{:S(2)}) collective-permute-start(s32[8]{0:T(128)S(1)} %pad_add_fusion), channel_id=1, source_target_pairs={{0,98},{1,99},{2,100},{3,101},{4,102},{5,103},{6,0},{7,1},{8,106},... | collective-permute-start | bytes 104 | tf_op jit(solution)/shard_map/ppermute | solution.py:104
  13.2 21.0 %collective-permute-start.1 = (s32[8]{0:T(128)S(1)}, s32[8]{0:T(128)S(1)}, u32[]{:S(2)}, u32[]{:S(2)}) collective-permute-start(s32[8]{0:T(128)S(1)} %pad_add_fusion), channel_id=1, source_target_pairs={{0,6},{1,7},{2,32},{3,33},{4,34},{5,35},{6,36},{7,37},{8,14},{9,15... | collective-permute-start | bytes 104 | tf_op jit(solution)/shard_map/ppermute | solution.py:104
  16.5 41.3 %collective-permute-start.3 = (f32[256,512]{1,0:T(8,128)S(1)}, f32[256,512]{1,0:T(8,128)S(1)}, u32[]{:S(2)}, u32[]{:S(2)}) collective-permute-start(f32[256,512]{1,0:T(8,128)S(1)} %get-tuple-element.25), channel_id=1, source_target_pairs={{6,14},{7,15},{8,0},{9,1},{14,22},{15,23},{16,8},{17,9},{22,30},{2... | collective-permute-start | bytes 1572872 | tf_op jit(solution)/shard_map/ppermute | solution.py:104
  18.9 41.8 %collective-permute-start.14 = (f32[256,512]{1,0:T(8,128)S(1)}, f32[256,512]{1,0:T(8,128)}, u32[]{:S(2)}, u32[]{:S(2)}) collective-permute-start(f32[256,512]{1,0:T(8,128)S(1)} %get-tuple-element.25), channel_id=1, source_target_pairs={{32,6},{33,7},{34,32},{35,33},{36,34},{37,35},{38,36},{39,37},{40,... | collective-permute-start | bytes 1572872 | tf_op jit(solution)/shard_map/ppermute | solution.py:104
  25.8 40.3 %collective-permute-start.2 = (f32[256,512]{1,0:T(8,128)S(1)}, f32[256,512]{1,0:T(8,128)}, u32[]{:S(2)}, u32[]{:S(2)}) collective-permute-start(f32[256,512]{1,0:T(8,128)S(1)} %get-tuple-element.25), channel_id=1, source_target_pairs={{0,2},{1,3},{2,4},{3,5},{4,6},{5,7},{6,32},{7,33},{8,10},{9,11},{1... | collective-permute-start | bytes 1572872 | tf_op jit(solution)/shard_map/ppermute | solution.py:104
  39.2 23.5 %collective-permute-start.9 = (f32[256,512]{1,0:T(8,128)S(1)}, f32[256,512]{1,0:T(8,128)}, u32[]{:S(2)}, u32[]{:S(2)}) collective-permute-start(f32[256,512]{1,0:T(8,128)S(1)} %get-tuple-element.26), channel_id=1, source_target_pairs={{6,14},{7,15},{8,0},{9,1},{14,22},{15,23},{16,8},{17,9},{22,30},{2... | collective-permute-start | bytes 1572872 | tf_op jit(solution)/shard_map/ppermute | solution.py:104
  42.4 33.1 %collective-permute-start.19 = (f32[256,512]{1,0:T(8,128)S(1)}, f32[256,512]{1,0:T(8,128)}, u32[]{:S(2)}, u32[]{:S(2)}) collective-permute-start(f32[256,512]{1,0:T(8,128)S(1)} %get-tuple-element.26), channel_id=1, source_target_pairs={{32,6},{33,7},{34,32},{35,33},{36,34},{37,35},{38,36},{39,37},{40,... | collective-permute-start | bytes 1572872 | tf_op jit(solution)/shard_map/ppermute | solution.py:104
  60.7 18.3 %collective-permute-start.8 = (f32[256,512]{1,0:T(8,128)S(1)}, f32[256,512]{1,0:T(8,128)S(1)}, u32[]{:S(2)}, u32[]{:S(2)}) collective-permute-start(f32[256,512]{1,0:T(8,128)S(1)} %get-tuple-element.26), channel_id=1, source_target_pairs={{0,2},{1,3},{2,4},{3,5},{4,6},{5,7},{6,32},{7,33},{8,10},{9,11},{1... | collective-permute-start | bytes 1572872 | tf_op jit(solution)/shard_map/ppermute | solution.py:104
  66.1 27.9 %collective-permute-start.12 = (f32[256,512]{1,0:T(8,128)S(1)}, f32[256,512]{1,0:T(8,128)S(1)}, u32[]{:S(2)}, u32[]{:S(2)}) collective-permute-start(f32[256,512]{1,0:T(8,128)S(1)} %get-tuple-element.26), channel_id=1, source_target_pairs={{0,1},{1,0},{2,3},{3,2},{4,5},{5,4},{6,7},{7,6},{8,9},{9,8},{10,11... | collective-permute-start | bytes 1572872 | tf_op jit(solution)/shard_map/ppermute | solution.py:104
  68.1 28.7 %collective-permute-start.11 = (f32[256,512]{1,0:T(8,128)S(1)}, f32[256,512]{1,0:T(8,128)S(1)}, u32[]{:S(2)}, u32[]{:S(2)}) collective-permute-start(f32[256,512]{1,0:T(8,128)S(1)} %get-tuple-element.25), channel_id=1, source_target_pairs={{0,1},{1,0},{2,3},{3,2},{4,5},{5,4},{6,7},{7,6},{8,9},{9,8},{10,11... | collective-permute-start | bytes 1572872 | tf_op jit(solution)/shard_map/ppermute | solution.py:104
  84.1 44.2 %collective-permute-start.5 = (f32[256,512]{1,0:T(8,128)S(1)}, f32[256,512]{1,0:T(8,128)S(1)}, u32[]{:S(2)}, u32[]{:S(2)}) collective-permute-start(f32[256,512]{1,0:T(8,128)S(1)} %get-tuple-element.46), channel_id=1, source_target_pairs={{0,4},{1,5},{2,6},{3,7},{4,32},{5,33},{6,34},{7,35},{8,12},{9,13},... | collective-permute-start | bytes 1572872 | tf_op jit(solution)/shard_map/ppermute | solution.py:104
  86.1 56.7 %collective-permute-start.17 = (f32[256,512]{1,0:T(8,128)S(1)}, f32[256,512]{1,0:T(8,128)S(1)}, u32[]{:S(2)}, u32[]{:S(2)}) collective-permute-start(f32[256,512]{1,0:T(8,128)S(1)} %get-tuple-element.44), channel_id=1, source_target_pairs={{0,4},{1,5},{2,6},{3,7},{4,32},{5,33},{6,34},{7,35},{8,12},{9,13},... | collective-permute-start | bytes 1572872 | tf_op jit(solution)/shard_map/ppermute | solution.py:104
  88.0 38.2 %collective-permute-start.15 = (f32[256,512]{1,0:T(8,128)S(1)}, f32[256,512]{1,0:T(8,128)S(1)}, u32[]{:S(2)}, u32[]{:S(2)}) collective-permute-start(f32[256,512]{1,0:T(8,128)S(1)} %get-tuple-element.45), channel_id=1, source_target_pairs={{0,100},{1,101},{2,102},{3,103},{4,0},{5,1},{6,2},{7,3},{8,108},{9... | collective-permute-start | bytes 1572872 | tf_op jit(solution)/shard_map/ppermute | solution.py:104
  99.6 38.5 %collective-permute-start.20 = (f32[256,512]{1,0:T(8,128)S(1)}, f32[256,512]{1,0:T(8,128)S(1)}, u32[]{:S(2)}, u32[]{:S(2)}) collective-permute-start(f32[256,512]{1,0:T(8,128)S(1)} %get-tuple-element.43), channel_id=1, source_target_pairs={{0,100},{1,101},{2,102},{3,103},{4,0},{5,1},{6,2},{7,3},{8,108},{9... | collective-permute-start | bytes 1572872 | tf_op jit(solution)/shard_map/ppermute | solution.py:104
  126.3 23.2 %collective-permute-start.16 = (f32[256,512]{1,0:T(8,128)S(1)}, f32[256,512]{1,0:T(8,128)S(1)}, u32[]{:S(2)}, u32[]{:S(2)}) collective-permute-start(f32[256,512]{1,0:T(8,128)S(1)} %add.204), channel_id=1, source_target_pairs={{0,102},{1,103},{2,0},{3,1},{4,2},{5,3},{6,4},{7,5},{8,110},{9,111... | collective-permute-start | bytes 1572872 | tf_op jit(solution)/shard_map/ppermute | solution.py:104
  128.4 21.0 %collective-permute-start.13 = (f32[256,512]{1,0:T(8,128)S(1)}, f32[256,512]{1,0:T(8,128)S(1)}, u32[]{:S(2)}, u32[]{:S(2)}) collective-permute-start(f32[256,512]{1,0:T(8,128)S(1)} %add.201), channel_id=1, source_target_pairs={{0,2},{1,3},{2,4},{3,5},{4,6},{5,7},{6,32},{7,33},{8,10},{9,11},{1... | collective-permute-start | bytes 1572872 | tf_op jit(solution)/shard_map/ppermute | solution.py:104
  138.1 22.1 %collective-permute-start.21 = (f32[256,512]{1,0:T(8,128)S(1)}, f32[256,512]{1,0:T(8,128)S(1)}, u32[]{:S(2)}, u32[]{:S(2)}) collective-permute-start(f32[256,512]{1,0:T(8,128)S(1)} %add.210), channel_id=1, source_target_pairs={{0,102},{1,103},{2,0},{3,1},{4,2},{5,3},{6,4},{7,5},{8,110},{9,111... | collective-permute-start | bytes 1572872 | tf_op jit(solution)/shard_map/ppermute | solution.py:104
  142.8 17.4 %collective-permute-start.18 = (f32[256,512]{1,0:T(8,128)S(1)}, f32[256,512]{1,0:T(8,128)S(1)}, u32[]{:S(2)}, u32[]{:S(2)}) collective-permute-start(f32[256,512]{1,0:T(8,128)S(1)} %add.207), channel_id=1, source_target_pairs={{0,2},{1,3},{2,4},{3,5},{4,6},{5,7},{6,32},{7,33},{8,10},{9,11},{1... | collective-permute-start | bytes 1572872 | tf_op jit(solution)/shard_map/ppermute | solution.py:104
  163.9 25.7 %collective-permute-start.22 = (f32[256,512]{1,0:T(8,128)S(1)}, f32[256,512]{1,0:T(8,128)S(1)}, u32[]{:S(2)}, u32[]{:S(2)}) collective-permute-start(f32[256,512]{1,0:T(8,128)S(1)} %fusion.12), channel_id=1, source_target_pairs={{0,2},{1,3},{2,4},{3,5},{4,6},{5,7},{6,32},{7,33},{8,10},{9,11},{1... | collective-permute-start | bytes 1572872 | tf_op jit(solution)/shard_map/ppermute | solution.py:104
  166.0 26.6 %collective-permute-start.30 = (f32[256,512]{1,0:T(8,128)S(1)}, f32[256,512]{1,0:T(8,128)S(1)}, u32[]{:S(2)}, u32[]{:S(2)}) collective-permute-start(f32[256,512]{1,0:T(8,128)S(1)} %fusion.12), channel_id=1, source_target_pairs={{32,6},{33,7},{34,32},{35,33},{36,34},{37,35},{38,36},{39,37},{40,... | collective-permute-start | bytes 1572872 | tf_op jit(solution)/shard_map/ppermute | solution.py:104
  174.4 37.2 %collective-permute-start.26 = (f32[256,512]{1,0:T(8,128)S(1)}, f32[256,512]{1,0:T(8,128)S(1)}, u32[]{:S(2)}, u32[]{:S(2)}) collective-permute-start(f32[256,512]{1,0:T(8,128)S(1)} %fusion.10), channel_id=1, source_target_pairs={{0,2},{1,3},{2,4},{3,5},{4,6},{5,7},{6,32},{7,33},{8,10},{9,11},{1... | collective-permute-start | bytes 1572872 | tf_op jit(solution)/shard_map/ppermute | solution.py:104
  177.4 34.2 %collective-permute-start.35 = (f32[256,512]{1,0:T(8,128)S(1)}, f32[256,512]{1,0:T(8,128)S(1)}, u32[]{:S(2)}, u32[]{:S(2)}) collective-permute-start(f32[256,512]{1,0:T(8,128)S(1)} %fusion.10), channel_id=1, source_target_pairs={{32,6},{33,7},{34,32},{35,33},{36,34},{37,35},{38,36},{39,37},{40,... | collective-permute-start | bytes 1572872 | tf_op jit(solution)/shard_map/ppermute | solution.py:104
  184.8 16.7 %collective-permute-start.24 = (f32[256,512]{1,0:T(8,128)S(1)}, f32[256,512]{1,0:T(8,128)S(1)}, u32[]{:S(2)}, u32[]{:S(2)}) collective-permute-start(f32[256,512]{1,0:T(8,128)S(1)} %multiply_add_fusion.9), channel_id=1, source_target_pairs={{6,14},{7,15},{8,0},{9,1},{14,22},{15,23},{16,8},{17,9},{22,30},{2... | collective-permute-start | bytes 1572872 | tf_op jit(solution)/shard_map/ppermute | solution.py:104
  189.6 22.1 %collective-permute-start.28 = (f32[256,512]{1,0:T(8,128)S(1)}, f32[256,512]{1,0:T(8,128)S(1)}, u32[]{:S(2)}, u32[]{:S(2)}) collective-permute-start(f32[256,512]{1,0:T(8,128)S(1)} %multiply_add_fusion.7), channel_id=1, source_target_pairs={{6,14},{7,15},{8,0},{9,1},{14,22},{15,23},{16,8},{17,9},{22,30},{2... | collective-permute-start | bytes 1572872 | tf_op jit(solution)/shard_map/ppermute | solution.py:104
  213.0 59.2 %collective-permute-start.33 = (f32[256,512]{1,0:T(8,128)S(1)}, f32[256,512]{1,0:T(8,128)S(1)}, u32[]{:S(2)}, u32[]{:S(2)}) collective-permute-start(f32[256,512]{1,0:T(8,128)S(1)} %get-tuple-element.54), channel_id=1, source_target_pairs={{0,4},{1,5},{2,6},{3,7},{4,32},{5,33},{6,34},{7,35},{8,12},{9,13},... | collective-permute-start | bytes 1572872 | tf_op jit(solution)/shard_map/ppermute | solution.py:104
  215.0 47.9 %collective-permute-start.25 = (f32[256,512]{1,0:T(8,128)S(1)}, f32[256,512]{1,0:T(8,128)S(1)}, u32[]{:S(2)}, u32[]{:S(2)}) collective-permute-start(f32[256,512]{1,0:T(8,128)S(1)} %get-tuple-element.56), channel_id=1, source_target_pairs={{0,4},{1,5},{2,6},{3,7},{4,32},{5,33},{6,34},{7,35},{8,12},{9,13},... | collective-permute-start | bytes 1572872 | tf_op jit(solution)/shard_map/ppermute | solution.py:104
  218.4 36.5 %collective-permute-start.31 = (f32[256,512]{1,0:T(8,128)S(1)}, f32[256,512]{1,0:T(8,128)S(1)}, u32[]{:S(2)}, u32[]{:S(2)}) collective-permute-start(f32[256,512]{1,0:T(8,128)S(1)} %get-tuple-element.55), channel_id=1, source_target_pairs={{0,100},{1,101},{2,102},{3,103},{4,0},{5,1},{6,2},{7,3},{8,108},{9... | collective-permute-start | bytes 1572872 | tf_op jit(solution)/shard_map/ppermute | solution.py:104
  228.5 38.8 %collective-permute-start.36 = (f32[256,512]{1,0:T(8,128)S(1)}, f32[256,512]{1,0:T(8,128)S(1)}, u32[]{:S(2)}, u32[]{:S(2)}) collective-permute-start(f32[256,512]{1,0:T(8,128)S(1)} %get-tuple-element.53), channel_id=1, source_target_pairs={{0,100},{1,101},{2,102},{3,103},{4,0},{5,1},{6,2},{7,3},{8,108},{9... | collective-permute-start | bytes 1572872 | tf_op jit(solution)/shard_map/ppermute | solution.py:104
  255.0 23.7 %collective-permute-start.32 = (f32[256,512]{1,0:T(8,128)S(1)}, f32[256,512]{1,0:T(8,128)S(1)}, u32[]{:S(2)}, u32[]{:S(2)}) collective-permute-start(f32[256,512]{1,0:T(8,128)S(1)} %add.229), channel_id=1, source_target_pairs={{0,102},{1,103},{2,0},{3,1},{4,2},{5,3},{6,4},{7,5},{8,110},{9,111... | collective-permute-start | bytes 1572872 | tf_op jit(solution)/shard_map/ppermute | solution.py:104
  263.0 17.9 %collective-permute-start.29 = (f32[256,512]{1,0:T(8,128)S(1)}, f32[256,512]{1,0:T(8,128)S(1)}, u32[]{:S(2)}, u32[]{:S(2)}) collective-permute-start(f32[256,512]{1,0:T(8,128)S(1)} %add.227), channel_id=1, source_target_pairs={{0,2},{1,3},{2,4},{3,5},{4,6},{5,7},{6,32},{7,33},{8,10},{9,11},{1... | collective-permute-start | bytes 1572872 | tf_op jit(solution)/shard_map/ppermute | solution.py:104
  267.4 21.6 %collective-permute-start.37 = (f32[256,512]{1,0:T(8,128)S(1)}, f32[256,512]{1,0:T(8,128)S(1)}, u32[]{:S(2)}, u32[]{:S(2)}) collective-permute-start(f32[256,512]{1,0:T(8,128)S(1)} %add.234), channel_id=1, source_target_pairs={{0,102},{1,103},{2,0},{3,1},{4,2},{5,3},{6,4},{7,5},{8,110},{9,111... | collective-permute-start | bytes 1572872 | tf_op jit(solution)/shard_map/ppermute | solution.py:104
  272.3 18.8 %collective-permute-start.34 = (f32[256,512]{1,0:T(8,128)S(1)}, f32[256,512]{1,0:T(8,128)S(1)}, u32[]{:S(2)}, u32[]{:S(2)}) collective-permute-start(f32[256,512]{1,0:T(8,128)S(1)} %add.232), channel_id=1, source_target_pairs={{0,2},{1,3},{2,4},{3,5},{4,6},{5,7},{6,32},{7,33},{8,10},{9,11},{1... | collective-permute-start | bytes 1572872 | tf_op jit(solution)/shard_map/ppermute | solution.py:104
  (14 other events, 239.5 us)

commit v4 on v3

v4 whole, which is shorter than its diff:
```python
import jax
import jax.numpy as jnp
import numpy as np
from jax import lax
from jax.sharding import PartitionSpec as P

ITERS = 2
NX, NY, NHI, NLO = 4, 4, 4, 4
NZ = NHI * NLO
NI = NY * NHI
NJ = NX * NLO * 2

HIGH = lax.Precision.HIGH
AXES = ("ia", "ja")


def chip(i, j):
    return j // (2 * NLO), i // NHI, (i % NHI) * NLO + (j // 2) % NLO, j % 2


def pair(x, y, z, c):
    z = z % NZ
    return y * NHI + z // NLO, (x * NLO + z % NLO) * 2 + c


def moves(target):
    pairs = []
    for i in range(NI):
        for j in range(NJ):
            to = target(i, j)
            if to is not None:
                pairs.append((i * NJ + j, to[0] * NJ + to[1]))
    return pairs


def way(core):
    return 1 - 2 * core


def first_leg(mate):
    def target(i, j):
        x, _, z, c = chip(i, j)
        relay = 1 - c if mate else c
        step = way(relay)
        if not 0 <= i + step < NI:
            return None
        return pair(x, (i + step) // NHI, z + step, relay)

    return moves(target)


def middle_leg(i, j):
    x, y, z, c = chip(i, j)
    step = way(c)
    di, dj = pair(x, y, z + 3 * step, c)
    edge = NLO - 1 if step > 0 else 0
    if not 0 <= di - step < NI and (dj // 2) % NLO != edge:
        return None
    return pair(x, y, z + 2 * step, c)


def last_leg(mate):
    def target(i, j):
        x, y, z, c = chip(i, j)
        step = way(c)
        di, dj = pair(x, y, z + step, 1 - c if mate else c)
        near = 0 if step > 0 else NLO - 1
        if not 0 <= di - step < NI and (dj // 2) % NLO == near:
            return None
        return di, dj

    return moves(target)


def across(mate):
    def target(i, j):
        x, y, z, c = chip(i, j)
        relay = 1 - c if mate else c
        if z % NLO == 0 and relay == 0 and x > 0:
            return pair(x - 1, y, z, relay)
        if z % NLO == NLO - 1 and relay == 1 and x + 1 < NX:
            return pair(x + 1, y, z, relay)
        return None

    return moves(target)


def goal_links(hops, mate):
    def target(i, j):
        x, y, z, c = chip(i, j)
        relay = 1 - c if mate else c
        return pair(x, y, z - hops * way(relay), relay)

    return moves(target)


FIRST = {"A": first_leg(False), "B": first_leg(True)}
MIDDLE = moves(middle_leg)
LAST = {"A": last_leg(False), "B": last_leg(True)}
ACROSS = {"A": across(False), "B": across(True)}
PARTNER = moves(lambda i, j: (i, j ^ 1))


def send(x, pairs):
    return lax.ppermute(x, AXES, pairs)


def mm(a, b):
    return jnp.dot(a, b, precision=HIGH, preferred_element_type=jnp.float32)


def build_dense(blocks, columns):
    block_rows, block_size, block_wide = blocks.shape
    wide = block_rows * block_size
    slot = jnp.arange(block_wide, dtype=jnp.int32)
    place = jnp.repeat(columns, block_size, axis=1) * block_size + (slot % block_size)[None, :]
    spread = (place[:, :, None] == jnp.arange(wide, dtype=jnp.int32)[None, None, :]).astype(jnp.float32)
    dense = jnp.einsum("rxk,rkn->rxn", blocks, spread, precision=HIGH)
    return dense.reshape(wide, wide)


SOURCES = ("own", "far", "far_mate", "next", "next_mate")
LINK = {name: 8 * n for n, name in enumerate(SOURCES)}
UNIT = 8 * len(SOURCES)
(
    PASS,
    PASS_MATE,
    CROSS,
    CROSS_MATE,
    CROSS_OWN,
    NEAR,
    NEAR_OTHER,
    NEAR_MATE,
    MATE,
    FIRST_DIAGONAL,
    SECOND_DIAGONAL,
) = range(11)
COLUMN = 4


def tables():
    places = np.zeros((NI * NJ, 11, 3), np.int8)
    for i in range(NI):
        for j in range(NJ):
            x, y, z, c = chip(i, j)
            s = way(c)
            low = z % NLO
            di, dj = pair(x, y, z + 3 * s, c)
            _, nj = pair(x, y, z + s, c)
            inside = 0 <= di - s < NI
            crosses = low == (0 if s > 0 else NLO - 1)
            joins = low != (NLO - 1 if s > 0 else 0)
            column = COLUMN + (0 if s > 0 else 1)
            on2, on1, back2, back1 = (3, 2, 0, 1) if s > 0 else (0, 1, 3, 2)
            entries = [
                (di, di - s, LINK["far"] + column, inside),
                (di, di - s, LINK["far_mate"] + column, inside),
                (dj + 2 * s, dj, LINK["far"] + on2, crosses),
                (dj + 3 * s, dj + s, LINK["far_mate"] + on2, crosses),
                (dj + 2 * s, dj + s, LINK["far_mate"] + on1, crosses),
                (j, nj, LINK["next"] + back2, joins),
                (j + s, nj, LINK["next"] + back1, joins),
                (j + s, nj + s, LINK["next_mate"] + back2, joins),
                (j + s, j, LINK["own"] + on1, True),
                (i, i, UNIT, True),
                (j, j, UNIT, True),
            ]
            for n, (row, to, link, used) in enumerate(entries):
                used = used and 0 <= row < NJ and 0 <= to < NJ
                places[i * NJ + j, n] = (row, to, link) if used else (-1, 0, 0)
    return places


TABLE = tables()


def chosen(place, occ_fock, got):
    rows, columns, link = place[:, 0], place[:, 1], place[:, 2]
    spots = jnp.arange(NJ, dtype=jnp.int32)
    hot = (rows[:, None, None] == spots[None, :, None]) & (columns[:, None, None] == spots[None, None, :])
    picked = jnp.sum(jnp.where(hot, occ_fock[None], 0.0), axis=(1, 2))
    nothing = jnp.zeros((8,), jnp.int32)
    flat = jnp.concatenate([got.get(name, nothing) for name in SOURCES] + [jnp.ones((8,), jnp.int32)])
    taken = link[:, None] == jnp.arange(UNIT + 8, dtype=jnp.int32)[None, :]
    weights = jnp.sum(jnp.where(taken, flat[None, :], 0), axis=1)
    return picked * weights.astype(jnp.float32)


def coefficients(occ_fock, row_links, column_links):
    links = jnp.concatenate([row_links, column_links, jnp.zeros((2,), jnp.int32)])
    where = lax.axis_index("ia") * NJ + lax.axis_index("ja")
    place = lax.dynamic_slice_in_dim(jnp.asarray(TABLE), where, 1, axis=0)[0].astype(jnp.int32)
    got = {
        "own": links,
        "far": send(links, goal_links(3, False)),
        "far_mate": send(links, goal_links(3, True)),
        "next": send(links, goal_links(1, False)),
        "next_mate": send(links, goal_links(1, True)),
    }
    return chosen(place, occ_fock, got)


def after(value, earlier):
    return lax.optimization_barrier((value, earlier))[0]


def neighbour_sum(current, weight):
    cross_own = send(current, ACROSS["A"])
    first_own = send(current, FIRST["A"])
    mate = send(current, PARTNER)
    cross_mate = send(current, ACROSS["B"])
    first_mate = send(current, FIRST["B"])
    passed = weight[PASS] * first_own + weight[CROSS] * cross_own
    middle_own = send(passed, MIDDLE)
    cross_own = after(cross_own, passed)
    passed = weight[PASS_MATE] * first_mate + weight[CROSS_MATE] * cross_mate + weight[CROSS_OWN] * cross_own
    middle_mate = send(passed, MIDDLE)
    held = after(current, passed)
    near = (weight[NEAR] * held + weight[NEAR_OTHER] * mate, weight[NEAR_MATE] * mate)
    near_own, near_mate = lax.optimization_barrier(near)
    last_own = send(middle_own + near_own, LAST["A"])
    last_mate = send(middle_mate + near_mate, LAST["B"])
    return last_own + weight[MATE] * mate, last_mate


def body(
    amplitudes,
    integrals,
    pao_fock,
    pao_intersection,
    block_columns,
    occ_fock,
    pao_energies,
    row_links,
    column_links,
):
    start = amplitudes[0, 0]
    integral = integrals[0, 0]
    current = start
    for sweep_number in range(ITERS):
        if sweep_number == 0:
            weight = coefficients(occ_fock, row_links[0, 0], column_links[0, 0])
            diagonal = weight[FIRST_DIAGONAL] + weight[SECOND_DIAGONAL]
            fock_dense = build_dense(pao_fock, block_columns)
            intersection_dense = build_dense(pao_intersection, block_columns)
            shifted = fock_dense - diagonal * intersection_dense
            inverse_gap = 1.0 / (pao_energies[:, None] + pao_energies[None, :] - diagonal)
        parts = neighbour_sum(current, weight)
        from_fock = mm(shifted, current)
        from_intersection = mm(intersection_dense, current)
        local = mm(from_fock, intersection_dense)
        local = local + mm(from_intersection, fock_dense) + integral.astype(jnp.float32)
        for part in parts:
            local = local - mm(intersection_dense, mm(part, intersection_dense))
        current = current - local * inverse_gap
    return current[None, None]


def solution(mesh):
    placed = (
        P("ia", "ja", None, None),
        P("ia", "ja", None, None),
        P(),
        P(),
        P(),
        P(),
        P(),
        P("ia", "ja", None),
        P("ia", "ja", None),
    )
    return jax.shard_map(
        body, mesh=mesh, in_specs=placed, out_specs=P("ia", "ja", None, None), check_vma=False
    )
```

time: 296 us -> 252 us (0.85)
  the two profiles are of different devices: /device:TPU:10 before, /device:TPU:15 now
where the time goes in v4:
time: 252 us; the launch traced here: 251 us
  starting transfers between devices  139 us (55%)
  waiting for transfers between devices  65.7 us (26%)
  matrix products  24.3 us (10%)
  other arithmetic  18.7 us (7%)
    ppermute x22, starting transfers between devices, send(): return lax.ppermute(x, AXES, pairs)  139 us
    ppermute x22, waiting for transfers between devices, send(): return lax.ppermute(x, AXES, pairs)  65.7 us
    dot_general x16, matrix products, mm(): return jnp.dot(a, b, precision=HIGH, preferred_element_type=jnp.float32)  19.4 us
    add x2, other arithmetic, neighbour_sum(): weight[PASS_MATE] * first_mate + weight[CROSS_MATE] * cross_mate  5.91 us
  transfers between devices with their start and end apart: 22, of which 13 were waited for; matrix products, arithmetic and copies ran while one was open for 16% of the time, Pallas kernels for 0%

profile of v4, /device:TPU:15, one launch (start us, length us, event | category | flops | bytes accessed | tf_op | source)
XLA Modules:
  0.0 250.9 jit_solution(8292497972122983985)
XLA Ops:
  0.0 4.2 %collective-permute-start.8 = (f32[512,512]{1,0:T(8,128)}, f32[512,512]{1,0:T(8,128)}, u32[]{:S(2)}, u32[]{:S(2)}) collective-permute-start(f32[512,512]{1,0:T(8,128)} %bitcast.89), channel_id=1, source_target_pairs={{6,15},{9,0},{14,23},{17,8},{22,31},{25,16},{38,47},{41,32},{46,55... | collective-permute-start | bytes 3145736 | tf_op jit(solution)/shard_map/ppermute | solution.py:105
  6.8 8.9 %collective-permute-start.4 = (f32[512,512]{1,0:T(8,128)}, f32[512,512]{1,0:T(8,128)}, u32[]{:S(2)}, u32[]{:S(2)}) collective-permute-start(f32[512,512]{1,0:T(8,128)} %bitcast.92), channel_id=1, source_target_pairs={{0,2},{2,4},{4,6},{6,32},{8,10},{10,12},{12,14},{14,40},{16,18},{1... | collective-permute-start | bytes 3145736 | tf_op jit(solution)/shard_map/ppermute | solution.py:105
  16.4 7.6 %collective-permute-start.3 = (s32[8]{0:T(128)S(1)}, s32[8]{0:T(128)S(1)}, u32[]{:S(2)}, u32[]{:S(2)}) collective-permute-start(s32[8]{0:T(128)S(1)} %pad_add_fusion), channel_id=1, source_target_pairs={{0,3},{1,102},{2,5},{3,0},{4,7},{5,2},{6,33},{7,4},{8,11},{9,110},... | collective-permute-start | bytes 104 | tf_op jit(solution)/shard_map/ppermute | solution.py:105
  26.7 9.8 %collective-permute-done.3 = s32[8]{0:T(128)S(1)} collective-permute-done((s32[8]{0:T(128)S(1)}, s32[8]{0:T(128)S(1)}, u32[]{:S(2)}, u32[]{:S(2)}) %collective-permute-start.3) | collective-permute-done | bytes 64 | tf_op jit(solution)/shard_map/ppermute | solution.py:105
  38.4 4.3 %collective-permute-done.2 = s32[8]{0:T(128)S(1)} collective-permute-done((s32[8]{0:T(128)S(1)}, s32[8]{0:T(128)S(1)}, u32[]{:S(2)}, u32[]{:S(2)}) %collective-permute-start.2) | collective-permute-done | bytes 64 | tf_op jit(solution)/shard_map/ppermute | solution.py:105
  42.7 5.8 %collective-permute-start.1 = (s32[8]{0:T(128)S(1)}, s32[8]{0:T(128)S(1)}, u32[]{:S(2)}, u32[]{:S(2)}) collective-permute-start(s32[8]{0:T(128)S(1)} %pad_add_fusion), channel_id=1, source_target_pairs={{0,7},{1,98},{2,33},{3,100},{4,35},{5,102},{6,37},{7,0},{8,15},{9,... | collective-permute-start | bytes 104 | tf_op jit(solution)/shard_map/ppermute | solution.py:105
  48.5 2.1 collective-permute-done.1
  52.5 5.4 %collective-permute-done = s32[8]{0:T(128)S(1)} collective-permute-done((s32[8]{0:T(128)S(1)}, s32[8]{0:T(128)S(1)}, u32[]{:S(2)}, u32[]{:S(2)}) %collective-permute-start) | collective-permute-done | bytes 64 | tf_op jit(solution)/shard_map/ppermute | solution.py:105
  61.6 2.8 %multiply_add_fusion.5 = f32[512,512]{1,0:T(8,128)S(1)} fusion(f32[512,512]{1,0:T(8,128)S(1)} %collective-permute-done.5, f32[512,512]{1,0:T(8,128)} %collective-permute-done.4, f32[]{:T(128)} %bitcast.17, f32[]{:T(128)} %bitcast.16), kind=kLoop, calls=%fused_computation.35 | loop fusion | flops 786432 | bytes 3145736 | tf_op jit(solution)/shard_map/add | solution.py:213
  64.4 5.4 %collective-permute-start.6 = (f32[512,512]{1,0:T(8,128)S(1)}, f32[512,512]{1,0:T(8,128)S(1)}, u32[]{:S(2)}, u32[]{:S(2)}) collective-permute-start(f32[512,512]{1,0:T(8,128)S(1)} %multiply_add_fusion.5), channel_id=1, source_target_pairs={{0,4},{1,101},{2,6},{3,103},{4,32},{5,1},{6,34},{7,3},{8,12},{9,10... | collective-permute-start | bytes 3145736 | tf_op jit(solution)/shard_map/ppermute | solution.py:105
  69.8 2.5 fusion.1
  73.6 3.7 %multiply_add_fusion.4 = f32[512,512]{1,0:T(8,128)S(1)} fusion(f32[512,512]{1,0:T(8,128)S(1)} %collective-permute-done.5, f32[512,512]{1,0:T(8,128)} %collective-permute-done.8, f32[512,512]{1,0:T(8,128)} %collective-permute-done.7, f32[]{:T(128)} %bitcast.21, f32[]{:T(128)} %bitcast.20, f32[]{:T(128)} %bitcast.19), kind=kLoop, calls=%fused_computation.34 | loop fusion | flops 1310720 | bytes 4194316 | tf_op jit(solution)/shard_map/add | solution.py:216
  77.3 3.0 %collective-permute-start.11 = (f32[512,512]{1,0:T(8,128)S(1)}, f32[512,512]{1,0:T(8,128)S(1)}, u32[]{:S(2)}, u32[]{:S(2)}) collective-permute-start(f32[512,512]{1,0:T(8,128)S(1)} %multiply_add_fusion.4), channel_id=1, source_target_pairs={{0,4},{1,101},{2,6},{3,103},{4,32},{5,1},{6,34},{7,3},{8,12},{9,10... | collective-permute-start | bytes 3145736 | tf_op jit(solution)/shard_map/ppermute | solution.py:105
  80.4 2.5 fusion.11
  82.9 2.2 broadcast_multiply_fusion.1
  85.4 26.1 %collective-permute-start.10 = (f32[512,512]{1,0:T(8,128)S(1)}, f32[512,512]{1,0:T(8,128)S(1)}, u32[]{:S(2)}, u32[]{:S(2)}) collective-permute-start(f32[512,512]{1,0:T(8,128)S(1)} %add.120), channel_id=1, source_target_pairs={{0,2},{1,103},{2,4},{3,1},{4,6},{5,3},{6,32},{7,5},{8,10},{9,111},... | collective-permute-start | bytes 3145736 | tf_op jit(solution)/shard_map/ppermute | solution.py:105
  113.8 7.6 %collective-permute-start.12 = (f32[512,512]{1,0:T(8,128)S(1)}, f32[512,512]{1,0:T(8,128)S(1)}, u32[]{:S(2)}, u32[]{:S(2)}) collective-permute-start(f32[512,512]{1,0:T(8,128)S(1)} %add.122), channel_id=1, source_target_pairs={{0,3},{1,102},{2,5},{3,0},{4,7},{5,2},{6,33},{7,4},{8,11},{9,110},... | collective-permute-start | bytes 3145736 | tf_op jit(solution)/shard_map/ppermute | solution.py:105
  123.6 5.9 %collective-permute-done.10 = f32[512,512]{1,0:T(8,128)S(1)} collective-permute-done((f32[512,512]{1,0:T(8,128)S(1)}, f32[512,512]{1,0:T(8,128)S(1)}, u32[]{:S(2)}, u32[]{:S(2)}) %collective-permute-start.10) | collective-permute-done | bytes 1048608 | tf_op jit(solution)/shard_map/ppermute | solution.py:105
  132.3 7.7 %collective-permute-done.12 = f32[512,512]{1,0:T(8,128)S(1)} collective-permute-done((f32[512,512]{1,0:T(8,128)S(1)}, f32[512,512]{1,0:T(8,128)S(1)}, u32[]{:S(2)}, u32[]{:S(2)}) %collective-permute-start.12) | collective-permute-done | bytes 1048608 | tf_op jit(solution)/shard_map/ppermute | solution.py:105
  143.0 2.1 collective-permute-start.13
  145.1 5.9 %collective-permute-start.17 = (f32[512,512]{1,0:T(8,128)S(1)}, f32[512,512]{1,0:T(8,128)S(1)}, u32[]{:S(2)}, u32[]{:S(2)}) collective-permute-start(f32[512,512]{1,0:T(8,128)S(1)} %fusion.8), channel_id=1, source_target_pairs={{6,15},{9,0},{14,23},{17,8},{22,31},{25,16},{38,47},{41,32},{46,55... | collective-permute-start | bytes 3145736 | tf_op jit(solution)/shard_map/ppermute | solution.py:105
  154.8 7.6 %collective-permute-done.13 = f32[512,512]{1,0:T(8,128)S(1)} collective-permute-done((f32[512,512]{1,0:T(8,128)S(1)}, f32[512,512]{1,0:T(8,128)S(1)}, u32[]{:S(2)}, u32[]{:S(2)}) %collective-permute-start.13) | collective-permute-done | bytes 1048608 | tf_op jit(solution)/shard_map/ppermute | solution.py:105
  163.9 5.6 %collective-permute-start.15 = (f32[512,512]{1,0:T(8,128)S(1)}, f32[512,512]{1,0:T(8,128)S(1)}, u32[]{:S(2)}, u32[]{:S(2)}) collective-permute-start(f32[512,512]{1,0:T(8,128)S(1)} %multiply_add_fusion.2), channel_id=1, source_target_pairs={{0,4},{1,101},{2,6},{3,103},{4,32},{5,1},{6,34},{7,3},{8,12},{9,10... | collective-permute-start | bytes 3145736 | tf_op jit(solution)/shard_map/ppermute | solution.py:105
  169.9 2.2 collective-permute-done.16
  172.1 2.2 multiply_add_fusion.1
  174.2 4.1 %collective-permute-start.20 = (f32[512,512]{1,0:T(8,128)S(1)}, f32[512,512]{1,0:T(8,128)S(1)}, u32[]{:S(2)}, u32[]{:S(2)}) collective-permute-start(f32[512,512]{1,0:T(8,128)S(1)} %multiply_add_fusion.1), channel_id=1, source_target_pairs={{0,4},{1,101},{2,6},{3,103},{4,32},{5,1},{6,34},{7,3},{8,12},{9,10... | collective-permute-start | bytes 3145736 | tf_op jit(solution)/shard_map/ppermute | solution.py:105
  178.4 2.2 broadcast_multiply_fusion
  181.8 25.6 %collective-permute-start.19 = (f32[512,512]{1,0:T(8,128)S(1)}, f32[512,512]{1,0:T(8,128)S(1)}, u32[]{:S(2)}, u32[]{:S(2)}) collective-permute-start(f32[512,512]{1,0:T(8,128)S(1)} %add.132), channel_id=1, source_target_pairs={{0,2},{1,103},{2,4},{3,1},{4,6},{5,3},{6,32},{7,5},{8,10},{9,111},... | collective-permute-start | bytes 3145736 | tf_op jit(solution)/shard_map/ppermute | solution.py:105
  209.5 5.4 %collective-permute-done.20 = f32[512,512]{1,0:T(8,128)S(1)} collective-permute-done((f32[512,512]{1,0:T(8,128)S(1)}, f32[512,512]{1,0:T(8,128)S(1)}, u32[]{:S(2)}, u32[]{:S(2)}) %collective-permute-start.20) | collective-permute-done | bytes 1048608 | tf_op jit(solution)/shard_map/ppermute | solution.py:105
  215.2 13.7 %collective-permute-start.21 = (f32[512,512]{1,0:T(8,128)S(1)}, f32[512,512]{1,0:T(8,128)S(1)}, u32[]{:S(2)}, u32[]{:S(2)}) collective-permute-start(f32[512,512]{1,0:T(8,128)S(1)} %add.134), channel_id=1, source_target_pairs={{0,3},{1,102},{2,5},{3,0},{4,7},{5,2},{6,33},{7,4},{8,11},{9,110},... | collective-permute-start | bytes 3145736 | tf_op jit(solution)/shard_map/ppermute | solution.py:105
  233.9 13.8 %collective-permute-done.21 = f32[512,512]{1,0:T(8,128)S(1)} collective-permute-done((f32[512,512]{1,0:T(8,128)S(1)}, f32[512,512]{1,0:T(8,128)S(1)}, u32[]{:S(2)}, u32[]{:S(2)}) %collective-permute-start.21) | collective-permute-done | bytes 1048608 | tf_op jit(solution)/shard_map/ppermute | solution.py:105
  248.7 2.2 fusion.10
  (66 shorter events, 39.1 us)
Async XLA Ops:
  0.0 80.4 %copy-start = (f32[8,64,384]{2,1,0:T(8,128)S(1)}, f32[8,64,384]{2,1,0:T(8,128)}, u32[]{:S(2)}) copy-start(f32[8,64,384]{2,1,0:T(8,128)} %param.13) | copy-start | bytes 2359300
  0.0 73.6 %collective-permute-start.8 = (f32[512,512]{1,0:T(8,128)}, f32[512,512]{1,0:T(8,128)}, u32[]{:S(2)}, u32[]{:S(2)}) collective-permute-start(f32[512,512]{1,0:T(8,128)} %bitcast.89), channel_id=1, source_target_pairs={{6,15},{9,0},{14,23},{17,8},{22,31},{25,16},{38,47},{41,32},{46,55... | collective-permute-start | bytes 3145736 | tf_op jit(solution)/shard_map/ppermute | solution.py:105
  4.2 69.4 %collective-permute-start.7 = (f32[512,512]{1,0:T(8,128)}, f32[512,512]{1,0:T(8,128)}, u32[]{:S(2)}, u32[]{:S(2)}) collective-permute-start(f32[512,512]{1,0:T(8,128)} %bitcast.90), channel_id=1, source_target_pairs={{1,2},{3,4},{5,6},{7,32},{9,10},{11,12},{13,14},{15,40},{17,18},{1... | collective-permute-start | bytes 3145736 | tf_op jit(solution)/shard_map/ppermute | solution.py:105
  6.1 55.5 %collective-permute-start.5 = (f32[512,512]{1,0:T(8,128)}, f32[512,512]{1,0:T(8,128)S(1)}, u32[]{:S(2)}, u32[]{:S(2)}) collective-permute-start(f32[512,512]{1,0:T(8,128)} %bitcast.91), channel_id=1, source_target_pairs={{7,15},{8,0},{15,23},{16,8},{23,31},{24,16},{39,47},{40,32},{47,55... | collective-permute-start | bytes 3145736 | tf_op jit(solution)/shard_map/ppermute | solution.py:105
  6.8 54.8 %collective-permute-start.4 = (f32[512,512]{1,0:T(8,128)}, f32[512,512]{1,0:T(8,128)}, u32[]{:S(2)}, u32[]{:S(2)}) collective-permute-start(f32[512,512]{1,0:T(8,128)} %bitcast.92), channel_id=1, source_target_pairs={{0,2},{2,4},{4,6},{6,32},{8,10},{10,12},{12,14},{14,40},{16,18},{1... | collective-permute-start | bytes 3145736 | tf_op jit(solution)/shard_map/ppermute | solution.py:105
  16.4 20.0 %collective-permute-start.3 = (s32[8]{0:T(128)S(1)}, s32[8]{0:T(128)S(1)}, u32[]{:S(2)}, u32[]{:S(2)}) collective-permute-start(s32[8]{0:T(128)S(1)} %pad_add_fusion), channel_id=1, source_target_pairs={{0,3},{1,102},{2,5},{3,0},{4,7},{5,2},{6,33},{7,4},{8,11},{9,110},... | collective-permute-start | bytes 104 | tf_op jit(solution)/shard_map/ppermute | solution.py:105
  36.5 6.2 %collective-permute-start.2 = (s32[8]{0:T(128)S(1)}, s32[8]{0:T(128)S(1)}, u32[]{:S(2)}, u32[]{:S(2)}) collective-permute-start(s32[8]{0:T(128)S(1)} %pad_add_fusion), channel_id=1, source_target_pairs={{0,102},{1,3},{2,0},{3,5},{4,2},{5,7},{6,4},{7,33},{8,110},{9,11},... | collective-permute-start | bytes 104 | tf_op jit(solution)/shard_map/ppermute | solution.py:105
  42.7 7.9 %collective-permute-start.1 = (s32[8]{0:T(128)S(1)}, s32[8]{0:T(128)S(1)}, u32[]{:S(2)}, u32[]{:S(2)}) collective-permute-start(s32[8]{0:T(128)S(1)} %pad_add_fusion), channel_id=1, source_target_pairs={{0,7},{1,98},{2,33},{3,100},{4,35},{5,102},{6,37},{7,0},{8,15},{9,... | collective-permute-start | bytes 104 | tf_op jit(solution)/shard_map/ppermute | solution.py:105
  50.6 7.3 %collective-permute-start = (s32[8]{0:T(128)S(1)}, s32[8]{0:T(128)S(1)}, u32[]{:S(2)}, u32[]{:S(2)}) collective-permute-start(s32[8]{0:T(128)S(1)} %pad_add_fusion), channel_id=1, source_target_pairs={{0,98},{1,7},{2,100},{3,33},{4,102},{5,35},{6,0},{7,37},{8,106},{9... | collective-permute-start | bytes 104 | tf_op jit(solution)/shard_map/ppermute | solution.py:105
  57.9 25.0 %collective-permute-start.9 = (f32[512,512]{1,0:T(8,128)}, f32[512,512]{1,0:T(8,128)S(1)}, u32[]{:S(2)}, u32[]{:S(2)}) collective-permute-start(f32[512,512]{1,0:T(8,128)} %bitcast.93), channel_id=1, source_target_pairs={{0,1},{1,0},{2,3},{3,2},{4,5},{5,4},{6,7},{7,6},{8,9},{9,8},{10,11... | collective-permute-start | bytes 3145736 | tf_op jit(solution)/shard_map/ppermute | solution.py:105
  61.6 8.2 %copy-start.3 = (f32[8,64,384]{2,1,0:T(8,128)S(1)}, f32[8,64,384]{2,1,0:T(8,128)}, u32[]{:S(2)}) copy-start(f32[8,64,384]{2,1,0:T(8,128)} %param.12) | copy-start | bytes 2359300
  64.4 20.7 %collective-permute-start.6 = (f32[512,512]{1,0:T(8,128)S(1)}, f32[512,512]{1,0:T(8,128)S(1)}, u32[]{:S(2)}, u32[]{:S(2)}) collective-permute-start(f32[512,512]{1,0:T(8,128)S(1)} %multiply_add_fusion.5), channel_id=1, source_target_pairs={{0,4},{1,101},{2,6},{3,103},{4,32},{5,1},{6,34},{7,3},{8,12},{9,10... | collective-permute-start | bytes 3145736 | tf_op jit(solution)/shard_map/ppermute | solution.py:105
  77.3 36.3 %collective-permute-start.11 = (f32[512,512]{1,0:T(8,128)S(1)}, f32[512,512]{1,0:T(8,128)S(1)}, u32[]{:S(2)}, u32[]{:S(2)}) collective-permute-start(f32[512,512]{1,0:T(8,128)S(1)} %multiply_add_fusion.4), channel_id=1, source_target_pairs={{0,4},{1,101},{2,6},{3,103},{4,32},{5,1},{6,34},{7,3},{8,12},{9,10... | collective-permute-start | bytes 3145736 | tf_op jit(solution)/shard_map/ppermute | solution.py:105
  80.4 2.5 copy-start.1
  85.4 44.1 %collective-permute-start.10 = (f32[512,512]{1,0:T(8,128)S(1)}, f32[512,512]{1,0:T(8,128)S(1)}, u32[]{:S(2)}, u32[]{:S(2)}) collective-permute-start(f32[512,512]{1,0:T(8,128)S(1)} %add.120), channel_id=1, source_target_pairs={{0,2},{1,103},{2,4},{3,1},{4,6},{5,3},{6,32},{7,5},{8,10},{9,111},... | collective-permute-start | bytes 3145736 | tf_op jit(solution)/shard_map/ppermute | solution.py:105
  113.8 8.7 %copy-start.2 = (bf16[1,1,512,512]{3,2,1,0:T(8,128)(2,1)S(1)}, bf16[1,1,512,512]{3,2,1,0:T(8,128)(2,1)}, u32[]{:S(2)}) copy-start(bf16[1,1,512,512]{3,2,1,0:T(8,128)(2,1)} %param.11) | copy-start | bytes 1572868
  113.8 26.1 %collective-permute-start.12 = (f32[512,512]{1,0:T(8,128)S(1)}, f32[512,512]{1,0:T(8,128)S(1)}, u32[]{:S(2)}, u32[]{:S(2)}) collective-permute-start(f32[512,512]{1,0:T(8,128)S(1)} %add.122), channel_id=1, source_target_pairs={{0,3},{1,102},{2,5},{3,0},{4,7},{5,2},{6,33},{7,4},{8,11},{9,110},... | collective-permute-start | bytes 3145736 | tf_op jit(solution)/shard_map/ppermute | solution.py:105
  132.3 8.8 %copy-start.4 = (f32[512]{0:T(512)S(1)}, f32[512]{0:T(512)}, u32[]{:S(2)}) copy-start(f32[512]{0:T(512)} %param.16) | copy-start | bytes 6148
  142.2 12.6 %collective-permute-start.14 = (f32[512,512]{1,0:T(8,128)S(1)}, f32[512,512]{1,0:T(8,128)S(1)}, u32[]{:S(2)}, u32[]{:S(2)}) collective-permute-start(f32[512,512]{1,0:T(8,128)S(1)} %fusion.8), channel_id=1, source_target_pairs={{7,15},{8,0},{15,23},{16,8},{23,31},{24,16},{39,47},{40,32},{47,55... | collective-permute-start | bytes 3145736 | tf_op jit(solution)/shard_map/ppermute | solution.py:105
  143.0 19.4 %collective-permute-start.13 = (f32[512,512]{1,0:T(8,128)S(1)}, f32[512,512]{1,0:T(8,128)S(1)}, u32[]{:S(2)}, u32[]{:S(2)}) collective-permute-start(f32[512,512]{1,0:T(8,128)S(1)} %fusion.8), channel_id=1, source_target_pairs={{0,2},{2,4},{4,6},{6,32},{8,10},{10,12},{12,14},{14,40},{16,18},{1... | collective-permute-start | bytes 3145736 | tf_op jit(solution)/shard_map/ppermute | solution.py:105
  145.1 24.8 %collective-permute-start.17 = (f32[512,512]{1,0:T(8,128)S(1)}, f32[512,512]{1,0:T(8,128)S(1)}, u32[]{:S(2)}, u32[]{:S(2)}) collective-permute-start(f32[512,512]{1,0:T(8,128)S(1)} %fusion.8), channel_id=1, source_target_pairs={{6,15},{9,0},{14,23},{17,8},{22,31},{25,16},{38,47},{41,32},{46,55... | collective-permute-start | bytes 3145736 | tf_op jit(solution)/shard_map/ppermute | solution.py:105
  150.9 21.1 %collective-permute-start.16 = (f32[512,512]{1,0:T(8,128)S(1)}, f32[512,512]{1,0:T(8,128)S(1)}, u32[]{:S(2)}, u32[]{:S(2)}) collective-permute-start(f32[512,512]{1,0:T(8,128)S(1)} %fusion.8), channel_id=1, source_target_pairs={{1,2},{3,4},{5,6},{7,32},{9,10},{11,12},{13,14},{15,40},{17,18},{1... | collective-permute-start | bytes 3145736 | tf_op jit(solution)/shard_map/ppermute | solution.py:105
  152.9 25.5 %collective-permute-start.18 = (f32[512,512]{1,0:T(8,128)S(1)}, f32[512,512]{1,0:T(8,128)S(1)}, u32[]{:S(2)}, u32[]{:S(2)}) collective-permute-start(f32[512,512]{1,0:T(8,128)S(1)} %fusion.8), channel_id=1, source_target_pairs={{0,1},{1,0},{2,3},{3,2},{4,5},{5,4},{6,7},{7,6},{8,9},{9,8},{10,11... | collective-permute-start | bytes 3145736 | tf_op jit(solution)/shard_map/ppermute | solution.py:105
  163.9 17.8 %collective-permute-start.15 = (f32[512,512]{1,0:T(8,128)S(1)}, f32[512,512]{1,0:T(8,128)S(1)}, u32[]{:S(2)}, u32[]{:S(2)}) collective-permute-start(f32[512,512]{1,0:T(8,128)S(1)} %multiply_add_fusion.2), channel_id=1, source_target_pairs={{0,4},{1,101},{2,6},{3,103},{4,32},{5,1},{6,34},{7,3},{8,12},{9,10... | collective-permute-start | bytes 3145736 | tf_op jit(solution)/shard_map/ppermute | solution.py:105
  174.2 40.7 %collective-permute-start.20 = (f32[512,512]{1,0:T(8,128)S(1)}, f32[512,512]{1,0:T(8,128)S(1)}, u32[]{:S(2)}, u32[]{:S(2)}) collective-permute-start(f32[512,512]{1,0:T(8,128)S(1)} %multiply_add_fusion.1), channel_id=1, source_target_pairs={{0,4},{1,101},{2,6},{3,103},{4,32},{5,1},{6,34},{7,3},{8,12},{9,10... | collective-permute-start | bytes 3145736 | tf_op jit(solution)/shard_map/ppermute | solution.py:105
  181.8 49.2 %collective-permute-start.19 = (f32[512,512]{1,0:T(8,128)S(1)}, f32[512,512]{1,0:T(8,128)S(1)}, u32[]{:S(2)}, u32[]{:S(2)}) collective-permute-start(f32[512,512]{1,0:T(8,128)S(1)} %add.132), channel_id=1, source_target_pairs={{0,2},{1,103},{2,4},{3,1},{4,6},{5,3},{6,32},{7,5},{8,10},{9,111},... | collective-permute-start | bytes 3145736 | tf_op jit(solution)/shard_map/ppermute | solution.py:105
  215.2 32.5 %collective-permute-start.21 = (f32[512,512]{1,0:T(8,128)S(1)}, f32[512,512]{1,0:T(8,128)S(1)}, u32[]{:S(2)}, u32[]{:S(2)}) collective-permute-start(f32[512,512]{1,0:T(8,128)S(1)} %add.134), channel_id=1, source_target_pairs={{0,3},{1,102},{2,5},{3,0},{4,7},{5,2},{6,33},{7,4},{8,11},{9,110},... | collective-permute-start | bytes 3145736 | tf_op jit(solution)/shard_map/ppermute | solution.py:105

commit v5 on v4

--- a/solution.py
+++ b/solution.py
@@ -122,19 +122,8 @@
 SOURCES = ("own", "far", "far_mate", "next", "next_mate")
 LINK = {name: 8 * n for n, name in enumerate(SOURCES)}
 UNIT = 8 * len(SOURCES)
-(
-    PASS,
-    PASS_MATE,
-    CROSS,
-    CROSS_MATE,
-    CROSS_OWN,
-    NEAR,
-    NEAR_OTHER,
-    NEAR_MATE,
-    MATE,
-    FIRST_DIAGONAL,
-    SECOND_DIAGONAL,
-) = range(11)
+PASS, PASS_MATE, CROSS, CROSS_MATE, CROSS_OWN, FIRST_DIAGONAL, SECOND_DIAGONAL = range(7)
+NEAR, NEAR_OTHER, NEAR_MATE, MATE = range(4)
 COLUMN = 4
 
 
@@ -158,12 +147,12 @@
                 (dj + 2 * s, dj, LINK["far"] + on2, crosses),
                 (dj + 3 * s, dj + s, LINK["far_mate"] + on2, crosses),
                 (dj + 2 * s, dj + s, LINK["far_mate"] + on1, crosses),
+                (i, i, UNIT, True),
+                (j, j, UNIT, True),
                 (j, nj, LINK["next"] + back2, joins),
                 (j + s, nj, LINK["next"] + back1, joins),
                 (j + s, nj + s, LINK["next_mate"] + back2, joins),
                 (j + s, j, LINK["own"] + on1, True),
-                (i, i, UNIT, True),
-                (j, j, UNIT, True),
             ]
             for n, (row, to, link, used) in enumerate(entries):
                 used = used and 0 <= row < NJ and 0 <= to < NJ
@@ -190,21 +179,17 @@
     links = jnp.concatenate([row_links, column_links, jnp.zeros((2,), jnp.int32)])
     where = lax.axis_index("ia") * NJ + lax.axis_index("ja")
     place = lax.dynamic_slice_in_dim(jnp.asarray(TABLE), where, 1, axis=0)[0].astype(jnp.int32)
-    got = {
-        "own": links,
-        "far": send(links, goal_links(3, False)),
-        "far_mate": send(links, goal_links(3, True)),
-        "next": send(links, goal_links(1, False)),
-        "next_mate": send(links, goal_links(1, True)),
-    }
-    return chosen(place, occ_fock, got)
+    far = {"far": send(links, goal_links(3, False)), "far_mate": send(links, goal_links(3, True))}
+    close = {"own": links, "next": send(links, goal_links(1, False)), "next_mate": send(links, goal_links(1, True))}
+    first = chosen(place[:7], occ_fock, far)
+    return first, chosen(place[7:], occ_fock, close)
 
 
 def after(value, earlier):
     return lax.optimization_barrier((value, earlier))[0]
 
 
-def neighbour_sum(current, weight):
+def neighbour_sum(current, weight, last_weight):
     cross_own = send(current, ACROSS["A"])
     first_own = send(current, FIRST["A"])
     mate = send(current, PARTNER)
@@ -216,11 +201,11 @@
     passed = weight[PASS_MATE] * first_mate + weight[CROSS_MATE] * cross_mate + weight[CROSS_OWN] * cross_own
     middle_mate = send(passed, MIDDLE)
     held = after(current, passed)
-    near = (weight[NEAR] * held + weight[NEAR_OTHER] * mate, weight[NEAR_MATE] * mate)
+    near = (last_weight[NEAR] * held + last_weight[NEAR_OTHER] * mate, last_weight[NEAR_MATE] * mate)
     near_own, near_mate = lax.optimization_barrier(near)
     last_own = send(middle_own + near_own, LAST["A"])
     last_mate = send(middle_mate + near_mate, LAST["B"])
-    return last_own + weight[MATE] * mate, last_mate
+    return last_own + last_weight[MATE] * mate, last_mate
 
 
 def body(
@@ -239,13 +224,13 @@
     current = start
     for sweep_number in range(ITERS):
         if sweep_number == 0:
-            weight = coefficients(occ_fock, row_links[0, 0], column_links[0, 0])
+            weight, last_weight = coefficients(occ_fock, row_links[0, 0], column_links[0, 0])
             diagonal = weight[FIRST_DIAGONAL] + weight[SECOND_DIAGONAL]
             fock_dense = build_dense(pao_fock, block_columns)
             intersection_dense = build_dense(pao_intersection, block_columns)
             shifted = fock_dense - diagonal * intersection_dense
             inverse_gap = 1.0 / (pao_energies[:, None] + pao_energies[None, :] - diagonal)
-        parts = neighbour_sum(current, weight)
+        parts = neighbour_sum(current, weight, last_weight)
         from_fock = mm(shifted, current)
         from_intersection = mm(intersection_dense, current)
         local = mm(from_fock, intersection_dense)

time: 252 us -> 243 us (0.964)
  starting transfers between devices: 139 us -> 85.6 us
  waiting for transfers between devices: 65.7 us -> 104 us
  other arithmetic: 18.7 us -> 21.8 us
    ppermute x22, starting transfers between devices: 139 us -> 85.6 us  [send(): return lax.ppermute(x, AXES, pairs)]
    ppermute x22, waiting for transfers between devices: 65.7 us -> 104 us  [send(): return lax.ppermute(x, AXES, pairs)]
  transfers between devices with their start and end apart: 22 -> 22, of which waited for: 13 -> 11; matrix products, arithmetic and copies ran while one was open for 16% -> 18% of each run, Pallas kernels for 0% -> 0%
where the time goes in v5:
time: 243 us; the launch traced here: 242 us
  waiting for transfers between devices  104 us (43%)
  starting transfers between devices  85.6 us (35%)
  matrix products  26.2 us (11%)
  other arithmetic  21.8 us (9%)
    ppermute x22, waiting for transfers between devices, send(): return lax.ppermute(x, AXES, pairs)  104 us
    ppermute x22, starting transfers between devices, send(): return lax.ppermute(x, AXES, pairs)  85.6 us
    dot_general x16, matrix products, mm(): return jnp.dot(a, b, precision=HIGH, preferred_element_type=jnp.float32)  20.6 us
    add x2, other arithmetic, neighbour_sum(): weight[PASS_MATE] * first_mate + weight[CROSS_MATE] * cross_mate  6.28 us
    dot_general x2, matrix products, build_dense(): dense = jnp.einsum('rxk,rkn->rxn', blocks, spread, precision=HIGH)  5.62 us
    mul x2, other arithmetic, neighbour_sum(): last_weight[NEAR_MATE] * mate  5.57 us
  transfers between devices with their start and end apart: 22, of which 11 were waited for; matrix products, arithmetic and copies ran while one was open for 18% of the time, Pallas kernels for 0%

profile of v5, /device:TPU:15, one launch (start us, length us, event | category | flops | bytes accessed | tf_op | source)
XLA Modules:
  0.0 241.6 jit_solution(16110307352435942497)
XLA Ops:
  0.8 11.7 %collective-permute-start.6 = (s32[8]{0:T(128)S(1)}, s32[8]{0:T(128)S(1)}, u32[]{:S(2)}, u32[]{:S(2)}) collective-permute-start(s32[8]{0:T(128)S(1)} %pad_add_fusion), channel_id=1, source_target_pairs={{0,3},{1,102},{2,5},{3,0},{4,7},{5,2},{6,33},{7,4},{8,11},{9,110},... | collective-permute-start | bytes 104 | tf_op jit(solution)/shard_map/ppermute | solution.py:105
  12.5 3.3 %collective-permute-start.1 = (s32[8]{0:T(128)S(1)}, s32[8]{0:T(128)S(1)}, u32[]{:S(2)}, u32[]{:S(2)}) collective-permute-start(s32[8]{0:T(128)S(1)} %pad_add_fusion), channel_id=1, source_target_pairs={{0,7},{1,98},{2,33},{3,100},{4,35},{5,102},{6,37},{7,0},{8,15},{9,... | collective-permute-start | bytes 104 | tf_op jit(solution)/shard_map/ppermute | solution.py:105
  15.8 1.9 collective-permute-start
  19.4 4.6 %collective-permute-start.2 = (f32[512,512]{1,0:T(8,128)}, f32[512,512]{1,0:T(8,128)}, u32[]{:S(2)}, u32[]{:S(2)}) collective-permute-start(f32[512,512]{1,0:T(8,128)} %bitcast.96), channel_id=1, source_target_pairs={{0,2},{2,4},{4,6},{6,32},{8,10},{10,12},{12,14},{14,40},{16,18},{1... | collective-permute-start | bytes 3145736 | tf_op jit(solution)/shard_map/ppermute | solution.py:105
  27.5 3.1 %fusion.1 = f32[8,512,64]{1,2,0:T(8,128)S(1)} fusion(f32[8,64,384]{2,1,0:T(8,128)} %param.12, s32[8,384]{1,0:T(8,128)S(1)} %broadcast_add_fusion), kind=kOutput, calls=%fused_computation.2 | convolution fusion | flops 605552640 | bytes 1847296 | tf_op jit(solution)/shard_map/rxk,rkn->rxn/dot_general | solution.py:118
  30.7 5.2 %collective-permute-start.8 = (f32[512,512]{1,0:T(8,128)S(1)}, f32[512,512]{1,0:T(8,128)}, u32[]{:S(2)}, u32[]{:S(2)}) collective-permute-start(f32[512,512]{1,0:T(8,128)S(1)} %bitcast.97), channel_id=1, source_target_pairs={{6,15},{9,0},{14,23},{17,8},{22,31},{25,16},{38,47},{41,32},{46,55... | collective-permute-start | bytes 3145736 | tf_op jit(solution)/shard_map/ppermute | solution.py:105
  40.1 1.9 collective-permute-start.5
  42.1 13.1 %collective-permute-done.5 = s32[8]{0:T(128)S(1)} collective-permute-done((s32[8]{0:T(128)S(1)}, s32[8]{0:T(128)S(1)}, u32[]{:S(2)}, u32[]{:S(2)}) %collective-permute-start.5) | collective-permute-done | bytes 64 | tf_op jit(solution)/shard_map/ppermute | solution.py:105
  57.4 3.1 %multiply_add_fusion.5 = f32[512,512]{1,0:T(8,128)S(1)} fusion(f32[512,512]{1,0:T(8,128)} %collective-permute-done.3, f32[512,512]{1,0:T(8,128)} %collective-permute-done.2, f32[]{:T(128)} %bitcast.17, f32[]{:T(128)} %bitcast.16), kind=kLoop, calls=%fused_computation.35 | loop fusion | flops 786432 | bytes 3145736 | tf_op jit(solution)/shard_map/add | solution.py:198
  60.5 2.4 collective-permute-start.4
  62.9 2.5 %fusion.11 = (f32[8,64,512]{2,1,0:T(8,128)S(1)}, f32[8,512,64]{1,2,0:T(8,128)S(1)}) fusion(f32[8,512,64]{1,2,0:T(8,128)S(1)} %fusion.1, f32[]{:T(128)} %bitcast.9, f32[8,64,384]{2,1,0:T(8,128)S(1)} %copy-done, s32[8,384]{1,0:T(8,128)S(1)} %broadcast_add_fusion), kind=kOutput, calls=%fused_computation.19 | convolution fusion | flops 606076928 | bytes 3944452 | tf_op jit(solution)/shard_map/rxk,rkn->rxn/dot_general | solution.py:118
  65.4 4.1 %multiply_add_fusion.4 = f32[512,512]{1,0:T(8,128)S(1)} fusion(f32[512,512]{1,0:T(8,128)} %collective-permute-done.3, f32[512,512]{1,0:T(8,128)} %collective-permute-done.8, f32[512,512]{1,0:T(8,128)} %collective-permute-done.7, f32[]{:T(128)} %bitcast.24, f32[]{:T(128)} %bitcast.23, f32[]{:T(128)} %bitcast.22), kind=kLoop, calls=%fused_computation.34 | loop fusion | flops 1310720 | bytes 4194316 | tf_op jit(solution)/shard_map/add | solution.py:201
  69.5 4.1 %collective-permute-start.11 = (f32[512,512]{1,0:T(8,128)S(1)}, f32[512,512]{1,0:T(8,128)S(1)}, u32[]{:S(2)}, u32[]{:S(2)}) collective-permute-start(f32[512,512]{1,0:T(8,128)S(1)} %multiply_add_fusion.4), channel_id=1, source_target_pairs={{0,4},{1,101},{2,6},{3,103},{4,32},{5,1},{6,34},{7,3},{8,12},{9,10... | collective-permute-start | bytes 3145736 | tf_op jit(solution)/shard_map/ppermute | solution.py:105
  74.2 3.4 %broadcast_multiply_fusion.1 = (f32[512,512]{1,0:T(8,128)S(1)}, f32[512,512]{1,0:T(8,128)S(1)}) fusion(f32[512,512]{1,0:T(8,128)} %collective-permute-done.9, f32[]{:T(128)} %bitcast.26, f32[]{:T(128)} %bitcast.25, f32[512,512]{1,0:T(8,128)S(1)} %bitcast.100, f32[]{:T(128)} %bitcast.21), kind=kLoop, calls=%fused_computation.40 | loop fusion | flops 1048576 | bytes 4194316 | tf_op jit(solution)/shard_map/mul | solution.py:204
  77.6 18.0 %collective-permute-done.4 = f32[512,512]{1,0:T(8,128)S(1)} collective-permute-done((f32[512,512]{1,0:T(8,128)S(1)}, f32[512,512]{1,0:T(8,128)S(1)}, u32[]{:S(2)}, u32[]{:S(2)}) %collective-permute-start.4) | collective-permute-done | bytes 1048608 | tf_op jit(solution)/shard_map/ppermute | solution.py:105
  95.9 1.9 collective-permute-start.10
  99.8 9.2 %collective-permute-done.11 = f32[512,512]{1,0:T(8,128)S(1)} collective-permute-done((f32[512,512]{1,0:T(8,128)S(1)}, f32[512,512]{1,0:T(8,128)S(1)}, u32[]{:S(2)}, u32[]{:S(2)}) %collective-permute-start.11) | collective-permute-done | bytes 1048608 | tf_op jit(solution)/shard_map/ppermute | solution.py:105
  109.3 5.5 %collective-permute-start.12 = (f32[512,512]{1,0:T(8,128)S(1)}, f32[512,512]{1,0:T(8,128)S(1)}, u32[]{:S(2)}, u32[]{:S(2)}) collective-permute-start(f32[512,512]{1,0:T(8,128)S(1)} %add.122), channel_id=1, source_target_pairs={{0,3},{1,102},{2,5},{3,0},{4,7},{5,2},{6,33},{7,4},{8,11},{9,110},... | collective-permute-start | bytes 3145736 | tf_op jit(solution)/shard_map/ppermute | solution.py:105
  117.0 5.1 %collective-permute-done.10 = f32[512,512]{1,0:T(8,128)S(1)} collective-permute-done((f32[512,512]{1,0:T(8,128)S(1)}, f32[512,512]{1,0:T(8,128)S(1)}, u32[]{:S(2)}, u32[]{:S(2)}) %collective-permute-start.10) | collective-permute-done | bytes 1048608 | tf_op jit(solution)/shard_map/ppermute | solution.py:105
  122.0 3.0 %fusion.18 = f32[512,512]{1,0:T(8,128)S(1)} fusion(f32[512,512]{1,0:T(8,128)S(1)} %bitcast.81, f32[512,512]{1,0:T(8,128)S(1)} %collective-permute-done.10, f32[512,512]{1,0:T(8,128)} %collective-permute-done.9, f32[]{:T(128)} %bitcast.27), kind=kOutput, calls=%fused_computation.30 | convolution fusion | flops 805830656 | bytes 4194308 | tf_op jit(solution)/shard_map/dot_general | solution.py:109
  126.1 8.7 %collective-permute-done.12 = f32[512,512]{1,0:T(8,128)S(1)} collective-permute-done((f32[512,512]{1,0:T(8,128)S(1)}, f32[512,512]{1,0:T(8,128)S(1)}, u32[]{:S(2)}, u32[]{:S(2)}) %collective-permute-start.12) | collective-permute-done | bytes 1048608 | tf_op jit(solution)/shard_map/ppermute | solution.py:105
  139.6 2.4 collective-permute-start.17
  145.9 14.9 %collective-permute-done.13 = f32[512,512]{1,0:T(8,128)S(1)} collective-permute-done((f32[512,512]{1,0:T(8,128)S(1)}, f32[512,512]{1,0:T(8,128)S(1)}, u32[]{:S(2)}, u32[]{:S(2)}) %collective-permute-start.13) | collective-permute-done | bytes 1048608 | tf_op jit(solution)/shard_map/ppermute | solution.py:105
  165.7 2.2 multiply_add_fusion.1
  169.8 2.2 broadcast_multiply_fusion
  172.0 8.6 %collective-permute-done.15 = f32[512,512]{1,0:T(8,128)S(1)} collective-permute-done((f32[512,512]{1,0:T(8,128)S(1)}, f32[512,512]{1,0:T(8,128)S(1)}, u32[]{:S(2)}, u32[]{:S(2)}) %collective-permute-start.15) | collective-permute-done | bytes 1048608 | tf_op jit(solution)/shard_map/ppermute | solution.py:105
  180.8 22.5 %collective-permute-start.19 = (f32[512,512]{1,0:T(8,128)S(1)}, f32[512,512]{1,0:T(8,128)S(1)}, u32[]{:S(2)}, u32[]{:S(2)}) collective-permute-start(f32[512,512]{1,0:T(8,128)S(1)} %add.132), channel_id=1, source_target_pairs={{0,2},{1,103},{2,4},{3,1},{4,6},{5,3},{6,32},{7,5},{8,10},{9,111},... | collective-permute-start | bytes 3145736 | tf_op jit(solution)/shard_map/ppermute | solution.py:105
  205.4 6.8 %collective-permute-done.20 = f32[512,512]{1,0:T(8,128)S(1)} collective-permute-done((f32[512,512]{1,0:T(8,128)S(1)}, f32[512,512]{1,0:T(8,128)S(1)}, u32[]{:S(2)}, u32[]{:S(2)}) %collective-permute-start.20) | collective-permute-done | bytes 1048608 | tf_op jit(solution)/shard_map/ppermute | solution.py:105
  212.4 2.5 %collective-permute-start.21 = (f32[512,512]{1,0:T(8,128)S(1)}, f32[512,512]{1,0:T(8,128)S(1)}, u32[]{:S(2)}, u32[]{:S(2)}) collective-permute-start(f32[512,512]{1,0:T(8,128)S(1)} %add.134), channel_id=1, source_target_pairs={{0,3},{1,102},{2,5},{3,0},{4,7},{5,2},{6,33},{7,4},{8,11},{9,110},... | collective-permute-start | bytes 3145736 | tf_op jit(solution)/shard_map/ppermute | solution.py:105
  216.9 8.6 %collective-permute-done.19 = f32[512,512]{1,0:T(8,128)S(1)} collective-permute-done((f32[512,512]{1,0:T(8,128)S(1)}, f32[512,512]{1,0:T(8,128)S(1)}, u32[]{:S(2)}, u32[]{:S(2)}) %collective-permute-start.19) | collective-permute-done | bytes 1048608 | tf_op jit(solution)/shard_map/ppermute | solution.py:105
  228.4 10.0 %collective-permute-done.21 = f32[512,512]{1,0:T(8,128)S(1)} collective-permute-done((f32[512,512]{1,0:T(8,128)S(1)}, f32[512,512]{1,0:T(8,128)S(1)}, u32[]{:S(2)}, u32[]{:S(2)}) %collective-permute-start.21) | collective-permute-done | bytes 1048608 | tf_op jit(solution)/shard_map/ppermute | solution.py:105
  239.4 2.2 fusion.10
  (77 shorter events, 41.4 us)
Async XLA Ops:
  0.0 62.9 %copy-start = (f32[8,64,384]{2,1,0:T(8,128)S(1)}, f32[8,64,384]{2,1,0:T(8,128)}, u32[]{:S(2)}) copy-start(f32[8,64,384]{2,1,0:T(8,128)} %param.13) | copy-start | bytes 2359300
  0.8 39.3 %collective-permute-start.6 = (s32[8]{0:T(128)S(1)}, s32[8]{0:T(128)S(1)}, u32[]{:S(2)}, u32[]{:S(2)}) collective-permute-start(s32[8]{0:T(128)S(1)} %pad_add_fusion), channel_id=1, source_target_pairs={{0,3},{1,102},{2,5},{3,0},{4,7},{5,2},{6,33},{7,4},{8,11},{9,110},... | collective-permute-start | bytes 104 | tf_op jit(solution)/shard_map/ppermute | solution.py:105
  12.5 18.2 %collective-permute-start.1 = (s32[8]{0:T(128)S(1)}, s32[8]{0:T(128)S(1)}, u32[]{:S(2)}, u32[]{:S(2)}) collective-permute-start(s32[8]{0:T(128)S(1)} %pad_add_fusion), channel_id=1, source_target_pairs={{0,7},{1,98},{2,33},{3,100},{4,35},{5,102},{6,37},{7,0},{8,15},{9,... | collective-permute-start | bytes 104 | tf_op jit(solution)/shard_map/ppermute | solution.py:105
  15.8 20.2 %collective-permute-start = (s32[8]{0:T(128)S(1)}, s32[8]{0:T(128)S(1)}, u32[]{:S(2)}, u32[]{:S(2)}) collective-permute-start(s32[8]{0:T(128)S(1)} %pad_add_fusion), channel_id=1, source_target_pairs={{0,98},{1,7},{2,100},{3,33},{4,102},{5,35},{6,0},{7,37},{8,106},{9... | collective-permute-start | bytes 104 | tf_op jit(solution)/shard_map/ppermute | solution.py:105
  17.7 39.7 %collective-permute-start.3 = (f32[512,512]{1,0:T(8,128)}, f32[512,512]{1,0:T(8,128)}, u32[]{:S(2)}, u32[]{:S(2)}) collective-permute-start(f32[512,512]{1,0:T(8,128)} %bitcast.95), channel_id=1, source_target_pairs={{7,15},{8,0},{15,23},{16,8},{23,31},{24,16},{39,47},{40,32},{47,55... | collective-permute-start | bytes 3145736 | tf_op jit(solution)/shard_map/ppermute | solution.py:105
  19.4 38.0 %collective-permute-start.2 = (f32[512,512]{1,0:T(8,128)}, f32[512,512]{1,0:T(8,128)}, u32[]{:S(2)}, u32[]{:S(2)}) collective-permute-start(f32[512,512]{1,0:T(8,128)} %bitcast.96), channel_id=1, source_target_pairs={{0,2},{2,4},{4,6},{6,32},{8,10},{10,12},{12,14},{14,40},{16,18},{1... | collective-permute-start | bytes 3145736 | tf_op jit(solution)/shard_map/ppermute | solution.py:105
  27.5 3.2 %copy-start.1 = (f32[1,1,512,512]{3,2,1,0:T(8,128)S(1)}, f32[1,1,512,512]{3,2,1,0:T(8,128)}, u32[]{:S(2)}) copy-start(f32[1,1,512,512]{3,2,1,0:T(8,128)} %param.10) | copy-start | bytes 3145732
  27.5 29.6 %copy-start.3 = (s32[1,1,2]{2,1,0:T(1,128)S(1)}, s32[1,1,2]{2,1,0:T(1,128)}, u32[]{:S(2)}) copy-start(s32[1,1,2]{2,1,0:T(1,128)} %param.18) | copy-start | bytes 28
  27.5 29.6 %copy-start.4 = (s32[1,1,4]{2,1,0:T(1,128)S(1)}, s32[1,1,4]{2,1,0:T(1,128)}, u32[]{:S(2)}) copy-start(s32[1,1,4]{2,1,0:T(1,128)} %param.17) | copy-start | bytes 52
  30.7 34.6 %collective-permute-start.8 = (f32[512,512]{1,0:T(8,128)S(1)}, f32[512,512]{1,0:T(8,128)}, u32[]{:S(2)}, u32[]{:S(2)}) collective-permute-start(f32[512,512]{1,0:T(8,128)S(1)} %bitcast.97), channel_id=1, source_target_pairs={{6,15},{9,0},{14,23},{17,8},{22,31},{25,16},{38,47},{41,32},{46,55... | collective-permute-start | bytes 3145736 | tf_op jit(solution)/shard_map/ppermute | solution.py:105
  36.0 29.4 %collective-permute-start.7 = (f32[512,512]{1,0:T(8,128)S(1)}, f32[512,512]{1,0:T(8,128)}, u32[]{:S(2)}, u32[]{:S(2)}) collective-permute-start(f32[512,512]{1,0:T(8,128)S(1)} %bitcast.98), channel_id=1, source_target_pairs={{1,2},{3,4},{5,6},{7,32},{9,10},{11,12},{13,14},{15,40},{17,18},{1... | collective-permute-start | bytes 3145736 | tf_op jit(solution)/shard_map/ppermute | solution.py:105
  40.1 15.1 %collective-permute-start.5 = (s32[8]{0:T(128)S(1)}, s32[8]{0:T(128)S(1)}, u32[]{:S(2)}, u32[]{:S(2)}) collective-permute-start(s32[8]{0:T(128)S(1)} %pad_add_fusion), channel_id=1, source_target_pairs={{0,102},{1,3},{2,0},{3,5},{4,2},{5,7},{6,4},{7,33},{8,110},{9,11},... | collective-permute-start | bytes 104 | tf_op jit(solution)/shard_map/ppermute | solution.py:105
  55.2 19.1 %collective-permute-start.9 = (f32[512,512]{1,0:T(8,128)S(1)}, f32[512,512]{1,0:T(8,128)}, u32[]{:S(2)}, u32[]{:S(2)}) collective-permute-start(f32[512,512]{1,0:T(8,128)S(1)} %bitcast.99), channel_id=1, source_target_pairs={{0,1},{1,0},{2,3},{3,2},{4,5},{5,4},{6,7},{7,6},{8,9},{9,8},{10,11... | collective-permute-start | bytes 3145736 | tf_op jit(solution)/shard_map/ppermute | solution.py:105
  60.5 35.2 %collective-permute-start.4 = (f32[512,512]{1,0:T(8,128)S(1)}, f32[512,512]{1,0:T(8,128)S(1)}, u32[]{:S(2)}, u32[]{:S(2)}) collective-permute-start(f32[512,512]{1,0:T(8,128)S(1)} %multiply_add_fusion.5), channel_id=1, source_target_pairs={{0,4},{1,101},{2,6},{3,103},{4,32},{5,1},{6,34},{7,3},{8,12},{9,10... | collective-permute-start | bytes 3145736 | tf_op jit(solution)/shard_map/ppermute | solution.py:105
  69.5 39.6 %collective-permute-start.11 = (f32[512,512]{1,0:T(8,128)S(1)}, f32[512,512]{1,0:T(8,128)S(1)}, u32[]{:S(2)}, u32[]{:S(2)}) collective-permute-start(f32[512,512]{1,0:T(8,128)S(1)} %multiply_add_fusion.4), channel_id=1, source_target_pairs={{0,4},{1,101},{2,6},{3,103},{4,32},{5,1},{6,34},{7,3},{8,12},{9,10... | collective-permute-start | bytes 3145736 | tf_op jit(solution)/shard_map/ppermute | solution.py:105
  95.9 26.2 %collective-permute-start.10 = (f32[512,512]{1,0:T(8,128)S(1)}, f32[512,512]{1,0:T(8,128)S(1)}, u32[]{:S(2)}, u32[]{:S(2)}) collective-permute-start(f32[512,512]{1,0:T(8,128)S(1)} %add.120), channel_id=1, source_target_pairs={{0,2},{1,103},{2,4},{3,1},{4,6},{5,3},{6,32},{7,5},{8,10},{9,111},... | collective-permute-start | bytes 3145736 | tf_op jit(solution)/shard_map/ppermute | solution.py:105
  109.3 6.6 %copy-start.2 = (bf16[1,1,512,512]{3,2,1,0:T(8,128)(2,1)S(1)}, bf16[1,1,512,512]{3,2,1,0:T(8,128)(2,1)}, u32[]{:S(2)}) copy-start(bf16[1,1,512,512]{3,2,1,0:T(8,128)(2,1)} %param.11) | copy-start | bytes 1572868
  109.3 25.4 %collective-permute-start.12 = (f32[512,512]{1,0:T(8,128)S(1)}, f32[512,512]{1,0:T(8,128)S(1)}, u32[]{:S(2)}, u32[]{:S(2)}) collective-permute-start(f32[512,512]{1,0:T(8,128)S(1)} %add.122), channel_id=1, source_target_pairs={{0,3},{1,102},{2,5},{3,0},{4,7},{5,2},{6,33},{7,4},{8,11},{9,110},... | collective-permute-start | bytes 3145736 | tf_op jit(solution)/shard_map/ppermute | solution.py:105
  126.0 9.7 %copy-start.5 = (f32[512]{0:T(512)S(1)}, f32[512]{0:T(512)}, u32[]{:S(2)}) copy-start(f32[512]{0:T(512)} %param.16) | copy-start | bytes 6148
  136.9 8.9 %collective-permute-start.14 = (f32[512,512]{1,0:T(8,128)S(1)}, f32[512,512]{1,0:T(8,128)S(1)}, u32[]{:S(2)}, u32[]{:S(2)}) collective-permute-start(f32[512,512]{1,0:T(8,128)S(1)} %fusion.8), channel_id=1, source_target_pairs={{7,15},{8,0},{15,23},{16,8},{23,31},{24,16},{39,47},{40,32},{47,55... | collective-permute-start | bytes 3145736 | tf_op jit(solution)/shard_map/ppermute | solution.py:105
  137.7 23.1 %collective-permute-start.13 = (f32[512,512]{1,0:T(8,128)S(1)}, f32[512,512]{1,0:T(8,128)S(1)}, u32[]{:S(2)}, u32[]{:S(2)}) collective-permute-start(f32[512,512]{1,0:T(8,128)S(1)} %fusion.8), channel_id=1, source_target_pairs={{0,2},{2,4},{4,6},{6,32},{8,10},{10,12},{12,14},{14,40},{16,18},{1... | collective-permute-start | bytes 3145736 | tf_op jit(solution)/shard_map/ppermute | solution.py:105
  139.6 24.6 %collective-permute-start.17 = (f32[512,512]{1,0:T(8,128)S(1)}, f32[512,512]{1,0:T(8,128)S(1)}, u32[]{:S(2)}, u32[]{:S(2)}) collective-permute-start(f32[512,512]{1,0:T(8,128)S(1)} %fusion.8), channel_id=1, source_target_pairs={{6,15},{9,0},{14,23},{17,8},{22,31},{25,16},{38,47},{41,32},{46,55... | collective-permute-start | bytes 3145736 | tf_op jit(solution)/shard_map/ppermute | solution.py:105
  142.0 23.7 %collective-permute-start.16 = (f32[512,512]{1,0:T(8,128)S(1)}, f32[512,512]{1,0:T(8,128)S(1)}, u32[]{:S(2)}, u32[]{:S(2)}) collective-permute-start(f32[512,512]{1,0:T(8,128)S(1)} %fusion.8), channel_id=1, source_target_pairs={{1,2},{3,4},{5,6},{7,32},{9,10},{11,12},{13,14},{15,40},{17,18},{1... | collective-permute-start | bytes 3145736 | tf_op jit(solution)/shard_map/ppermute | solution.py:105
  143.9 25.9 %collective-permute-start.18 = (f32[512,512]{1,0:T(8,128)S(1)}, f32[512,512]{1,0:T(8,128)S(1)}, u32[]{:S(2)}, u32[]{:S(2)}) collective-permute-start(f32[512,512]{1,0:T(8,128)S(1)} %fusion.8), channel_id=1, source_target_pairs={{0,1},{1,0},{2,3},{3,2},{4,5},{5,4},{6,7},{7,6},{8,9},{9,8},{10,11... | collective-permute-start | bytes 3145736 | tf_op jit(solution)/shard_map/ppermute | solution.py:105
  162.3 18.3 %collective-permute-start.15 = (f32[512,512]{1,0:T(8,128)S(1)}, f32[512,512]{1,0:T(8,128)S(1)}, u32[]{:S(2)}, u32[]{:S(2)}) collective-permute-start(f32[512,512]{1,0:T(8,128)S(1)} %multiply_add_fusion.2), channel_id=1, source_target_pairs={{0,4},{1,101},{2,6},{3,103},{4,32},{5,1},{6,34},{7,3},{8,12},{9,10... | collective-permute-start | bytes 3145736 | tf_op jit(solution)/shard_map/ppermute | solution.py:105
  167.9 44.3 %collective-permute-start.20 = (f32[512,512]{1,0:T(8,128)S(1)}, f32[512,512]{1,0:T(8,128)S(1)}, u32[]{:S(2)}, u32[]{:S(2)}) collective-permute-start(f32[512,512]{1,0:T(8,128)S(1)} %multiply_add_fusion.1), channel_id=1, source_target_pairs={{0,4},{1,101},{2,6},{3,103},{4,32},{5,1},{6,34},{7,3},{8,12},{9,10... | collective-permute-start | bytes 3145736 | tf_op jit(solution)/shard_map/ppermute | solution.py:105
  180.8 44.8 %collective-permute-start.19 = (f32[512,512]{1,0:T(8,128)S(1)}, f32[512,512]{1,0:T(8,128)S(1)}, u32[]{:S(2)}, u32[]{:S(2)}) collective-permute-start(f32[512,512]{1,0:T(8,128)S(1)} %add.132), channel_id=1, source_target_pairs={{0,2},{1,103},{2,4},{3,1},{4,6},{5,3},{6,32},{7,5},{8,10},{9,111},... | collective-permute-start | bytes 3145736 | tf_op jit(solution)/shard_map/ppermute | solution.py:105
  212.4 26.0 %collective-permute-start.21 = (f32[512,512]{1,0:T(8,128)S(1)}, f32[512,512]{1,0:T(8,128)S(1)}, u32[]{:S(2)}, u32[]{:S(2)}) collective-permute-start(f32[512,512]{1,0:T(8,128)S(1)} %add.134), channel_id=1, source_target_pairs={{0,3},{1,102},{2,5},{3,0},{4,7},{5,2},{6,33},{7,4},{8,11},{9,110},... | collective-permute-start | bytes 3145736 | tf_op jit(solution)/shard_map/ppermute | solution.py:105
